TPU v7x, 32 devices: a whole 2x2x4 slice. The times are simulated.
32 devices in a mesh: parts: 2 (over y), panel: 4 (over z), zone: 2 (over x), rhs: 2 (over core).
Axes of the slice: x: 2, y: 2, z: 4, core: 2. Of those that a mesh axis runs over, the one named last changes fastest.
Arguments:
- source: bfloat16 [4, 4096, 512], P(('parts', 'zone'), 'panel', 'rhs'), parts along dimension 0, may hold values from -6 to 6
- inverse: bfloat16 [4, 4096, 4096], P(('parts', 'zone'), 'panel'), parts along dimension 0, may hold values from -0.09375 to 0.09375
- coupling: bfloat16 [4, 4096, 4096], P(('parts', 'zone'), 'panel'), parts along dimension 0, may hold values from -0.078125 to 0.078125
Outputs:
- eliminated: bfloat16 [4, 4096, 512], P(('parts', 'zone'), 'panel', 'rhs'), parts along dimension 0
There are 2 independent parts, one for each index of `parts`. A program takes and returns all parts, laid end to end along the dimension named above; each array names one. Nothing has to cross between parts.
All inputs are finite; a program needn't handle non-finite values.
Results may differ from a plain program's by a relative error of at most 0.013.
Values may be sent and summed in bfloat16 or wider, within the bound.
No kernel may reach another device: no remote copies, remote signals or barrier semaphores. Data moves between devices by JAX's collectives and lax.ppermute only.
A program may use at most 64 MiB of HBM per device.

v0:
```python
import jax
import jax.numpy as jnp
from jax import lax
from jax.sharding import PartitionSpec as P


def from_behind(block, axis, distance):
    devices = range(lax.axis_size(axis))
    route = [(i - distance, i) for i in devices if i - distance in devices]
    return lax.ppermute(block, axis, route)


def local(source, inverse, coupling):
    inverse_block = inverse[0]
    coupling_block = coupling[0]
    local_rhs = source[0]
    row_count = local_rhs.shape[0]
    local_cols = local_rhs.shape[1]
    batch_count = 4
    group_cols = local_cols // batch_count
    zone_count = lax.axis_size("zone")
    zone_index = lax.axis_index("zone")
    total_steps = zone_count + batch_count - 1
    reduced = jnp.dot(
        inverse_block,
        lax.all_gather(local_rhs, "panel", axis=0, tiled=True),
        preferred_element_type=jnp.float32,
    )

    def advance(position, carried):
        previous, result = carried
        micro_index = position - zone_index
        is_live = jnp.logical_and(micro_index >= 0, micro_index < batch_count)
        clipped = jnp.clip(micro_index, 0, batch_count - 1)
        start_col = clipped * group_cols
        incoming = from_behind(previous, "zone", 1)
        initial = lax.dynamic_slice_in_dim(reduced, start_col, group_cols, 1)
        combined = initial - jnp.dot(
            coupling_block,
            lax.all_gather(incoming, "panel", axis=0, tiled=True),
            preferred_element_type=jnp.float32,
        )
        rounded = combined.astype(jnp.bfloat16)
        current = lax.dynamic_slice_in_dim(result, start_col, group_cols, 1)
        updated = lax.dynamic_update_slice_in_dim(
            result, jnp.where(is_live, rounded, current), start_col, 1
        )
        return (rounded, updated)

    starting = (
        jnp.zeros((row_count, group_cols), jnp.bfloat16),
        jnp.zeros((row_count, local_cols), jnp.bfloat16),
    )
    _, result = lax.fori_loop(0, total_steps, advance, starting)
    return result[None]


def solution(mesh):
    in_specs = (
        P(("parts", "zone"), "panel", "rhs"),
        P(("parts", "zone"), "panel", None),
        P(("parts", "zone"), "panel", None),
    )
    out_specs = P(("parts", "zone"), "panel", "rhs")
    return jax.shard_map(local, mesh=mesh, in_specs=in_specs, out_specs=out_specs, check_vma=False)
```

profile of v0, /device:TPU:6, one launch (start us, length us, event | category | flops | bytes accessed | tf_op | source)
XLA Modules:
  0.0 210.9 jit_solution(5797174708042044751)
XLA Ops:
  7.3 48.8 %all-gather.3.cloned.1.call-done = bf16[1,4096,256]{2,1,0:T(8,128)(2,1)} async-done(((bf16[1,1024,256]{2,1,0:T(8,128)(2,1)}), bf16[1,4096,256]{2,1,0:T(8,128)(2,1)}) %all-gather.3.cloned.1.call-update) | async-done | bytes 2097168 | tf_op jit(solution)/shard_map/all_gather | solution.py:26
  56.1 6.3 %fusion.1 = f32[1024,256]{0,1:T(8,128)S(1)} fusion(bf16[1,1024,4096]{2,1,0:T(8,128)(2,1)} %param.6, bf16[1,4096,256]{2,1,0:T(8,128)(2,1)} %all-gather.3.cloned.1.call-done), kind=kOutput, calls=%fused_computation.4 | convolution fusion | flops 2147483648 | bytes 11534336 | tf_op jit(solution)/shard_map/dot_general | solution.py:24
  62.5 140.6 %while.16 = (s32[]{:T(128)}, bf16[1024,64]{0,1:T(8,128)(2,1)S(1)}, bf16[1024,256]{0,1:T(8,128)(2,1)S(1)}, s32[]{:T(128)}, f32[1024,256]{0,1:T(8,128)S(1)}, /*ind...) while((s32[]{:T(128)}, bf16[1024,64]{0,1:T(8,128)(2,1)S(1)}, ...), condition=%wide.region_1.2_spmd.clone, body=%wide.region_0.1_spmd.clone.sunk | while | flops 537133056 | bytes 11010323 | solution.py:54
  62.5 1.3 collective-permute-start
  63.8 5.8 %collective-permute-done = bf16[1024,64]{0,1:T(8,128)(2,1)S(1)} collective-permute-done((bf16[1024,64]{0,1:T(8,128)(2,1)S(1)}, bf16[1024,64]{0,1:T(8,128)(2,1)S(1)}, u32[]{:S(2)}, u32[]{:S(2)}) %collective-permute-start) | collective-permute-done | bytes 131104 | tf_op jit(solution)/shard_map/while/body/eval_jaxpr/ppermute | solution.py:10
  69.6 16.2 %all_gather.13 = bf16[4096,64]{0,1:T(8,128)(2,1)S(1)} all-gather(bf16[1024,64]{0,1:T(8,128)(2,1)S(1)} %collective-permute-done), channel_id=1, replica_groups=mesh['parts'=2,'panel'=4,'zone'=2,'rhs'=2] {'panel'}, dimensions={0}, use_global_device_ids=true | all-gather | bytes 655360 | tf_op jit(solution)/shard_map/while/body/eval_jaxpr/all_gather | solution.py:40
  85.8 6.0 %select_dynamic-update-slice_fusion.2 = (bf16[1024,256]{0,1:T(8,128)(2,1)S(1)}, bf16[1024,64]{0,1:T(8,128)(2,1)S(1)}) fusion(bf16[1024,256]{0,1:T(8,128)(2,1)S(1)} %get-tuple-element.211, s32[]{:T(128)S(6)} %select_n.35, pred[]{:T(512)S(6)} %and.10, bf16[1024,4096]{1,0:T(8,128)(2,1)} %get-tuple-element.226, bf16[4096,64]{0,1:T(8,128)(2,1)S(1)} %all_gather.13, ...), kind=kOutput, calls=%fused_computation.2.clone.1 | convolution fusion | flops 537067520 | bytes 9568261 | tf_op jit(solution)/shard_map/while/body/eval_jaxpr/dot_general | solution.py:38
  91.9 1.3 collective-permute-start
  93.2 5.5 %collective-permute-done = bf16[1024,64]{0,1:T(8,128)(2,1)S(1)} collective-permute-done((bf16[1024,64]{0,1:T(8,128)(2,1)S(1)}, bf16[1024,64]{0,1:T(8,128)(2,1)S(1)}, u32[]{:S(2)}, u32[]{:S(2)}) %collective-permute-start) | collective-permute-done | bytes 131104 | tf_op jit(solution)/shard_map/while/body/eval_jaxpr/ppermute | solution.py:10
  98.8 15.4 %all_gather.13 = bf16[4096,64]{0,1:T(8,128)(2,1)S(1)} all-gather(bf16[1024,64]{0,1:T(8,128)(2,1)S(1)} %collective-permute-done), channel_id=1, replica_groups=mesh['parts'=2,'panel'=4,'zone'=2,'rhs'=2] {'panel'}, dimensions={0}, use_global_device_ids=true | all-gather | bytes 655360 | tf_op jit(solution)/shard_map/while/body/eval_jaxpr/all_gather | solution.py:40
  114.2 6.0 %select_dynamic-update-slice_fusion.2 = (bf16[1024,256]{0,1:T(8,128)(2,1)S(1)}, bf16[1024,64]{0,1:T(8,128)(2,1)S(1)}) fusion(bf16[1024,256]{0,1:T(8,128)(2,1)S(1)} %get-tuple-element.211, s32[]{:T(128)S(6)} %select_n.35, pred[]{:T(512)S(6)} %and.10, bf16[1024,4096]{1,0:T(8,128)(2,1)} %get-tuple-element.226, bf16[4096,64]{0,1:T(8,128)(2,1)S(1)} %all_gather.13, ...), kind=kOutput, calls=%fused_computation.2.clone.1 | convolution fusion | flops 537067520 | bytes 9568261 | tf_op jit(solution)/shard_map/while/body/eval_jaxpr/dot_general | solution.py:38
  120.3 1.3 collective-permute-start
  121.6 5.5 %collective-permute-done = bf16[1024,64]{0,1:T(8,128)(2,1)S(1)} collective-permute-done((bf16[1024,64]{0,1:T(8,128)(2,1)S(1)}, bf16[1024,64]{0,1:T(8,128)(2,1)S(1)}, u32[]{:S(2)}, u32[]{:S(2)}) %collective-permute-start) | collective-permute-done | bytes 131104 | tf_op jit(solution)/shard_map/while/body/eval_jaxpr/ppermute | solution.py:10
  127.2 14.7 %all_gather.13 = bf16[4096,64]{0,1:T(8,128)(2,1)S(1)} all-gather(bf16[1024,64]{0,1:T(8,128)(2,1)S(1)} %collective-permute-done), channel_id=1, replica_groups=mesh['parts'=2,'panel'=4,'zone'=2,'rhs'=2] {'panel'}, dimensions={0}, use_global_device_ids=true | all-gather | bytes 655360 | tf_op jit(solution)/shard_map/while/body/eval_jaxpr/all_gather | solution.py:40
  141.8 6.0 %select_dynamic-update-slice_fusion.2 = (bf16[1024,256]{0,1:T(8,128)(2,1)S(1)}, bf16[1024,64]{0,1:T(8,128)(2,1)S(1)}) fusion(bf16[1024,256]{0,1:T(8,128)(2,1)S(1)} %get-tuple-element.211, s32[]{:T(128)S(6)} %select_n.35, pred[]{:T(512)S(6)} %and.10, bf16[1024,4096]{1,0:T(8,128)(2,1)} %get-tuple-element.226, bf16[4096,64]{0,1:T(8,128)(2,1)S(1)} %all_gather.13, ...), kind=kOutput, calls=%fused_computation.2.clone.1 | convolution fusion | flops 537067520 | bytes 9568261 | tf_op jit(solution)/shard_map/while/body/eval_jaxpr/dot_general | solution.py:38
  147.9 1.3 collective-permute-start
  149.2 5.5 %collective-permute-done = bf16[1024,64]{0,1:T(8,128)(2,1)S(1)} collective-permute-done((bf16[1024,64]{0,1:T(8,128)(2,1)S(1)}, bf16[1024,64]{0,1:T(8,128)(2,1)S(1)}, u32[]{:S(2)}, u32[]{:S(2)}) %collective-permute-start) | collective-permute-done | bytes 131104 | tf_op jit(solution)/shard_map/while/body/eval_jaxpr/ppermute | solution.py:10
  154.8 14.7 %all_gather.13 = bf16[4096,64]{0,1:T(8,128)(2,1)S(1)} all-gather(bf16[1024,64]{0,1:T(8,128)(2,1)S(1)} %collective-permute-done), channel_id=1, replica_groups=mesh['parts'=2,'panel'=4,'zone'=2,'rhs'=2] {'panel'}, dimensions={0}, use_global_device_ids=true | all-gather | bytes 655360 | tf_op jit(solution)/shard_map/while/body/eval_jaxpr/all_gather | solution.py:40
  169.4 6.0 %select_dynamic-update-slice_fusion.2 = (bf16[1024,256]{0,1:T(8,128)(2,1)S(1)}, bf16[1024,64]{0,1:T(8,128)(2,1)S(1)}) fusion(bf16[1024,256]{0,1:T(8,128)(2,1)S(1)} %get-tuple-element.211, s32[]{:T(128)S(6)} %select_n.35, pred[]{:T(512)S(6)} %and.10, bf16[1024,4096]{1,0:T(8,128)(2,1)} %get-tuple-element.226, bf16[4096,64]{0,1:T(8,128)(2,1)S(1)} %all_gather.13, ...), kind=kOutput, calls=%fused_computation.2.clone.1 | convolution fusion | flops 537067520 | bytes 9568261 | tf_op jit(solution)/shard_map/while/body/eval_jaxpr/dot_general | solution.py:38
  175.5 1.3 collective-permute-start
  176.8 5.5 %collective-permute-done = bf16[1024,64]{0,1:T(8,128)(2,1)S(1)} collective-permute-done((bf16[1024,64]{0,1:T(8,128)(2,1)S(1)}, bf16[1024,64]{0,1:T(8,128)(2,1)S(1)}, u32[]{:S(2)}, u32[]{:S(2)}) %collective-permute-start) | collective-permute-done | bytes 131104 | tf_op jit(solution)/shard_map/while/body/eval_jaxpr/ppermute | solution.py:10
  182.4 14.7 %all_gather.13 = bf16[4096,64]{0,1:T(8,128)(2,1)S(1)} all-gather(bf16[1024,64]{0,1:T(8,128)(2,1)S(1)} %collective-permute-done), channel_id=1, replica_groups=mesh['parts'=2,'panel'=4,'zone'=2,'rhs'=2] {'panel'}, dimensions={0}, use_global_device_ids=true | all-gather | bytes 655360 | tf_op jit(solution)/shard_map/while/body/eval_jaxpr/all_gather | solution.py:40
  197.0 6.0 %select_dynamic-update-slice_fusion.2 = (bf16[1024,256]{0,1:T(8,128)(2,1)S(1)}, bf16[1024,64]{0,1:T(8,128)(2,1)S(1)}) fusion(bf16[1024,256]{0,1:T(8,128)(2,1)S(1)} %get-tuple-element.211, s32[]{:T(128)S(6)} %select_n.35, pred[]{:T(512)S(6)} %and.10, bf16[1024,4096]{1,0:T(8,128)(2,1)} %get-tuple-element.226, bf16[4096,64]{0,1:T(8,128)(2,1)S(1)} %all_gather.13, ...), kind=kOutput, calls=%fused_computation.2.clone.1 | convolution fusion | flops 537067520 | bytes 9568261 | tf_op jit(solution)/shard_map/while/body/eval_jaxpr/dot_general | solution.py:38
  203.1 1.0 copy.5
  (9 shorter events, 0.8 us)
Async XLA Ops:
  6.5 49.5 %all-gather.3.cloned.1.call-start = ((), (), s32[]{:S(2)}) async-start(), calls=%async_computation | async-start | bytes 2621440 | tf_op jit(solution)/shard_map/all_gather | solution.py:26
  62.5 7.1 %collective-permute-start = (bf16[1024,64]{0,1:T(8,128)(2,1)S(1)}, bf16[1024,64]{0,1:T(8,128)(2,1)S(1)}, u32[]{:S(2)}, u32[]{:S(2)}) collective-permute-start(bf16[1024,64]{0,1:T(8,128)(2,1)S(1)} %broadcast_select_fusion.2), channel_id=1, source_target_pairs={{0,2},{1,3},{4,6},{5,7},{8,10},{9,11},{12,14},{13,15},{16,18},{17,... | collective-permute-start | bytes 393224 | tf_op jit(solution)/shard_map/while/body/eval_jaxpr/ppermute | solution.py:10
  91.9 6.9 %collective-permute-start = (bf16[1024,64]{0,1:T(8,128)(2,1)S(1)}, bf16[1024,64]{0,1:T(8,128)(2,1)S(1)}, u32[]{:S(2)}, u32[]{:S(2)}) collective-permute-start(bf16[1024,64]{0,1:T(8,128)(2,1)S(1)} %broadcast_select_fusion.2), channel_id=1, source_target_pairs={{0,2},{1,3},{4,6},{5,7},{8,10},{9,11},{12,14},{13,15},{16,18},{17,... | collective-permute-start | bytes 393224 | tf_op jit(solution)/shard_map/while/body/eval_jaxpr/ppermute | solution.py:10
  120.3 6.9 %collective-permute-start = (bf16[1024,64]{0,1:T(8,128)(2,1)S(1)}, bf16[1024,64]{0,1:T(8,128)(2,1)S(1)}, u32[]{:S(2)}, u32[]{:S(2)}) collective-permute-start(bf16[1024,64]{0,1:T(8,128)(2,1)S(1)} %broadcast_select_fusion.2), channel_id=1, source_target_pairs={{0,2},{1,3},{4,6},{5,7},{8,10},{9,11},{12,14},{13,15},{16,18},{17,... | collective-permute-start | bytes 393224 | tf_op jit(solution)/shard_map/while/body/eval_jaxpr/ppermute | solution.py:10
  147.9 6.9 %collective-permute-start = (bf16[1024,64]{0,1:T(8,128)(2,1)S(1)}, bf16[1024,64]{0,1:T(8,128)(2,1)S(1)}, u32[]{:S(2)}, u32[]{:S(2)}) collective-permute-start(bf16[1024,64]{0,1:T(8,128)(2,1)S(1)} %broadcast_select_fusion.2), channel_id=1, source_target_pairs={{0,2},{1,3},{4,6},{5,7},{8,10},{9,11},{12,14},{13,15},{16,18},{17,... | collective-permute-start | bytes 393224 | tf_op jit(solution)/shard_map/while/body/eval_jaxpr/ppermute | solution.py:10
  175.5 6.9 %collective-permute-start = (bf16[1024,64]{0,1:T(8,128)(2,1)S(1)}, bf16[1024,64]{0,1:T(8,128)(2,1)S(1)}, u32[]{:S(2)}, u32[]{:S(2)}) collective-permute-start(bf16[1024,64]{0,1:T(8,128)(2,1)S(1)} %broadcast_select_fusion.2), channel_id=1, source_target_pairs={{0,2},{1,3},{4,6},{5,7},{8,10},{9,11},{12,14},{13,15},{16,18},{17,... | collective-permute-start | bytes 393224 | tf_op jit(solution)/shard_map/while/body/eval_jaxpr/ppermute | solution.py:10
Sparse Core Ops, SparseCore 0:
  8.9 47.0 all-gather.2
where the time goes:
time: 212 us; the launch traced here: 211 us
  waiting for transfers between devices  77.5 us (37%)
  blocking collectives  75.6 us (36%)
  matrix products  36.6 us (17%)
  between operations  13.4 us (6%)
  starting transfers between devices  6.46 us (3%)
    all_gather x5, blocking collectives, advance(): lax.all_gather(incoming, 'panel', axis=0, tiled=True)  75.6 us
    all_gather x1, waiting for transfers between devices, local(): lax.all_gather(local_rhs, 'panel', axis=0, tiled=True)  48.8 us
    dot_general x5, matrix products, advance(): jnp.dot(coupling_block, lax.all_gather(incoming, 'panel', axis=0, tiled=T...  30.2 us
    ppermute x5, waiting for transfers between devices, from_behind(): return lax.ppermute(block, axis, route)  28 us
    ppermute x5, starting transfers between devices, from_behind(): return lax.ppermute(block, axis, route)  6.46 us
    dot_general x1, matrix products, local(): jnp.dot(inverse_block, lax.all_gather(local_rhs, 'panel', axis=0, tiled=T...  6.35 us
  transfers between devices with their start and end apart: 6, of which 6 were waited for; matrix products, arithmetic and copies ran while one was open for 0% of the time, Pallas kernels for 0%

commit v1 on v0

v1 whole, which is shorter than its diff:
```python
import functools

import jax
import jax.numpy as jnp
from jax import lax
from jax.experimental import pallas as pl
from jax.experimental.pallas import tpu as pltpu
from jax.sharding import PartitionSpec as P

CHUNKS = 2
MIB = 1 << 20
VMEM = pl.BlockSpec(memory_space=pltpu.VMEM)
HBM = pl.BlockSpec(memory_space=pltpu.HBM)


def params(mib):
    return pltpu.CompilerParams(vmem_limit_bytes=mib * MIB)


def fetch_kernel(first, second, first_out, second_out, sems):
    copies = [
        pltpu.make_async_copy(first, first_out, sems.at[0]),
        pltpu.make_async_copy(second, second_out, sems.at[1]),
    ]
    for copy in copies:
        copy.start()
    for copy in copies:
        copy.wait()


def fetch(inverse, coupling):
    shape = jax.ShapeDtypeStruct(inverse.shape, inverse.dtype)
    return pl.pallas_call(
        fetch_kernel,
        out_shape=(shape, shape),
        in_specs=[HBM, HBM],
        out_specs=(VMEM, VMEM),
        scratch_shapes=[pltpu.SemaphoreType.DMA((2,))],
        compiler_params=params(18),
        name="fetch",
    )(inverse, coupling)


def relay_kernel(own, up, down, out):
    me = lax.axis_index("panel")

    @pl.when(me == 2)
    def _():
        out[...] = up[...]

    @pl.when(me == 1)
    def _():
        out[...] = down[...]

    @pl.when(jnp.logical_and(me != 1, me != 2))
    def _():
        out[...] = own[...]


def relay(own, up, down):
    return pl.pallas_call(
        relay_kernel,
        out_shape=jax.ShapeDtypeStruct(own.shape, own.dtype),
        in_specs=[VMEM] * 3,
        out_specs=VMEM,
        compiler_params=params(2),
        name="relay",
    )(own, up, down)


UP = [(0, 1), (1, 2), (2, 3), (3, 0)]
DOWN = [(1, 0), (2, 1), (3, 2), (0, 3)]


def gather_source(block):
    n = lax.axis_size("panel")
    if n != 4:
        return gather_any(block)
    up = lax.ppermute(block, "panel", UP)
    down = lax.ppermute(block, "panel", DOWN)
    across = lax.ppermute(relay(block, up, down), "panel", [(0, 2), (3, 1), (2, 3), (1, 0)])
    return [block, up, down, across], (0, 3, 1, 2)


def gather_any(block):
    n = lax.axis_size("panel")
    return [
        block if d == 0 else lax.ppermute(block, "panel", [((i + d) % n, i) for i in range(n)])
        for d in range(n)
    ], tuple(range(n))


def gather_behind(block, k):
    n, zones = lax.axis_size("panel"), lax.axis_size("zone")
    if n != 4:
        return gather_any(lax.ppermute(block, "zone", [(i, (i + 1) % zones) for i in range(zones)]))
    both = ("panel", "zone")
    own = lax.ppermute(block, "zone", [(i, (i + 1) % zones) for i in range(zones)])
    across = lax.ppermute(
        block, both, [(p * zones + k - 1, (p + 2) % 4 * zones + k) for p in range(4)]
    )
    up, down = (
        lax.ppermute(own, both, [(p * zones + k, q * zones + k) for p, q in pairs])
        for pairs in (UP, DOWN)
    )
    return [own, across, up, down], (0, 2, 3, 1)


def product(ahead, n, matrix, blocks):
    me = lax.axis_index("panel")
    depth = blocks[0].shape[0]
    total = None
    for d, block in zip(ahead, blocks):
        start = pl.multiple_of(lax.rem(me + d, n) * depth, depth)
        part = jnp.dot(
            matrix[:, pl.ds(start, depth)], block[...], preferred_element_type=jnp.float32
        )
        total = part if total is None else total + part
    return total


def project_kernel(ahead, n, matrix, *refs):
    blocks, (wide, narrow) = refs[:n], refs[n:]
    total = product(ahead, n, matrix, blocks)
    wide[...] = total
    narrow[...] = total.astype(jnp.bfloat16)


def eliminate_kernel(ahead, n, k, matrix, wide, narrow, *refs):
    blocks, (out,) = refs[:n], refs[n:]
    total = product(ahead, n, matrix, blocks)
    mine = lax.axis_index("zone") == k
    out[...] = jnp.where(mine, (wide[...] - total).astype(jnp.bfloat16), narrow[...])


def project(matrix, blocks, ahead):
    n, (rows, _), cols = len(blocks), matrix.shape, blocks[0].shape[1]
    return pl.pallas_call(
        functools.partial(project_kernel, ahead, n),
        out_shape=(
            jax.ShapeDtypeStruct((rows, cols), jnp.float32),
            jax.ShapeDtypeStruct((rows, cols), jnp.bfloat16),
        ),
        in_specs=[VMEM] * (n + 1),
        out_specs=(VMEM,) * 2,
        compiler_params=params(8),
        name="project",
    )(matrix, *blocks)


def eliminate(matrix, blocks, ahead, wide, narrow, k):
    n, (rows, _), cols = len(blocks), matrix.shape, blocks[0].shape[1]
    return pl.pallas_call(
        functools.partial(eliminate_kernel, ahead, n, k),
        out_shape=jax.ShapeDtypeStruct((rows, cols), jnp.bfloat16),
        in_specs=[VMEM] * (n + 3),
        out_specs=VMEM,
        compiler_params=params(8),
        name="eliminate",
    )(matrix, wide, narrow, *blocks)


def local(source, inverse, coupling):
    inverse, coupling, source = inverse[0], coupling[0], source[0]
    zones = lax.axis_size("zone")
    width = source.shape[1] // CHUNKS
    inverse, coupling = fetch(inverse, coupling)
    results = []
    for c in range(CHUNKS):
        part = source[:, c * width : (c + 1) * width]
        wide, narrow = project(inverse, *gather_source(part))
        for k in range(1, zones):
            narrow = eliminate(coupling, *gather_behind(narrow, k), wide, narrow, k)
        results.append(narrow)
    return jnp.concatenate(results, 1)[None]


def solution(mesh):
    rows = P(("parts", "zone"), "panel", "rhs")
    square = P(("parts", "zone"), "panel", None)
    return jax.shard_map(
        local, mesh=mesh, in_specs=(rows, square, square), out_specs=rows, check_vma=False
    )
```

time: 212 us -> 78 us (0.37)
  blocking collectives: 75.6 us -> 0 us
  waiting for transfers between devices: 77.5 us -> 28.3 us
  matrix products: 36.6 us -> 0 us
  starting transfers between devices: 6.46 us -> 30.1 us
  between operations: 13.4 us -> 0.14 us
  Pallas kernels: 0 us -> 10.5 us
  local copies, waits for them, and re-layouts: 1.05 us -> 7.83 us
    all_gather x5 -> x0, blocking collectives: 75.6 us -> none  [advance(): lax.all_gather(incoming, 'panel', axis=0, tiled=True)]
    all_gather x1 -> x0, waiting for transfers between devices: 48.8 us -> none  [local(): lax.all_gather(local_rhs, 'panel', axis=0, tiled=True)]
    dot_general x6 -> x0, matrix products: 36.6 us -> none  [the longest x5 30.2 us: advance(): jnp.dot(coupling_block, lax.all_gather(incoming, 'panel', axis=0, tiled=T...]
    ppermute x5 -> x14, starting transfers between devices: 6.46 us -> 30.1 us  [the longest x4 15.4 us: gather_behind(): lax.ppermute(own, both, [(p * zones + k, q * zones + k) for p, q in pairs])]
    pallas_call x0 -> x7, Pallas kernels: none -> 10.5 us  [the longest x2 4.67 us: eliminate(): pl.pallas_call(functools.partial(eliminate_kernel, ahead, n, k), out_shap...]
    unnamed x0 -> x4, local copies, waits for them, and re-layouts: none -> 6.76 us
    ppermute x5 -> x14, waiting for transfers between devices: 28 us -> 28.3 us  [the longest x2 10.4 us: gather_source(): down = lax.ppermute(block, 'panel', DOWN)]
  transfers between devices with their start and end apart: 6 -> 14, of which waited for: 6 -> 8; matrix products, arithmetic and copies ran while one was open for 0% -> 0% of each run, Pallas kernels for 0% -> 10%
where the time goes in v1:
time: 78 us; the launch traced here: 77.7 us
  starting transfers between devices  30.1 us (39%)
  waiting for transfers between devices  28.3 us (36%)
  Pallas kernels  10.5 us (13%)
  local copies, waits for them, and re-layouts  7.83 us (10%)
  other arithmetic  0.85 us (1%)
    ppermute x4, starting transfers between devices, gather_behind(): lax.ppermute(own, both, [(p * zones + k, q * zones + k) for p, q in pairs])  15.4 us
    ppermute x2, waiting for transfers between devices, gather_source(): down = lax.ppermute(block, 'panel', DOWN)  10.4 us
    ppermute x2, waiting for transfers between devices, gather_source(): up = lax.ppermute(block, 'panel', UP)  8.2 us
    unnamed x4, local copies, waits for them, and re-layouts  6.76 us
    ppermute x2, starting transfers between devices, gather_source(): down = lax.ppermute(block, 'panel', DOWN)  6.07 us
    pallas_call x2, Pallas kernels, eliminate(): pl.pallas_call(functools.partial(eliminate_kernel, ahead, n, k), out_shap...  4.67 us
    pallas_call x2, Pallas kernels, project(): pl.pallas_call(functools.partial(project_kernel, ahead, n), out_shape=(ja...  4.64 us
    ppermute x2, waiting for transfers between devices, gather_behind(): lax.ppermute(block, 'zone', [(i, (i + 1) % zones) for i in range(zones)])  4.61 us
  transfers between devices with their start and end apart: 14, of which 8 were waited for; matrix products, arithmetic and copies ran while one was open for 0% of the time, Pallas kernels for 10%

profile of v1, /device:TPU:6, one launch (start us, length us, event | category | flops | bytes accessed | tf_op | source)
XLA Modules:
  0.0 77.7 jit_solution(5649722574811563430)
XLA Ops:
  1.1 1.6 %collective-permute-start = (bf16[1024,128]{1,0:T(8,128)(2,1)S(1)}, bf16[1024,128]{1,0:T(8,128)(2,1)S(1)}, u32[]{:S(2)}, u32[]{:S(2)}) collective-permute-start(bf16[1024,128]{1,0:T(8,128)(2,1)S(1)} %get-tuple-element.17.own.refs_0_), channel_id=1, source_target_pairs={{0,4},{4,8},{8,12},{12,0},{1,5},{5,9},{9,13},{13,1},{2,6},{6,10},{... | collective-permute-start | bytes 786440 | tf_op jit(solution)/shard_map/ppermute | solution.py:79
  2.7 2.2 %collective-permute-start.1 = (bf16[1024,128]{1,0:T(8,128)(2,1)S(1)}, bf16[1024,128]{1,0:T(8,128)(2,1)S(1)}, u32[]{:S(2)}, u32[]{:S(2)}) collective-permute-start(bf16[1024,128]{1,0:T(8,128)(2,1)S(1)} %get-tuple-element.17.own.refs_0_), channel_id=1, source_target_pairs={{4,0},{8,4},{12,8},{0,12},{5,1},{9,5},{13,9},{1,13},{6,2},{10,6},{... | collective-permute-start | bytes 786440 | tf_op jit(solution)/shard_map/ppermute | solution.py:80
  4.9 3.8 %collective-permute-start.8 = (bf16[1024,128]{1,0:T(8,128)(2,1)S(1)}, bf16[1024,128]{1,0:T(8,128)(2,1)S(1)}, u32[]{:S(2)}, u32[]{:S(2)}) collective-permute-start(bf16[1024,128]{1,0:T(8,128)(2,1)S(1)} %get-tuple-element.18.own.refs_0_), channel_id=1, source_target_pairs={{4,0},{8,4},{12,8},{0,12},{5,1},{9,5},{13,9},{1,13},{6,2},{10,6},{... | collective-permute-start | bytes 786440 | tf_op jit(solution)/shard_map/ppermute | solution.py:80
  8.8 3.4 %collective-permute-done.up.refs_1_ = bf16[1024,128]{1,0:T(8,128)(2,1)S(1)} collective-permute-done((bf16[1024,128]{1,0:T(8,128)(2,1)S(1)}, bf16[1024,128]{1,0:T(8,128)(2,1)S(1)}, u32[]{:S(2)}, u32[]{:S(2)}) %collective-permute-start) | collective-permute-done | bytes 262176 | tf_op jit(solution)/shard_map/ppermute | solution.py:79
  12.1 5.8 %collective-permute-done.1.down.refs_2_ = bf16[1024,128]{1,0:T(8,128)(2,1)S(1)} collective-permute-done((bf16[1024,128]{1,0:T(8,128)(2,1)S(1)}, bf16[1024,128]{1,0:T(8,128)(2,1)S(1)}, u32[]{:S(2)}, u32[]{:S(2)}) %collective-permute-start.1) | collective-permute-done | bytes 262176 | tf_op jit(solution)/shard_map/ppermute | solution.py:80
  18.6 4.8 %collective-permute-done.7.up.refs_1_ = bf16[1024,128]{1,0:T(8,128)(2,1)S(1)} collective-permute-done((bf16[1024,128]{1,0:T(8,128)(2,1)S(1)}, bf16[1024,128]{1,0:T(8,128)(2,1)S(1)}, u32[]{:S(2)}, u32[]{:S(2)}) %collective-permute-start.7) | collective-permute-done | bytes 262176 | tf_op jit(solution)/shard_map/ppermute | solution.py:79
  23.4 4.6 %collective-permute-done.8.down.refs_2_ = bf16[1024,128]{1,0:T(8,128)(2,1)S(1)} collective-permute-done((bf16[1024,128]{1,0:T(8,128)(2,1)S(1)}, bf16[1024,128]{1,0:T(8,128)(2,1)S(1)}, u32[]{:S(2)}, u32[]{:S(2)}) %collective-permute-start.8) | collective-permute-done | bytes 262176 | tf_op jit(solution)/shard_map/ppermute | solution.py:80
  28.1 1.6 %collective-permute-start.9 = (bf16[1024,128]{1,0:T(8,128)(2,1)S(1)}, bf16[1024,128]{1,0:T(8,128)(2,1)S(1)}, u32[]{:S(2)}, u32[]{:S(2)}) collective-permute-start(bf16[1024,128]{1,0:T(8,128)(2,1)S(1)} %relay.3), channel_id=1, source_target_pairs={{0,8},{12,4},{8,12},{4,0},{1,9},{13,5},{9,13},{5,1},{2,10},{14,6},... | collective-permute-start | bytes 786440 | tf_op jit(solution)/shard_map/ppermute | solution.py:81
  29.7 3.4 %copy-done = bf16[1,1024,4096]{2,1,0:T(8,128)(2,1)S(1)} copy-done((bf16[1,1024,4096]{2,1,0:T(8,128)(2,1)S(1)}, bf16[1,1024,4096]{2,1,0:T(8,128)(2,1)}, u32[]{:S(2)}) %copy-start) | copy-done | bytes 8388632
  33.1 3.4 %copy-done.1 = bf16[1,1024,4096]{2,1,0:T(8,128)(2,1)S(1)} copy-done((bf16[1,1024,4096]{2,1,0:T(8,128)(2,1)S(1)}, bf16[1,1024,4096]{2,1,0:T(8,128)(2,1)}, u32[]{:S(2)}) %copy-start.1) | copy-done | bytes 8388632
  37.6 2.3 %project.2 = (f32[1024,128]{1,0:T(8,128)S(1)}, bf16[1024,128]{1,0:T(8,128)(2,1)S(1)}) custom-call(bf16[1024,4096]{1,0:T(8,128)(2,1)S(1)} %get-tuple-element.12.matrix, bf16[1024,128]{1,0:T(8,128)(2,1)S(1)} %get-tuple-element.17.own.refs_0_, bf16[1024,128]{1,0:T(8,128)(2,1)S(1)} %collective-permute-done.up.refs_1_, ...), custom_call_target="tpu_custom_call" | custom-call | tf_op jit(solution)/shard_map/project/pallas_call | solution.py:138
  40.5 2.3 %project.3 = (f32[1024,128]{1,0:T(8,128)S(1)}, bf16[1024,128]{1,0:T(8,128)(2,1)S(1)}) custom-call(bf16[1024,4096]{1,0:T(8,128)(2,1)S(1)} %get-tuple-element.12.matrix, bf16[1024,128]{1,0:T(8,128)(2,1)S(1)} %get-tuple-element.18.own.refs_0_, bf16[1024,128]{1,0:T(8,128)(2,1)S(1)} %collective-permute-done.7.up.refs_1_, ...), custom_call_target="tpu_custom_call" | custom-call | tf_op jit(solution)/shard_map/project/pallas_call | solution.py:138
  42.9 1.6 %collective-permute-start.10 = (bf16[1024,128]{1,0:T(8,128)(2,1)S(1)}, bf16[1024,128]{1,0:T(8,128)(2,1)S(1)}, u32[]{:S(2)}, u32[]{:S(2)}) collective-permute-start(bf16[1024,128]{1,0:T(8,128)(2,1)S(1)} %get-tuple-element.16.narrow), channel_id=1, source_target_pairs={{0,2},{2,0},{1,3},{3,1},{4,6},{6,4},{5,7},{7,5},{8,10},{10,8},{9,1... | collective-permute-start | bytes 786440 | tf_op jit(solution)/shard_map/ppermute | solution.py:98
  44.4 1.3 %collective-permute-start.4 = (bf16[1024,128]{1,0:T(8,128)(2,1)S(1)}, bf16[1024,128]{1,0:T(8,128)(2,1)S(1)}, u32[]{:S(2)}, u32[]{:S(2)}) collective-permute-start(bf16[1024,128]{1,0:T(8,128)(2,1)S(1)} %get-tuple-element.14.narrow), channel_id=1, source_target_pairs={{0,10},{4,14},{8,2},{12,6},{1,11},{5,15},{9,3},{13,7},{16,26},{20,... | collective-permute-start | bytes 786440 | tf_op jit(solution)/shard_map/ppermute | solution.py:99
  45.7 4.6 %collective-permute-done.3.refs_0_ = bf16[1024,128]{1,0:T(8,128)(2,1)S(1)} collective-permute-done((bf16[1024,128]{1,0:T(8,128)(2,1)S(1)}, bf16[1024,128]{1,0:T(8,128)(2,1)S(1)}, u32[]{:S(2)}, u32[]{:S(2)}) %collective-permute-start.3) | collective-permute-done | bytes 262176 | tf_op jit(solution)/shard_map/ppermute | solution.py:98
  50.3 1.9 %collective-permute-start.5 = (bf16[1024,128]{1,0:T(8,128)(2,1)S(1)}, bf16[1024,128]{1,0:T(8,128)(2,1)S(1)}, u32[]{:S(2)}, u32[]{:S(2)}) collective-permute-start(bf16[1024,128]{1,0:T(8,128)(2,1)S(1)} %collective-permute-done.3.refs_0_), channel_id=1, source_target_pairs={{2,6},{6,10},{10,14},{14,2},{3,7},{7,11},{11,15},{15,3},{18,22},{2... | collective-permute-start | bytes 786440 | tf_op jit(solution)/shard_map/ppermute | solution.py:103
  52.2 5.7 %collective-permute-start.6 = (bf16[1024,128]{1,0:T(8,128)(2,1)S(1)}, bf16[1024,128]{1,0:T(8,128)(2,1)S(1)}, u32[]{:S(2)}, u32[]{:S(2)}) collective-permute-start(bf16[1024,128]{1,0:T(8,128)(2,1)S(1)} %collective-permute-done.3.refs_0_), channel_id=1, source_target_pairs={{6,2},{10,6},{14,10},{2,14},{7,3},{11,7},{15,11},{3,15},{22,18},{2... | collective-permute-start | bytes 786440 | tf_op jit(solution)/shard_map/ppermute | solution.py:103
  58.0 1.3 %collective-permute-start.11 = (bf16[1024,128]{1,0:T(8,128)(2,1)S(1)}, bf16[1024,128]{1,0:T(8,128)(2,1)S(1)}, u32[]{:S(2)}, u32[]{:S(2)}) collective-permute-start(bf16[1024,128]{1,0:T(8,128)(2,1)S(1)} %get-tuple-element.16.narrow), channel_id=1, source_target_pairs={{0,10},{4,14},{8,2},{12,6},{1,11},{5,15},{9,3},{13,7},{16,26},{20,... | collective-permute-start | bytes 786440 | tf_op jit(solution)/shard_map/ppermute | solution.py:99
  59.3 4.6 %collective-permute-start.12 = (bf16[1024,128]{1,0:T(8,128)(2,1)S(1)}, bf16[1024,128]{1,0:T(8,128)(2,1)S(1)}, u32[]{:S(2)}, u32[]{:S(2)}) collective-permute-start(bf16[1024,128]{1,0:T(8,128)(2,1)S(1)} %collective-permute-done.10.refs_0_), channel_id=1, source_target_pairs={{2,6},{6,10},{10,14},{14,2},{3,7},{7,11},{11,15},{15,3},{18,22},{2... | collective-permute-start | bytes 786440 | tf_op jit(solution)/shard_map/ppermute | solution.py:103
  63.9 3.1 %collective-permute-start.13 = (bf16[1024,128]{1,0:T(8,128)(2,1)S(1)}, bf16[1024,128]{1,0:T(8,128)(2,1)S(1)}, u32[]{:S(2)}, u32[]{:S(2)}) collective-permute-start(bf16[1024,128]{1,0:T(8,128)(2,1)S(1)} %collective-permute-done.10.refs_0_), channel_id=1, source_target_pairs={{6,2},{10,6},{14,10},{2,14},{7,3},{11,7},{15,11},{3,15},{22,18},{2... | collective-permute-start | bytes 786440 | tf_op jit(solution)/shard_map/ppermute | solution.py:103
  67.1 2.3 %eliminate.2 = bf16[1024,128]{1,0:T(8,128)(2,1)S(1)} custom-call(bf16[1024,4096]{1,0:T(8,128)(2,1)S(1)} %get-tuple-element.11.matrix, f32[1024,128]{1,0:T(8,128)S(1)} %get-tuple-element.13.wide, bf16[1024,128]{1,0:T(8,128)(2,1)S(1)} %get-tuple-element.14.narrow, bf16[1024,128]{1,0:T(8,128)(2,1)S(1)} %collective-permute-done.3.refs_0_, ...), custom_call_target="tpu_custom_call" | custom-call | tf_op jit(solution)/shard_map/eliminate/pallas_call | solution.py:153
  70.6 1.2 %collective-permute-done.12.refs_2_ = bf16[1024,128]{1,0:T(8,128)(2,1)S(1)} collective-permute-done((bf16[1024,128]{1,0:T(8,128)(2,1)S(1)}, bf16[1024,128]{1,0:T(8,128)(2,1)S(1)}, u32[]{:S(2)}, u32[]{:S(2)}) %collective-permute-start.12) | collective-permute-done | bytes 262176 | tf_op jit(solution)/shard_map/ppermute | solution.py:103
  71.8 2.8 %collective-permute-done.13.refs_3_ = bf16[1024,128]{1,0:T(8,128)(2,1)S(1)} collective-permute-done((bf16[1024,128]{1,0:T(8,128)(2,1)S(1)}, bf16[1024,128]{1,0:T(8,128)(2,1)S(1)}, u32[]{:S(2)}, u32[]{:S(2)}) %collective-permute-start.13) | collective-permute-done | bytes 262176 | tf_op jit(solution)/shard_map/ppermute | solution.py:103
  74.5 2.3 %eliminate.3 = bf16[1024,128]{1,0:T(8,128)(2,1)S(1)} custom-call(bf16[1024,4096]{1,0:T(8,128)(2,1)S(1)} %get-tuple-element.11.matrix, f32[1024,128]{1,0:T(8,128)S(1)} %get-tuple-element.15.wide, bf16[1024,128]{1,0:T(8,128)(2,1)S(1)} %get-tuple-element.16.narrow, bf16[1024,128]{1,0:T(8,128)(2,1)S(1)} %collective-permute-done.10.refs_0_, ...), custom_call_target="tpu_custom_call" | custom-call | tf_op jit(solution)/shard_map/eliminate/pallas_call | solution.py:153
  (17 shorter events, 5.5 us)
Async XLA Ops:
  1.1 11.1 %collective-permute-start = (bf16[1024,128]{1,0:T(8,128)(2,1)S(1)}, bf16[1024,128]{1,0:T(8,128)(2,1)S(1)}, u32[]{:S(2)}, u32[]{:S(2)}) collective-permute-start(bf16[1024,128]{1,0:T(8,128)(2,1)S(1)} %get-tuple-element.17.own.refs_0_), channel_id=1, source_target_pairs={{0,4},{4,8},{8,12},{12,0},{1,5},{5,9},{9,13},{13,1},{2,6},{6,10},{... | collective-permute-start | bytes 786440 | tf_op jit(solution)/shard_map/ppermute | solution.py:79
  2.7 15.2 %collective-permute-start.1 = (bf16[1024,128]{1,0:T(8,128)(2,1)S(1)}, bf16[1024,128]{1,0:T(8,128)(2,1)S(1)}, u32[]{:S(2)}, u32[]{:S(2)}) collective-permute-start(bf16[1024,128]{1,0:T(8,128)(2,1)S(1)} %get-tuple-element.17.own.refs_0_), channel_id=1, source_target_pairs={{4,0},{8,4},{12,8},{0,12},{5,1},{9,5},{13,9},{1,13},{6,2},{10,6},{... | collective-permute-start | bytes 786440 | tf_op jit(solution)/shard_map/ppermute | solution.py:80
  4.9 18.5 %collective-permute-start.7 = (bf16[1024,128]{1,0:T(8,128)(2,1)S(1)}, bf16[1024,128]{1,0:T(8,128)(2,1)S(1)}, u32[]{:S(2)}, u32[]{:S(2)}) collective-permute-start(bf16[1024,128]{1,0:T(8,128)(2,1)S(1)} %get-tuple-element.18.own.refs_0_), channel_id=1, source_target_pairs={{0,4},{4,8},{8,12},{12,0},{1,5},{5,9},{9,13},{13,1},{2,6},{6,10},{... | collective-permute-start | bytes 786440 | tf_op jit(solution)/shard_map/ppermute | solution.py:79
  4.9 23.1 %collective-permute-start.8 = (bf16[1024,128]{1,0:T(8,128)(2,1)S(1)}, bf16[1024,128]{1,0:T(8,128)(2,1)S(1)}, u32[]{:S(2)}, u32[]{:S(2)}) collective-permute-start(bf16[1024,128]{1,0:T(8,128)(2,1)S(1)} %get-tuple-element.18.own.refs_0_), channel_id=1, source_target_pairs={{4,0},{8,4},{12,8},{0,12},{5,1},{9,5},{13,9},{1,13},{6,2},{10,6},{... | collective-permute-start | bytes 786440 | tf_op jit(solution)/shard_map/ppermute | solution.py:80
  17.9 19.7 %collective-permute-start.2 = (bf16[1024,128]{1,0:T(8,128)(2,1)S(1)}, bf16[1024,128]{1,0:T(8,128)(2,1)S(1)}, u32[]{:S(2)}, u32[]{:S(2)}) collective-permute-start(bf16[1024,128]{1,0:T(8,128)(2,1)S(1)} %relay.2), channel_id=1, source_target_pairs={{0,8},{12,4},{8,12},{4,0},{1,9},{13,5},{9,13},{5,1},{2,10},{14,6},... | collective-permute-start | bytes 786440 | tf_op jit(solution)/shard_map/ppermute | solution.py:81
  28.1 12.5 %collective-permute-start.9 = (bf16[1024,128]{1,0:T(8,128)(2,1)S(1)}, bf16[1024,128]{1,0:T(8,128)(2,1)S(1)}, u32[]{:S(2)}, u32[]{:S(2)}) collective-permute-start(bf16[1024,128]{1,0:T(8,128)(2,1)S(1)} %relay.3), channel_id=1, source_target_pairs={{0,8},{12,4},{8,12},{4,0},{1,9},{13,5},{9,13},{5,1},{2,10},{14,6},... | collective-permute-start | bytes 786440 | tf_op jit(solution)/shard_map/ppermute | solution.py:81
  29.7 3.4 %copy-start = (bf16[1,1024,4096]{2,1,0:T(8,128)(2,1)S(1)}, bf16[1,1024,4096]{2,1,0:T(8,128)(2,1)}, u32[]{:S(2)}) copy-start(bf16[1,1024,4096]{2,1,0:T(8,128)(2,1)} %param.4) | copy-start | bytes 25165828
  33.1 3.4 %copy-start.1 = (bf16[1,1024,4096]{2,1,0:T(8,128)(2,1)S(1)}, bf16[1,1024,4096]{2,1,0:T(8,128)(2,1)}, u32[]{:S(2)}) copy-start(bf16[1,1024,4096]{2,1,0:T(8,128)(2,1)} %param.5) | copy-start | bytes 25165828
  39.9 10.4 %collective-permute-start.3 = (bf16[1024,128]{1,0:T(8,128)(2,1)S(1)}, bf16[1024,128]{1,0:T(8,128)(2,1)S(1)}, u32[]{:S(2)}, u32[]{:S(2)}) collective-permute-start(bf16[1024,128]{1,0:T(8,128)(2,1)S(1)} %get-tuple-element.14.narrow), channel_id=1, source_target_pairs={{0,2},{2,0},{1,3},{3,1},{4,6},{6,4},{5,7},{7,5},{8,10},{10,8},{9,1... | collective-permute-start | bytes 786440 | tf_op jit(solution)/shard_map/ppermute | solution.py:98
  42.9 16.4 %collective-permute-start.10 = (bf16[1024,128]{1,0:T(8,128)(2,1)S(1)}, bf16[1024,128]{1,0:T(8,128)(2,1)S(1)}, u32[]{:S(2)}, u32[]{:S(2)}) collective-permute-start(bf16[1024,128]{1,0:T(8,128)(2,1)S(1)} %get-tuple-element.16.narrow), channel_id=1, source_target_pairs={{0,2},{2,0},{1,3},{3,1},{4,6},{6,4},{5,7},{7,5},{8,10},{10,8},{9,1... | collective-permute-start | bytes 786440 | tf_op jit(solution)/shard_map/ppermute | solution.py:98
  44.4 19.5 %collective-permute-start.4 = (bf16[1024,128]{1,0:T(8,128)(2,1)S(1)}, bf16[1024,128]{1,0:T(8,128)(2,1)S(1)}, u32[]{:S(2)}, u32[]{:S(2)}) collective-permute-start(bf16[1024,128]{1,0:T(8,128)(2,1)S(1)} %get-tuple-element.14.narrow), channel_id=1, source_target_pairs={{0,10},{4,14},{8,2},{12,6},{1,11},{5,15},{9,3},{13,7},{16,26},{20,... | collective-permute-start | bytes 786440 | tf_op jit(solution)/shard_map/ppermute | solution.py:99
  50.3 16.7 %collective-permute-start.5 = (bf16[1024,128]{1,0:T(8,128)(2,1)S(1)}, bf16[1024,128]{1,0:T(8,128)(2,1)S(1)}, u32[]{:S(2)}, u32[]{:S(2)}) collective-permute-start(bf16[1024,128]{1,0:T(8,128)(2,1)S(1)} %collective-permute-done.3.refs_0_), channel_id=1, source_target_pairs={{2,6},{6,10},{10,14},{14,2},{3,7},{7,11},{11,15},{15,3},{18,22},{2... | collective-permute-start | bytes 786440 | tf_op jit(solution)/shard_map/ppermute | solution.py:103
  52.2 14.8 %collective-permute-start.6 = (bf16[1024,128]{1,0:T(8,128)(2,1)S(1)}, bf16[1024,128]{1,0:T(8,128)(2,1)S(1)}, u32[]{:S(2)}, u32[]{:S(2)}) collective-permute-start(bf16[1024,128]{1,0:T(8,128)(2,1)S(1)} %collective-permute-done.3.refs_0_), channel_id=1, source_target_pairs={{6,2},{10,6},{14,10},{2,14},{7,3},{11,7},{15,11},{3,15},{22,18},{2... | collective-permute-start | bytes 786440 | tf_op jit(solution)/shard_map/ppermute | solution.py:103
  58.0 12.6 %collective-permute-start.11 = (bf16[1024,128]{1,0:T(8,128)(2,1)S(1)}, bf16[1024,128]{1,0:T(8,128)(2,1)S(1)}, u32[]{:S(2)}, u32[]{:S(2)}) collective-permute-start(bf16[1024,128]{1,0:T(8,128)(2,1)S(1)} %get-tuple-element.16.narrow), channel_id=1, source_target_pairs={{0,10},{4,14},{8,2},{12,6},{1,11},{5,15},{9,3},{13,7},{16,26},{20,... | collective-permute-start | bytes 786440 | tf_op jit(solution)/shard_map/ppermute | solution.py:99
  59.3 12.5 %collective-permute-start.12 = (bf16[1024,128]{1,0:T(8,128)(2,1)S(1)}, bf16[1024,128]{1,0:T(8,128)(2,1)S(1)}, u32[]{:S(2)}, u32[]{:S(2)}) collective-permute-start(bf16[1024,128]{1,0:T(8,128)(2,1)S(1)} %collective-permute-done.10.refs_0_), channel_id=1, source_target_pairs={{2,6},{6,10},{10,14},{14,2},{3,7},{7,11},{11,15},{15,3},{18,22},{2... | collective-permute-start | bytes 786440 | tf_op jit(solution)/shard_map/ppermute | solution.py:103
  63.9 10.6 %collective-permute-start.13 = (bf16[1024,128]{1,0:T(8,128)(2,1)S(1)}, bf16[1024,128]{1,0:T(8,128)(2,1)S(1)}, u32[]{:S(2)}, u32[]{:S(2)}) collective-permute-start(bf16[1024,128]{1,0:T(8,128)(2,1)S(1)} %collective-permute-done.10.refs_0_), channel_id=1, source_target_pairs={{6,2},{10,6},{14,10},{2,14},{7,3},{11,7},{15,11},{3,15},{22,18},{2... | collective-permute-start | bytes 786440 | tf_op jit(solution)/shard_map/ppermute | solution.py:103

commit v2 on v1

v2 whole, which is shorter than its diff:
```python
import functools

import jax
import jax.numpy as jnp
from jax import lax
from jax.experimental import pallas as pl
from jax.experimental.pallas import tpu as pltpu
from jax.sharding import PartitionSpec as P

MIB = 1 << 20
VMEM = pl.BlockSpec(memory_space=pltpu.VMEM)
HBM = pl.BlockSpec(memory_space=pltpu.HBM)


def params(mib):
    return pltpu.CompilerParams(vmem_limit_bytes=mib * MIB)


def fetch_kernel(first, second, first_out, second_out, sems):
    copies = [
        pltpu.make_async_copy(first, first_out, sems.at[0]),
        pltpu.make_async_copy(second, second_out, sems.at[1]),
    ]
    for copy in copies:
        copy.start()
    for copy in copies:
        copy.wait()


def fetch(inverse, coupling):
    shape = jax.ShapeDtypeStruct(inverse.shape, inverse.dtype)
    return pl.pallas_call(
        fetch_kernel,
        out_shape=(shape, shape),
        in_specs=[HBM, HBM],
        out_specs=(VMEM, VMEM),
        scratch_shapes=[pltpu.SemaphoreType.DMA((2,))],
        compiler_params=params(18),
        name="fetch",
    )(inverse, coupling)


def relay_kernel(own, up, down, *rest):
    out = rest[-1]
    me = lax.axis_index("panel")

    @pl.when(me == 2)
    def _():
        out[...] = up[...]

    @pl.when(me == 1)
    def _():
        out[...] = down[...]

    @pl.when(jnp.logical_and(me != 1, me != 2))
    def _():
        out[...] = own[...]


def relay(own, up, down, after=()):
    return pl.pallas_call(
        relay_kernel,
        out_shape=jax.ShapeDtypeStruct(own.shape, own.dtype),
        in_specs=[VMEM] * 3 + [HBM] * len(after),
        out_specs=VMEM,
        compiler_params=params(2),
        name="relay",
    )(own, up, down, *after)


UP = [(0, 1), (1, 2), (2, 3), (3, 0)]
DOWN = [(1, 0), (2, 1), (3, 2), (0, 3)]
ACROSS = [(0, 2), (3, 1), (2, 3), (1, 0)]
STRAIGHT = [(p, (p + 2) % 4) for p in range(4)]
BOTH = ("panel", "zone")
together = lax.optimization_barrier


def to_next_zone(block):
    zones = lax.axis_size("zone")
    return lax.ppermute(block, "zone", [(i, (i + 1) % zones) for i in range(zones)])


def along_panel(block, pairs, source_zone, zone):
    zones = lax.axis_size("zone")
    return lax.ppermute(
        block, BOTH, [(p * zones + source_zone, q * zones + zone) for p, q in pairs]
    )


def product(ahead, matrix, blocks):
    me = lax.axis_index("panel")
    depth = blocks[0].shape[0]
    total = None
    for d, block in zip(ahead, blocks):
        start = pl.multiple_of(lax.rem(me + d, 4) * depth, depth)
        part = jnp.dot(
            matrix[:, pl.ds(start, depth)], block[...], preferred_element_type=jnp.float32
        )
        total = part if total is None else total + part
    return total


def begin_kernel(ahead, matrix, *refs):
    out = refs[-1]
    out[...] = product(ahead, matrix, refs[: len(ahead)])


def begin(matrix, blocks, ahead, after=()):
    (rows, _), cols = matrix.shape, blocks[0].shape[1]
    return pl.pallas_call(
        functools.partial(begin_kernel, ahead),
        out_shape=jax.ShapeDtypeStruct((rows, cols), jnp.float32),
        in_specs=[VMEM] * (len(blocks) + 1) + [HBM] * len(after),
        out_specs=VMEM,
        compiler_params=params(8),
        name="begin",
    )(matrix, *blocks, *after)


def project_kernel(matrix, begun, across, wide, narrow):
    total = begun[...] + product((2,), matrix, [across])
    wide[...] = total
    narrow[...] = total.astype(jnp.bfloat16)


def project(matrix, begun, across):
    return pl.pallas_call(
        project_kernel,
        out_shape=(
            jax.ShapeDtypeStruct(across.shape, jnp.float32),
            jax.ShapeDtypeStruct(across.shape, jnp.bfloat16),
        ),
        in_specs=[VMEM] * 3,
        out_specs=(VMEM,) * 2,
        compiler_params=params(8),
        name="project",
    )(matrix, begun, across)


def finish_kernel(k, matrix, *refs):
    halves, out = (refs[0:4], refs[4:8]), refs[8]
    mine = lax.axis_index("zone") == k
    cols = out.shape[1] // 2
    for half, (begun, across, wide, narrow) in enumerate(halves):
        total = begun[...] + product(((2,), (1,))[half], matrix, [across])
        left = (wide[...] - total).astype(jnp.bfloat16)
        out[:, half * cols : (half + 1) * cols] = jnp.where(mine, left, narrow[...])


def finish(matrix, first, second, k):
    rows, cols = first[-1].shape
    return pl.pallas_call(
        functools.partial(finish_kernel, k),
        out_shape=jax.ShapeDtypeStruct((rows, 2 * cols), jnp.bfloat16),
        in_specs=[VMEM] * 9,
        out_specs=VMEM,
        compiler_params=params(8),
        name="finish",
    )(matrix, *first, *second)


def local_four(source, inverse, coupling):
    zones = lax.axis_size("zone")
    width = source.shape[1] // 2
    first, second = source[:, :width], source[:, width:]
    inverse, coupling = fetch(inverse, coupling)

    up = lax.ppermute(first, "panel", UP)
    down = lax.ppermute(first, "panel", DOWN)
    up2 = lax.ppermute(second, "panel", UP)
    down2 = lax.ppermute(second, "panel", DOWN)
    passed = relay(first, up, down, (inverse, coupling))
    across = lax.ppermute(passed, "panel", ACROSS)
    begun = begin(inverse, [first, up, down], (0, 3, 1), (passed,))
    passed2 = relay(second, up2, down2)
    across2 = lax.ppermute(passed2, "panel", ACROSS)
    begun2 = begin(inverse, [second, up2, down2], (0, 3, 1), (passed2,))
    wide, narrow = project(inverse, begun, across)
    wide2, narrow2 = project(inverse, begun2, across2)

    for k in range(1, zones):
        own = to_next_zone(narrow)
        up = along_panel(own, UP, k, k)
        down = along_panel(own, DOWN, k, k)
        own2 = to_next_zone(narrow2)
        late, late2, own2 = together((narrow, narrow2, own2))
        across = along_panel(late, STRAIGHT, k - 1, k)
        across2 = along_panel(late2, STRAIGHT, k - 1, k)
        up2 = along_panel(own2, UP, k, k)
        down2 = along_panel(own2, DOWN, k, k)
        begun = begin(coupling, [own, up, down], (0, 3, 1))
        begun2 = begin(coupling, [own2, across2, up2], (0, 2, 3))
        both = finish(coupling, (begun, across, wide, narrow), (begun2, down2, wide2, narrow2), k)
        narrow, narrow2 = both[:, :width], both[:, width:]
    return both


def local_any(source, inverse, coupling):
    def gathered(block):
        return lax.all_gather(block, "panel", axis=0, tiled=True)

    wide = jnp.dot(inverse, gathered(source), preferred_element_type=jnp.float32)
    narrow = wide.astype(jnp.bfloat16)
    for k in range(1, lax.axis_size("zone")):
        behind = gathered(to_next_zone(narrow))
        left = wide - jnp.dot(coupling, behind, preferred_element_type=jnp.float32)
        narrow = jnp.where(lax.axis_index("zone") == k, left.astype(jnp.bfloat16), narrow)
    return narrow


def local(source, inverse, coupling):
    run = local_four if lax.axis_size("panel") == 4 else local_any
    return run(source[0], inverse[0], coupling[0])[None]


def solution(mesh):
    rows = P(("parts", "zone"), "panel", "rhs")
    square = P(("parts", "zone"), "panel", None)
    return jax.shard_map(
        local, mesh=mesh, in_specs=(rows, square, square), out_specs=rows, check_vma=False
    )
```

time: 78 us -> 72.7 us (0.932)
  waiting for transfers between devices: 28.3 us -> 22.1 us
  Pallas kernels: 10.5 us -> 11.8 us
  other arithmetic: 0.85 us -> 0 us
    ppermute x14, waiting for transfers between devices: 28.3 us -> 22.1 us  [the longest x1 5.78 us: local_four(): down2 = lax.ppermute(second, 'panel', DOWN)]
    pallas_call x4 -> x7, Pallas kernels: 9.32 us -> 10.6 us  [the longest x4 7.13 us: begin(): pl.pallas_call(functools.partial(begin_kernel, ahead), out_shape=jax.Shap...]
    broadcast_in_dim x1 -> x0, other arithmetic: 0.85 us -> none  [local(): return jnp.concatenate(results, 1)[None]]
  transfers between devices with their start and end apart: 14 -> 14, of which waited for: 8 -> 9; matrix products, arithmetic and copies ran while one was open for 0% -> 0% of each run, Pallas kernels for 10% -> 13%
where the time goes in v2:
time: 72.7 us; the launch traced here: 72.4 us
  starting transfers between devices  30.6 us (42%)
  waiting for transfers between devices  22.1 us (30%)
  Pallas kernels  11.8 us (16%)
  local copies, waits for them, and re-layouts  7.83 us (11%)
    ppermute x6, starting transfers between devices, along_panel(): lax.ppermute(block, BOTH, [(p * zones + source_zone, q * zones + zone) fo...  19.4 us
    pallas_call x4, Pallas kernels, begin(): pl.pallas_call(functools.partial(begin_kernel, ahead), out_shape=jax.Shap...  7.13 us
    unnamed x4, local copies, waits for them, and re-layouts  6.76 us
    ppermute x1, waiting for transfers between devices, local_four(): down2 = lax.ppermute(second, 'panel', DOWN)  5.78 us
    ppermute x6, waiting for transfers between devices, along_panel(): lax.ppermute(block, BOTH, [(p * zones + source_zone, q * zones + zone) fo...  4.45 us
    ppermute x1, starting transfers between devices, local_four(): down = lax.ppermute(first, 'panel', DOWN)  3.82 us
    ppermute x1, waiting for transfers between devices, local_four(): up2 = lax.ppermute(second, 'panel', UP)  3.38 us
    ppermute x2, waiting for transfers between devices, to_next_zone(): lax.ppermute(block, 'zone', [(i, (i + 1) % zones) for i in range(zones)])  2.97 us
  transfers between devices with their start and end apart: 14, of which 9 were waited for; matrix products, arithmetic and copies ran while one was open for 0% of the time, Pallas kernels for 13%

profile of v2, /device:TPU:6, one launch (start us, length us, event | category | flops | bytes accessed | tf_op | source)
XLA Modules:
  0.0 72.4 jit_solution(12218113431888401742)
XLA Ops:
  1.1 1.6 %collective-permute-start.6 = (bf16[1024,128]{1,0:T(8,128)(2,1)S(1)}, bf16[1024,128]{1,0:T(8,128)(2,1)S(1)}, u32[]{:S(2)}, u32[]{:S(2)}) collective-permute-start(bf16[1024,128]{1,0:T(8,128)(2,1)S(1)} %get-tuple-element.23.own.refs_0_), channel_id=1, source_target_pairs={{0,4},{4,8},{8,12},{12,0},{1,5},{5,9},{9,13},{13,1},{2,6},{6,10},{... | collective-permute-start | bytes 786440 | tf_op jit(solution)/shard_map/ppermute | solution.py:171
  2.7 2.2 %collective-permute-start.7 = (bf16[1024,128]{1,0:T(8,128)(2,1)S(1)}, bf16[1024,128]{1,0:T(8,128)(2,1)S(1)}, u32[]{:S(2)}, u32[]{:S(2)}) collective-permute-start(bf16[1024,128]{1,0:T(8,128)(2,1)S(1)} %get-tuple-element.23.own.refs_0_), channel_id=1, source_target_pairs={{4,0},{8,4},{12,8},{0,12},{5,1},{9,5},{13,9},{1,13},{6,2},{10,6},{... | collective-permute-start | bytes 786440 | tf_op jit(solution)/shard_map/ppermute | solution.py:172
  4.9 3.8 %collective-permute-start.1 = (bf16[1024,128]{1,0:T(8,128)(2,1)S(1)}, bf16[1024,128]{1,0:T(8,128)(2,1)S(1)}, u32[]{:S(2)}, u32[]{:S(2)}) collective-permute-start(bf16[1024,128]{1,0:T(8,128)(2,1)S(1)} %get-tuple-element.24.own.refs_0_), channel_id=1, source_target_pairs={{4,0},{8,4},{12,8},{0,12},{5,1},{9,5},{13,9},{1,13},{6,2},{10,6},{... | collective-permute-start | bytes 786440 | tf_op jit(solution)/shard_map/ppermute | solution.py:170
  8.8 3.4 %collective-permute-done.6.up.refs_1_ = bf16[1024,128]{1,0:T(8,128)(2,1)S(1)} collective-permute-done((bf16[1024,128]{1,0:T(8,128)(2,1)S(1)}, bf16[1024,128]{1,0:T(8,128)(2,1)S(1)}, u32[]{:S(2)}, u32[]{:S(2)}) %collective-permute-start.6) | collective-permute-done | bytes 262176 | tf_op jit(solution)/shard_map/ppermute | solution.py:171
  12.1 5.8 %collective-permute-done.7.down.refs_2_ = bf16[1024,128]{1,0:T(8,128)(2,1)S(1)} collective-permute-done((bf16[1024,128]{1,0:T(8,128)(2,1)S(1)}, bf16[1024,128]{1,0:T(8,128)(2,1)S(1)}, u32[]{:S(2)}, u32[]{:S(2)}) %collective-permute-start.7) | collective-permute-done | bytes 262176 | tf_op jit(solution)/shard_map/ppermute | solution.py:172
  18.6 3.4 %copy-done = bf16[1,1024,4096]{2,1,0:T(8,128)(2,1)S(1)} copy-done((bf16[1,1024,4096]{2,1,0:T(8,128)(2,1)S(1)}, bf16[1,1024,4096]{2,1,0:T(8,128)(2,1)}, u32[]{:S(2)}) %copy-start) | copy-done | bytes 8388632
  22.0 3.4 %copy-done.1 = bf16[1,1024,4096]{2,1,0:T(8,128)(2,1)S(1)} copy-done((bf16[1,1024,4096]{2,1,0:T(8,128)(2,1)S(1)}, bf16[1,1024,4096]{2,1,0:T(8,128)(2,1)}, u32[]{:S(2)}) %copy-start.1) | copy-done | bytes 8388632
  26.5 1.5 %collective-permute-done.1.down.refs_2_ = bf16[1024,128]{1,0:T(8,128)(2,1)S(1)} collective-permute-done((bf16[1024,128]{1,0:T(8,128)(2,1)S(1)}, bf16[1024,128]{1,0:T(8,128)(2,1)S(1)}, u32[]{:S(2)}, u32[]{:S(2)}) %collective-permute-start.1) | collective-permute-done | bytes 262176 | tf_op jit(solution)/shard_map/ppermute | solution.py:170
  28.1 1.6 %collective-permute-start.2 = (bf16[1024,128]{1,0:T(8,128)(2,1)S(1)}, bf16[1024,128]{1,0:T(8,128)(2,1)S(1)}, u32[]{:S(2)}, u32[]{:S(2)}) collective-permute-start(bf16[1024,128]{1,0:T(8,128)(2,1)S(1)} %relay.2.refs_3_), channel_id=1, source_target_pairs={{0,8},{12,4},{8,12},{4,0},{1,9},{13,5},{9,13},{5,1},{2,10},{14,6},... | collective-permute-start | bytes 786440 | tf_op jit(solution)/shard_map/ppermute | solution.py:174
  29.7 1.8 %begin.6.begun = f32[1024,128]{1,0:T(8,128)S(1)} custom-call(bf16[1024,4096]{1,0:T(8,128)(2,1)S(1)} %get-tuple-element.15.rest_0_.matrix, bf16[1024,128]{1,0:T(8,128)(2,1)S(1)} %get-tuple-element.23.own.refs_0_, bf16[1024,128]{1,0:T(8,128)(2,1)S(1)} %collective-permute-done.6.up.refs_1_, bf16[1024,128]{1,0:T(8,128)(2,1)S(1)} %collective-permute-done.7.down.refs_2_, ...), custom_call_target="tpu_custom_call" | custom-call | tf_op jit(solution)/shard_map/begin/pallas_call | solution.py:111
  31.5 2.2 %collective-permute-done.8.across = bf16[1024,128]{1,0:T(8,128)(2,1)S(1)} collective-permute-done((bf16[1024,128]{1,0:T(8,128)(2,1)S(1)}, bf16[1024,128]{1,0:T(8,128)(2,1)S(1)}, u32[]{:S(2)}, u32[]{:S(2)}) %collective-permute-start.8) | collective-permute-done | bytes 262176 | tf_op jit(solution)/shard_map/ppermute | solution.py:177
  35.0 1.8 %begin.4.begun = f32[1024,128]{1,0:T(8,128)S(1)} custom-call(bf16[1024,4096]{1,0:T(8,128)(2,1)S(1)} %get-tuple-element.15.rest_0_.matrix, bf16[1024,128]{1,0:T(8,128)(2,1)S(1)} %get-tuple-element.24.own.refs_0_, bf16[1024,128]{1,0:T(8,128)(2,1)S(1)} %collective-permute-done.up.refs_1_, bf16[1024,128]{1,0:T(8,128)(2,1)S(1)} %collective-permute-done.1.down.refs_2_, ...), custom_call_target="tpu_custom_call" | custom-call | tf_op jit(solution)/shard_map/begin/pallas_call | solution.py:111
  36.7 1.8 %collective-permute-done.2.across = bf16[1024,128]{1,0:T(8,128)(2,1)S(1)} collective-permute-done((bf16[1024,128]{1,0:T(8,128)(2,1)S(1)}, bf16[1024,128]{1,0:T(8,128)(2,1)S(1)}, u32[]{:S(2)}, u32[]{:S(2)}) %collective-permute-start.2) | collective-permute-done | bytes 262176 | tf_op jit(solution)/shard_map/ppermute | solution.py:174
  39.9 1.5 %collective-permute-done.9.refs_0_ = bf16[1024,128]{1,0:T(8,128)(2,1)S(1)} collective-permute-done((bf16[1024,128]{1,0:T(8,128)(2,1)S(1)}, bf16[1024,128]{1,0:T(8,128)(2,1)S(1)}, u32[]{:S(2)}, u32[]{:S(2)}) %collective-permute-start.9) | collective-permute-done | bytes 262176 | tf_op jit(solution)/shard_map/ppermute | solution.py:81
  42.6 3.1 %collective-permute-start.12 = (bf16[1024,128]{1,0:T(8,128)(2,1)S(1)}, bf16[1024,128]{1,0:T(8,128)(2,1)S(1)}, u32[]{:S(2)}, u32[]{:S(2)}) collective-permute-start(bf16[1024,128]{1,0:T(8,128)(2,1)S(1)} %collective-permute-done.9.refs_0_), channel_id=1, source_target_pairs={{2,6},{6,10},{10,14},{14,2},{3,7},{7,11},{11,15},{15,3},{18,22},{2... | collective-permute-start | bytes 786440 | tf_op jit(solution)/shard_map/ppermute | solution.py:86
  45.7 1.5 %collective-permute-done.3.refs_0_ = bf16[1024,128]{1,0:T(8,128)(2,1)S(1)} collective-permute-done((bf16[1024,128]{1,0:T(8,128)(2,1)S(1)}, bf16[1024,128]{1,0:T(8,128)(2,1)S(1)}, u32[]{:S(2)}, u32[]{:S(2)}) %collective-permute-start.3) | collective-permute-done | bytes 262176 | tf_op jit(solution)/shard_map/ppermute | solution.py:81
  47.2 8.3 %collective-permute-start.4 = (bf16[1024,128]{1,0:T(8,128)(2,1)S(1)}, bf16[1024,128]{1,0:T(8,128)(2,1)S(1)}, u32[]{:S(2)}, u32[]{:S(2)}) collective-permute-start(bf16[1024,128]{1,0:T(8,128)(2,1)S(1)} %collective-permute-done.3.refs_0_), channel_id=1, source_target_pairs={{2,6},{6,10},{10,14},{14,2},{3,7},{7,11},{11,15},{15,3},{18,22},{2... | collective-permute-start | bytes 786440 | tf_op jit(solution)/shard_map/ppermute | solution.py:86
  55.5 1.9 %collective-permute-start.5 = (bf16[1024,128]{1,0:T(8,128)(2,1)S(1)}, bf16[1024,128]{1,0:T(8,128)(2,1)S(1)}, u32[]{:S(2)}, u32[]{:S(2)}) collective-permute-start(bf16[1024,128]{1,0:T(8,128)(2,1)S(1)} %collective-permute-done.3.refs_0_), channel_id=1, source_target_pairs={{6,2},{10,6},{14,10},{2,14},{7,3},{11,7},{15,11},{3,15},{22,18},{2... | collective-permute-start | bytes 786440 | tf_op jit(solution)/shard_map/ppermute | solution.py:86
  58.8 3.5 %collective-permute-start.13 = (bf16[1024,128]{1,0:T(8,128)(2,1)S(1)}, bf16[1024,128]{1,0:T(8,128)(2,1)S(1)}, u32[]{:S(2)}, u32[]{:S(2)}) collective-permute-start(bf16[1024,128]{1,0:T(8,128)(2,1)S(1)} %collective-permute-done.9.refs_0_), channel_id=1, source_target_pairs={{6,2},{10,6},{14,10},{2,14},{7,3},{11,7},{15,11},{3,15},{22,18},{2... | collective-permute-start | bytes 786440 | tf_op jit(solution)/shard_map/ppermute | solution.py:86
  62.3 1.8 %begin.7.refs_4_ = f32[1024,128]{1,0:T(8,128)S(1)} custom-call(bf16[1024,4096]{1,0:T(8,128)(2,1)S(1)} %get-tuple-element.14.rest_1_.matrix, bf16[1024,128]{1,0:T(8,128)(2,1)S(1)} %collective-permute-done.9.refs_0_, bf16[1024,128]{1,0:T(8,128)(2,1)S(1)} %collective-permute-done.11.refs_1_, bf16[1024,128]{1,0:T(8,128)(2,1)S(1)} %collective-permute-done.12.refs_2_), custom_call_target="tpu_custom_call" | custom-call | tf_op jit(solution)/shard_map/begin/pallas_call | solution.py:111
  64.1 2.6 %collective-permute-done.5.refs_2_ = bf16[1024,128]{1,0:T(8,128)(2,1)S(1)} collective-permute-done((bf16[1024,128]{1,0:T(8,128)(2,1)S(1)}, bf16[1024,128]{1,0:T(8,128)(2,1)S(1)}, u32[]{:S(2)}, u32[]{:S(2)}) %collective-permute-start.5) | collective-permute-done | bytes 262176 | tf_op jit(solution)/shard_map/ppermute | solution.py:86
  66.7 1.8 %begin.5.refs_0_ = f32[1024,128]{1,0:T(8,128)S(1)} custom-call(bf16[1024,4096]{1,0:T(8,128)(2,1)S(1)} %get-tuple-element.14.rest_1_.matrix, bf16[1024,128]{1,0:T(8,128)(2,1)S(1)} %collective-permute-done.3.refs_0_, bf16[1024,128]{1,0:T(8,128)(2,1)S(1)} %collective-permute-done.4.refs_1_, bf16[1024,128]{1,0:T(8,128)(2,1)S(1)} %collective-permute-done.5.refs_2_), custom_call_target="tpu_custom_call" | custom-call | tf_op jit(solution)/shard_map/begin/pallas_call | solution.py:111
  68.4 1.9 %collective-permute-done.10.refs_1_ = bf16[1024,128]{1,0:T(8,128)(2,1)S(1)} collective-permute-done((bf16[1024,128]{1,0:T(8,128)(2,1)S(1)}, bf16[1024,128]{1,0:T(8,128)(2,1)S(1)}, u32[]{:S(2)}, u32[]{:S(2)}) %collective-permute-start.10) | collective-permute-done | bytes 262176 | tf_op jit(solution)/shard_map/ppermute | solution.py:86
  70.3 2.1 %finish.1 = bf16[1024,256]{1,0:T(8,128)(2,1)} custom-call(bf16[1024,4096]{1,0:T(8,128)(2,1)S(1)} %get-tuple-element.14.rest_1_.matrix, f32[1024,128]{1,0:T(8,128)S(1)} %begin.5.refs_0_, bf16[1024,128]{1,0:T(8,128)(2,1)S(1)} %collective-permute-done.10.refs_1_, f32[1024,128]{1,0:T(8,128)S(1)} %get-tuple-element.19.refs_2_, ...), custom_call_target="tpu_custom_call" | custom-call | tf_op jit(solution)/shard_map/finish/pallas_call | solution.py:153
  (19 shorter events, 8.1 us)
Async XLA Ops:
  1.1 11.1 %collective-permute-start.6 = (bf16[1024,128]{1,0:T(8,128)(2,1)S(1)}, bf16[1024,128]{1,0:T(8,128)(2,1)S(1)}, u32[]{:S(2)}, u32[]{:S(2)}) collective-permute-start(bf16[1024,128]{1,0:T(8,128)(2,1)S(1)} %get-tuple-element.23.own.refs_0_), channel_id=1, source_target_pairs={{0,4},{4,8},{8,12},{12,0},{1,5},{5,9},{9,13},{13,1},{2,6},{6,10},{... | collective-permute-start | bytes 786440 | tf_op jit(solution)/shard_map/ppermute | solution.py:171
  2.7 15.2 %collective-permute-start.7 = (bf16[1024,128]{1,0:T(8,128)(2,1)S(1)}, bf16[1024,128]{1,0:T(8,128)(2,1)S(1)}, u32[]{:S(2)}, u32[]{:S(2)}) collective-permute-start(bf16[1024,128]{1,0:T(8,128)(2,1)S(1)} %get-tuple-element.23.own.refs_0_), channel_id=1, source_target_pairs={{4,0},{8,4},{12,8},{0,12},{5,1},{9,5},{13,9},{1,13},{6,2},{10,6},{... | collective-permute-start | bytes 786440 | tf_op jit(solution)/shard_map/ppermute | solution.py:172
  4.9 21.6 %collective-permute-start = (bf16[1024,128]{1,0:T(8,128)(2,1)S(1)}, bf16[1024,128]{1,0:T(8,128)(2,1)S(1)}, u32[]{:S(2)}, u32[]{:S(2)}) collective-permute-start(bf16[1024,128]{1,0:T(8,128)(2,1)S(1)} %get-tuple-element.24.own.refs_0_), channel_id=1, source_target_pairs={{0,4},{4,8},{8,12},{12,0},{1,5},{5,9},{9,13},{13,1},{2,6},{6,10},{... | collective-permute-start | bytes 786440 | tf_op jit(solution)/shard_map/ppermute | solution.py:169
  4.9 23.1 %collective-permute-start.1 = (bf16[1024,128]{1,0:T(8,128)(2,1)S(1)}, bf16[1024,128]{1,0:T(8,128)(2,1)S(1)}, u32[]{:S(2)}, u32[]{:S(2)}) collective-permute-start(bf16[1024,128]{1,0:T(8,128)(2,1)S(1)} %get-tuple-element.24.own.refs_0_), channel_id=1, source_target_pairs={{4,0},{8,4},{12,8},{0,12},{5,1},{9,5},{13,9},{1,13},{6,2},{10,6},{... | collective-permute-start | bytes 786440 | tf_op jit(solution)/shard_map/ppermute | solution.py:170
  17.9 15.7 %collective-permute-start.8 = (bf16[1024,128]{1,0:T(8,128)(2,1)S(1)}, bf16[1024,128]{1,0:T(8,128)(2,1)S(1)}, u32[]{:S(2)}, u32[]{:S(2)}) collective-permute-start(bf16[1024,128]{1,0:T(8,128)(2,1)S(1)} %relay.3.refs_3_), channel_id=1, source_target_pairs={{0,8},{12,4},{8,12},{4,0},{1,9},{13,5},{9,13},{5,1},{2,10},{14,6},... | collective-permute-start | bytes 786440 | tf_op jit(solution)/shard_map/ppermute | solution.py:177
  18.6 3.4 %copy-start = (bf16[1,1024,4096]{2,1,0:T(8,128)(2,1)S(1)}, bf16[1,1024,4096]{2,1,0:T(8,128)(2,1)}, u32[]{:S(2)}) copy-start(bf16[1,1024,4096]{2,1,0:T(8,128)(2,1)} %param.4) | copy-start | bytes 25165828
  22.0 3.4 %copy-start.1 = (bf16[1,1024,4096]{2,1,0:T(8,128)(2,1)S(1)}, bf16[1,1024,4096]{2,1,0:T(8,128)(2,1)}, u32[]{:S(2)}) copy-start(bf16[1,1024,4096]{2,1,0:T(8,128)(2,1)} %param.5) | copy-start | bytes 25165828
  28.1 10.5 %collective-permute-start.2 = (bf16[1024,128]{1,0:T(8,128)(2,1)S(1)}, bf16[1024,128]{1,0:T(8,128)(2,1)S(1)}, u32[]{:S(2)}, u32[]{:S(2)}) collective-permute-start(bf16[1024,128]{1,0:T(8,128)(2,1)S(1)} %relay.2.refs_3_), channel_id=1, source_target_pairs={{0,8},{12,4},{8,12},{4,0},{1,9},{13,5},{9,13},{5,1},{2,10},{14,6},... | collective-permute-start | bytes 786440 | tf_op jit(solution)/shard_map/ppermute | solution.py:174
  34.4 7.0 %collective-permute-start.9 = (bf16[1024,128]{1,0:T(8,128)(2,1)S(1)}, bf16[1024,128]{1,0:T(8,128)(2,1)S(1)}, u32[]{:S(2)}, u32[]{:S(2)}) collective-permute-start(bf16[1024,128]{1,0:T(8,128)(2,1)S(1)} %get-tuple-element.21.refs_7_), channel_id=1, source_target_pairs={{0,2},{2,0},{1,3},{3,1},{4,6},{6,4},{5,7},{7,5},{8,10},{10,8},{9,1... | collective-permute-start | bytes 786440 | tf_op jit(solution)/shard_map/ppermute | solution.py:81
  39.3 8.0 %collective-permute-start.3 = (bf16[1024,128]{1,0:T(8,128)(2,1)S(1)}, bf16[1024,128]{1,0:T(8,128)(2,1)S(1)}, u32[]{:S(2)}, u32[]{:S(2)}) collective-permute-start(bf16[1024,128]{1,0:T(8,128)(2,1)S(1)} %get-tuple-element.18.refs_3_), channel_id=1, source_target_pairs={{0,2},{2,0},{1,3},{3,1},{4,6},{6,4},{5,7},{7,5},{8,10},{10,8},{9,1... | collective-permute-start | bytes 786440 | tf_op jit(solution)/shard_map/ppermute | solution.py:81
  41.3 17.4 %collective-permute-start.11 = (bf16[1024,128]{1,0:T(8,128)(2,1)S(1)}, bf16[1024,128]{1,0:T(8,128)(2,1)S(1)}, u32[]{:S(2)}, u32[]{:S(2)}) collective-permute-start(bf16[1024,128]{1,0:T(8,128)(2,1)S(1)} %get-tuple-element.21.refs_7_), channel_id=1, source_target_pairs={{0,10},{4,14},{8,2},{12,6},{1,11},{5,15},{9,3},{13,7},{16,26},{20,... | collective-permute-start | bytes 786440 | tf_op jit(solution)/shard_map/ppermute | solution.py:86
  42.6 19.7 %collective-permute-start.12 = (bf16[1024,128]{1,0:T(8,128)(2,1)S(1)}, bf16[1024,128]{1,0:T(8,128)(2,1)S(1)}, u32[]{:S(2)}, u32[]{:S(2)}) collective-permute-start(bf16[1024,128]{1,0:T(8,128)(2,1)S(1)} %collective-permute-done.9.refs_0_), channel_id=1, source_target_pairs={{2,6},{6,10},{10,14},{14,2},{3,7},{7,11},{11,15},{15,3},{18,22},{2... | collective-permute-start | bytes 786440 | tf_op jit(solution)/shard_map/ppermute | solution.py:86
  47.2 16.8 %collective-permute-start.4 = (bf16[1024,128]{1,0:T(8,128)(2,1)S(1)}, bf16[1024,128]{1,0:T(8,128)(2,1)S(1)}, u32[]{:S(2)}, u32[]{:S(2)}) collective-permute-start(bf16[1024,128]{1,0:T(8,128)(2,1)S(1)} %collective-permute-done.3.refs_0_), channel_id=1, source_target_pairs={{2,6},{6,10},{10,14},{14,2},{3,7},{7,11},{11,15},{15,3},{18,22},{2... | collective-permute-start | bytes 786440 | tf_op jit(solution)/shard_map/ppermute | solution.py:86
  55.5 11.1 %collective-permute-start.5 = (bf16[1024,128]{1,0:T(8,128)(2,1)S(1)}, bf16[1024,128]{1,0:T(8,128)(2,1)S(1)}, u32[]{:S(2)}, u32[]{:S(2)}) collective-permute-start(bf16[1024,128]{1,0:T(8,128)(2,1)S(1)} %collective-permute-done.3.refs_0_), channel_id=1, source_target_pairs={{6,2},{10,6},{14,10},{2,14},{7,3},{11,7},{15,11},{3,15},{22,18},{2... | collective-permute-start | bytes 786440 | tf_op jit(solution)/shard_map/ppermute | solution.py:86
  57.4 12.9 %collective-permute-start.10 = (bf16[1024,128]{1,0:T(8,128)(2,1)S(1)}, bf16[1024,128]{1,0:T(8,128)(2,1)S(1)}, u32[]{:S(2)}, u32[]{:S(2)}) collective-permute-start(bf16[1024,128]{1,0:T(8,128)(2,1)S(1)} %get-tuple-element.18.refs_3_), channel_id=1, source_target_pairs={{0,10},{4,14},{8,2},{12,6},{1,11},{5,15},{9,3},{13,7},{16,26},{20,... | collective-permute-start | bytes 786440 | tf_op jit(solution)/shard_map/ppermute | solution.py:86
  58.8 11.6 %collective-permute-start.13 = (bf16[1024,128]{1,0:T(8,128)(2,1)S(1)}, bf16[1024,128]{1,0:T(8,128)(2,1)S(1)}, u32[]{:S(2)}, u32[]{:S(2)}) collective-permute-start(bf16[1024,128]{1,0:T(8,128)(2,1)S(1)} %collective-permute-done.9.refs_0_), channel_id=1, source_target_pairs={{6,2},{10,6},{14,10},{2,14},{7,3},{11,7},{15,11},{3,15},{22,18},{2... | collective-permute-start | bytes 786440 | tf_op jit(solution)/shard_map/ppermute | solution.py:86

commit v3 on v2

v3 whole, which is shorter than its diff:
```python
import functools

import jax
import jax.numpy as jnp
from jax import lax
from jax.experimental import pallas as pl
from jax.experimental.pallas import tpu as pltpu
from jax.sharding import PartitionSpec as P

MIB = 1 << 20
VMEM = pl.BlockSpec(memory_space=pltpu.VMEM)
HBM = pl.BlockSpec(memory_space=pltpu.HBM)


def params(mib):
    return pltpu.CompilerParams(vmem_limit_bytes=mib * MIB)


def fetch_kernel(first, second, first_out, second_out, sems):
    copies = [
        pltpu.make_async_copy(first, first_out, sems.at[0]),
        pltpu.make_async_copy(second, second_out, sems.at[1]),
    ]
    for copy in copies:
        copy.start()
    for copy in copies:
        copy.wait()


def fetch(inverse, coupling):
    shape = jax.ShapeDtypeStruct(inverse.shape, inverse.dtype)
    return pl.pallas_call(
        fetch_kernel,
        out_shape=(shape, shape),
        in_specs=[HBM, HBM],
        out_specs=(VMEM, VMEM),
        scratch_shapes=[pltpu.SemaphoreType.DMA((2,))],
        compiler_params=params(18),
        name="fetch",
    )(inverse, coupling)


together = lax.optimization_barrier


def swap_panels(block, apart):
    return lax.ppermute(block, "panel", [(p, p ^ apart) for p in range(4)])


def across_zones(block, pairs):
    zones = lax.axis_size("zone")
    return lax.ppermute(
        block, ("panel", "zone"), [(a * zones + y, b * zones + z) for a, y, b, z in pairs]
    )


def swap_in_zone(block, apart, k):
    return across_zones(block, [(p, k, p ^ apart, k) for p in range(4)])


def swap_zones(block, k):
    return straight(block, 0, k)


def straight(block, apart, k):
    there = [(p, k - 1, p ^ apart, k) for p in range(4)]
    return across_zones(block, there + [(p, k, p, k - 1) for p in range(4)])


def product(apart, matrix, blocks):
    me = lax.axis_index("panel")
    depth = blocks[0].shape[0]
    total = None
    for d, block in zip(apart, blocks):
        start = pl.multiple_of((me ^ d) * depth, depth)
        part = jnp.dot(
            matrix[:, pl.ds(start, depth)], block[...], preferred_element_type=jnp.float32
        )
        total = part if total is None else total + part
    return total


def begin_kernel(apart, base, matrix, *refs):
    out = refs[-1]
    total = product(apart, matrix, refs[base : base + len(apart)])
    out[...] = refs[0][...] - total if base else total


def begin(matrix, blocks, apart, wide=None, after=()):
    (rows, _), cols = matrix.shape, blocks[0].shape[1]
    held = (matrix,) if wide is None else (matrix, wide)
    return pl.pallas_call(
        functools.partial(begin_kernel, apart, len(held) - 1),
        out_shape=jax.ShapeDtypeStruct((rows, cols), jnp.float32),
        in_specs=[VMEM] * (len(held) + len(blocks)) + [HBM] * len(after),
        out_specs=VMEM,
        compiler_params=params(8),
        name="begin",
    )(*held, *blocks, *after)


def project_kernel(matrix, begun, across, wide, narrow):
    total = begun[...] + product((2,), matrix, [across])
    wide[...] = total
    narrow[...] = total.astype(jnp.bfloat16)


def project(matrix, begun, across):
    return pl.pallas_call(
        project_kernel,
        out_shape=(
            jax.ShapeDtypeStruct(across.shape, jnp.float32),
            jax.ShapeDtypeStruct(across.shape, jnp.bfloat16),
        ),
        in_specs=[VMEM] * 3,
        out_specs=(VMEM,) * 2,
        compiler_params=params(8),
        name="project",
    )(matrix, begun, across)


def finish_kernel(plan, k, matrix, *refs):
    left, narrow, blocks, out = refs[0:2], refs[2:4], list(refs[4:-1]), refs[-1]
    me = lax.axis_index("panel")
    mine = lax.axis_index("zone") == k
    depth, cols = blocks[0].shape
    totals = [None, None]
    for apart, halves in plan:
        start = pl.multiple_of((me ^ apart) * depth, depth)
        here, blocks = [block[...] for block in blocks[: len(halves)]], blocks[len(halves) :]
        block = here[0] if len(here) == 1 else jnp.concatenate(here, axis=1)
        part = jnp.dot(
            matrix[:, pl.ds(start, depth)], block, preferred_element_type=jnp.float32
        )
        for i, half in enumerate(halves):
            mine_part = part[:, i * cols : (i + 1) * cols]
            totals[half] = mine_part if totals[half] is None else totals[half] + mine_part
    for half, total in enumerate(totals):
        rest = (left[half][...] - total).astype(jnp.bfloat16)
        out[:, half * cols : (half + 1) * cols] = jnp.where(mine, rest, narrow[half][...])


def finish(matrix, left, narrow, last, k):
    rows, cols = narrow[0].shape
    plan = tuple((apart, tuple(blocks)) for apart, blocks in last)
    operands = (matrix, *left, *narrow, *(b for _, blocks in last for b in blocks.values()))
    return pl.pallas_call(
        functools.partial(finish_kernel, plan, k),
        out_shape=jax.ShapeDtypeStruct((rows, 2 * cols), jnp.bfloat16),
        in_specs=[VMEM] * len(operands),
        out_specs=VMEM,
        compiler_params=params(8),
        name="finish",
    )(*operands)


def local_four(source, inverse, coupling):
    zones = lax.axis_size("zone")
    width = source.shape[1] // 2
    first, second = source[:, :width], source[:, width:]
    inverse, coupling = fetch(inverse, coupling)

    far = swap_panels(first, 3)
    near = swap_panels(first, 1)
    passed, _ = together((far, inverse))
    across = swap_panels(passed, 1)
    second, _ = together((second, far))
    far2 = swap_panels(second, 3)
    begun = begin(inverse, [first, near, far], (0, 1, 3))
    wide, narrow = project(inverse, begun, across)
    near2 = swap_panels(second, 1)
    across2 = swap_panels(far2, 1)
    begun2 = begin(inverse, [second, near2, far2], (0, 1, 3))
    wide2, narrow2 = project(inverse, begun2, across2)

    for k in range(1, zones):
        own = swap_zones(narrow, k)
        own2 = swap_zones(narrow2, k)
        far = swap_in_zone(own, 3, k)
        near = swap_in_zone(own, 1, k)
        across = swap_in_zone(far, 1, k)
        near2 = swap_in_zone(own2, 1, k)
        far2 = straight(narrow2, 3, k)
        across2 = straight(narrow2, 2, k)
        left = begin(coupling, [own, far, across], (0, 3, 2,), wide)
        left2 = begin(coupling, [own2, far2], (0, 3,), wide2)
        both = finish(
            coupling, (left, left2), (narrow, narrow2), [(1, {0: near, 1: near2}), (2, {1: across2})], k
        )
        narrow, narrow2 = both[:, :width], both[:, width:]
    return both


def local_any(source, inverse, coupling):
    def gathered(block):
        return lax.all_gather(block, "panel", axis=0, tiled=True)

    wide = jnp.dot(inverse, gathered(source), preferred_element_type=jnp.float32)
    narrow = wide.astype(jnp.bfloat16)
    zones = lax.axis_size("zone")
    for k in range(1, zones):
        sent = lax.ppermute(narrow, "zone", [(z, (z + 1) % zones) for z in range(zones)])
        behind = gathered(sent)
        left = wide - jnp.dot(coupling, behind, preferred_element_type=jnp.float32)
        narrow = jnp.where(lax.axis_index("zone") == k, left.astype(jnp.bfloat16), narrow)
    return narrow


def local(source, inverse, coupling):
    run = local_four if lax.axis_size("panel") == 4 else local_any
    return run(source[0], inverse[0], coupling[0])[None]


def solution(mesh):
    rows = P(("parts", "zone"), "panel", "rhs")
    square = P(("parts", "zone"), "panel", None)
    return jax.shard_map(
        local, mesh=mesh, in_specs=(rows, square, square), out_specs=rows, check_vma=False
    )
```

time: 72.7 us -> 68.2 us (0.938)
  starting transfers between devices: 30.6 us -> 26.1 us
    ppermute x14, starting transfers between devices: 30.6 us -> 26.1 us  [the longest x8 13.7 us: across_zones(): lax.ppermute(block, ('panel', 'zone'), [(a * zones + y, b * zones + z) fo...]
    pallas_call x7 -> x5, Pallas kernels: 9.22 us -> 8.65 us  [the longest x4 6.6 us: begin(): pl.pallas_call(functools.partial(begin_kernel, apart, len(held) - 1), out...]
where the time goes in v3:
time: 68.2 us; the launch traced here: 67.9 us
  starting transfers between devices  26.1 us (38%)
  waiting for transfers between devices  22.7 us (33%)
  Pallas kernels  11.2 us (16%)
  local copies, waits for them, and re-layouts  7.83 us (11%)
    ppermute x8, starting transfers between devices, across_zones(): lax.ppermute(block, ('panel', 'zone'), [(a * zones + y, b * zones + z) fo...  13.7 us
    ppermute x6, starting transfers between devices, swap_panels(): return lax.ppermute(block, 'panel', [(p, p ^ apart) for p in range(4)])  12.3 us
    ppermute x6, waiting for transfers between devices, swap_panels(): return lax.ppermute(block, 'panel', [(p, p ^ apart) for p in range(4)])  12.3 us
    ppermute x8, waiting for transfers between devices, across_zones(): lax.ppermute(block, ('panel', 'zone'), [(a * zones + y, b * zones + z) fo...  10.4 us
    unnamed x4, local copies, waits for them, and re-layouts  6.76 us
    pallas_call x4, Pallas kernels, begin(): pl.pallas_call(functools.partial(begin_kernel, apart, len(held) - 1), out...  6.6 us
    pallas_call x1, Pallas kernels, finish(): pl.pallas_call(functools.partial(finish_kernel, plan, k), out_shape=jax.S...  2.05 us
    pallas_call x2, Pallas kernels, project(): pl.pallas_call(project_kernel, out_shape=(jax.ShapeDtypeStruct(across.sha...  1.42 us
  transfers between devices with their start and end apart: 14, of which 9 were waited for; matrix products, arithmetic and copies ran while one was open for 0% of the time, Pallas kernels for 13%

profile of v3, /device:TPU:6, one launch (start us, length us, event | category | flops | bytes accessed | tf_op | source)
XLA Modules:
  0.0 67.9 jit_solution(6318297061750514195)
XLA Ops:
  1.1 3.7 %collective-permute-start.1 = (bf16[1024,128]{1,0:T(8,128)(2,1)S(1)}, bf16[1024,128]{1,0:T(8,128)(2,1)S(1)}, u32[]{:S(2)}, u32[]{:S(2)}) collective-permute-start(bf16[1024,128]{1,0:T(8,128)(2,1)S(1)} %get-tuple-element.22.refs_0_), channel_id=1, source_target_pairs={{0,12},{4,8},{8,4},{12,0},{1,13},{5,9},{9,5},{13,1},{2,14},{6,10},... | collective-permute-start | bytes 786440 | tf_op jit(solution)/shard_map/ppermute | solution.py:47
  4.7 3.4 %copy-done = bf16[1,1024,4096]{2,1,0:T(8,128)(2,1)S(1)} copy-done((bf16[1,1024,4096]{2,1,0:T(8,128)(2,1)S(1)}, bf16[1,1024,4096]{2,1,0:T(8,128)(2,1)}, u32[]{:S(2)}) %copy-start) | copy-done | bytes 8388632
  8.1 3.4 %copy-done.1 = bf16[1,1024,4096]{2,1,0:T(8,128)(2,1)S(1)} copy-done((bf16[1,1024,4096]{2,1,0:T(8,128)(2,1)S(1)}, bf16[1,1024,4096]{2,1,0:T(8,128)(2,1)}, u32[]{:S(2)}) %copy-start.1) | copy-done | bytes 8388632
  11.5 1.1 %fetch.1 = (bf16[1024,4096]{1,0:T(8,128)(2,1)S(1)}, bf16[1024,4096]{1,0:T(8,128)(2,1)S(1)}) custom-call(bf16[1024,4096]{1,0:T(8,128)(2,1)S(1)} %bitcast.4, bf16[1024,4096]{1,0:T(8,128)(2,1)S(1)} %bitcast.5), custom_call_target="tpu_custom_call" | custom-call | tf_op jit(solution)/shard_map/fetch/pallas_call | solution.py:32
  12.7 3.7 %collective-permute-start.2 = (bf16[1024,128]{1,0:T(8,128)(2,1)S(1)}, bf16[1024,128]{1,0:T(8,128)(2,1)S(1)}, u32[]{:S(2)}, u32[]{:S(2)}) collective-permute-start(bf16[1024,128]{1,0:T(8,128)(2,1)S(1)} %collective-permute-done.1.refs_2_), channel_id=1, source_target_pairs={{0,4},{4,0},{8,12},{12,8},{1,5},{5,1},{9,13},{13,9},{2,6},{6,2},{1... | collective-permute-start | bytes 786440 | tf_op jit(solution)/shard_map/ppermute | solution.py:47
  16.4 2.5 %collective-permute-start.7 = (bf16[1024,128]{1,0:T(8,128)(2,1)S(1)}, bf16[1024,128]{1,0:T(8,128)(2,1)S(1)}, u32[]{:S(2)}, u32[]{:S(2)}) collective-permute-start(bf16[1024,128]{1,0:T(8,128)(2,1)S(1)} %get-tuple-element.18.refs_0_), channel_id=1, source_target_pairs={{0,12},{4,8},{8,4},{12,0},{1,13},{5,9},{9,5},{13,1},{2,14},{6,10},... | collective-permute-start | bytes 786440 | tf_op jit(solution)/shard_map/ppermute | solution.py:47
  18.9 1.8 %begin.4.begun = f32[1024,128]{1,0:T(8,128)S(1)} custom-call(bf16[1024,4096]{1,0:T(8,128)(2,1)S(1)} %get-tuple-element.14.matrix, bf16[1024,128]{1,0:T(8,128)(2,1)S(1)} %get-tuple-element.22.refs_0_, bf16[1024,128]{1,0:T(8,128)(2,1)S(1)} %collective-permute-done.refs_1_, bf16[1024,128]{1,0:T(8,128)(2,1)S(1)} %collective-permute-done.1.refs_2_), custom_call_target="tpu_custom_call" | custom-call | tf_op jit(solution)/shard_map/begin/pallas_call | solution.py:92
  20.6 2.5 %collective-permute-done.2.across = bf16[1024,128]{1,0:T(8,128)(2,1)S(1)} collective-permute-done((bf16[1024,128]{1,0:T(8,128)(2,1)S(1)}, bf16[1024,128]{1,0:T(8,128)(2,1)S(1)}, u32[]{:S(2)}, u32[]{:S(2)}) %collective-permute-start.2) | collective-permute-done | bytes 262176 | tf_op jit(solution)/shard_map/ppermute | solution.py:47
  24.5 2.5 %collective-permute-start.6 = (bf16[1024,128]{1,0:T(8,128)(2,1)S(1)}, bf16[1024,128]{1,0:T(8,128)(2,1)S(1)}, u32[]{:S(2)}, u32[]{:S(2)}) collective-permute-start(bf16[1024,128]{1,0:T(8,128)(2,1)S(1)} %get-tuple-element.18.refs_0_), channel_id=1, source_target_pairs={{0,4},{4,0},{8,12},{12,8},{1,5},{5,1},{9,13},{13,9},{2,6},{6,2},{1... | collective-permute-start | bytes 786440 | tf_op jit(solution)/shard_map/ppermute | solution.py:47
  26.9 4.7 %collective-permute-done.7.refs_2_ = bf16[1024,128]{1,0:T(8,128)(2,1)S(1)} collective-permute-done((bf16[1024,128]{1,0:T(8,128)(2,1)S(1)}, bf16[1024,128]{1,0:T(8,128)(2,1)S(1)}, u32[]{:S(2)}, u32[]{:S(2)}) %collective-permute-start.7) | collective-permute-done | bytes 262176 | tf_op jit(solution)/shard_map/ppermute | solution.py:47
  31.7 3.3 %collective-permute-start.4 = (bf16[1024,128]{1,0:T(8,128)(2,1)S(1)}, bf16[1024,128]{1,0:T(8,128)(2,1)S(1)}, u32[]{:S(2)}, u32[]{:S(2)}) collective-permute-start(bf16[1024,128]{1,0:T(8,128)(2,1)S(1)} %collective-permute-done.3.refs_1_), channel_id=1, source_target_pairs={{2,14},{6,10},{10,6},{14,2},{3,15},{7,11},{11,7},{15,3},{18,30},{2... | collective-permute-start | bytes 786440 | tf_op jit(solution)/shard_map/ppermute | solution.py:52
  35.8 1.8 %begin.6.begun = f32[1024,128]{1,0:T(8,128)S(1)} custom-call(bf16[1024,4096]{1,0:T(8,128)(2,1)S(1)} %get-tuple-element.14.matrix, bf16[1024,128]{1,0:T(8,128)(2,1)S(1)} %get-tuple-element.18.refs_0_, bf16[1024,128]{1,0:T(8,128)(2,1)S(1)} %collective-permute-done.6.refs_1_, bf16[1024,128]{1,0:T(8,128)(2,1)S(1)} %collective-permute-done.7.refs_2_), custom_call_target="tpu_custom_call" | custom-call | tf_op jit(solution)/shard_map/begin/pallas_call | solution.py:92
  37.5 4.2 %collective-permute-done.8.across = bf16[1024,128]{1,0:T(8,128)(2,1)S(1)} collective-permute-done((bf16[1024,128]{1,0:T(8,128)(2,1)S(1)}, bf16[1024,128]{1,0:T(8,128)(2,1)S(1)}, u32[]{:S(2)}, u32[]{:S(2)}) %collective-permute-start.8) | collective-permute-done | bytes 262176 | tf_op jit(solution)/shard_map/ppermute | solution.py:47
  42.5 2.0 %collective-permute-start.10 = (bf16[1024,128]{1,0:T(8,128)(2,1)S(1)}, bf16[1024,128]{1,0:T(8,128)(2,1)S(1)}, u32[]{:S(2)}, u32[]{:S(2)}) collective-permute-start(bf16[1024,128]{1,0:T(8,128)(2,1)S(1)} %get-tuple-element.20.refs_3_), channel_id=1, source_target_pairs={{0,14},{4,10},{8,6},{12,2},{2,0},{6,4},{10,8},{14,12},{1,15},{5,11... | collective-permute-start | bytes 786440 | tf_op jit(solution)/shard_map/ppermute | solution.py:52
  44.6 2.0 %collective-permute-done.4.refs_2_ = bf16[1024,128]{1,0:T(8,128)(2,1)S(1)} collective-permute-done((bf16[1024,128]{1,0:T(8,128)(2,1)S(1)}, bf16[1024,128]{1,0:T(8,128)(2,1)S(1)}, u32[]{:S(2)}, u32[]{:S(2)}) %collective-permute-start.4) | collective-permute-done | bytes 262176 | tf_op jit(solution)/shard_map/ppermute | solution.py:52
  46.6 2.9 %collective-permute-start.5 = (bf16[1024,128]{1,0:T(8,128)(2,1)S(1)}, bf16[1024,128]{1,0:T(8,128)(2,1)S(1)}, u32[]{:S(2)}, u32[]{:S(2)}) collective-permute-start(bf16[1024,128]{1,0:T(8,128)(2,1)S(1)} %collective-permute-done.4.refs_2_), channel_id=1, source_target_pairs={{2,6},{6,2},{10,14},{14,10},{3,7},{7,3},{11,15},{15,11},{18,22},{2... | collective-permute-start | bytes 786440 | tf_op jit(solution)/shard_map/ppermute | solution.py:52
  49.6 2.9 %collective-permute-start.11 = (bf16[1024,128]{1,0:T(8,128)(2,1)S(1)}, bf16[1024,128]{1,0:T(8,128)(2,1)S(1)}, u32[]{:S(2)}, u32[]{:S(2)}) collective-permute-start(bf16[1024,128]{1,0:T(8,128)(2,1)S(1)} %collective-permute-done.3.refs_1_), channel_id=1, source_target_pairs={{2,6},{6,2},{10,14},{14,10},{3,7},{7,3},{11,15},{15,11},{18,22},{2... | collective-permute-start | bytes 786440 | tf_op jit(solution)/shard_map/ppermute | solution.py:52
  52.5 2.2 %collective-permute-done.9.refs_1_ = bf16[1024,128]{1,0:T(8,128)(2,1)S(1)} collective-permute-done((bf16[1024,128]{1,0:T(8,128)(2,1)S(1)}, bf16[1024,128]{1,0:T(8,128)(2,1)S(1)}, u32[]{:S(2)}, u32[]{:S(2)}) %collective-permute-start.9) | collective-permute-done | bytes 262176 | tf_op jit(solution)/shard_map/ppermute | solution.py:52
  54.7 1.9 %collective-permute-start.12 = (bf16[1024,128]{1,0:T(8,128)(2,1)S(1)}, bf16[1024,128]{1,0:T(8,128)(2,1)S(1)}, u32[]{:S(2)}, u32[]{:S(2)}) collective-permute-start(bf16[1024,128]{1,0:T(8,128)(2,1)S(1)} %collective-permute-done.9.refs_1_), channel_id=1, source_target_pairs={{2,6},{6,2},{10,14},{14,10},{3,7},{7,3},{11,15},{15,11},{18,22},{2... | collective-permute-start | bytes 786440 | tf_op jit(solution)/shard_map/ppermute | solution.py:52
  56.6 1.2 %begin.7.refs_1_ = f32[1024,128]{1,0:T(8,128)S(1)} custom-call(bf16[1024,4096]{1,0:T(8,128)(2,1)S(1)} %get-tuple-element.13.matrix, f32[1024,128]{1,0:T(8,128)S(1)} %get-tuple-element.19.refs_0_, bf16[1024,128]{1,0:T(8,128)(2,1)S(1)} %collective-permute-done.9.refs_1_, bf16[1024,128]{1,0:T(8,128)(2,1)S(1)} %collective-permute-done.10.refs_2_), custom_call_target="tpu_custom_call" | custom-call | tf_op jit(solution)/shard_map/begin/pallas_call | solution.py:92
  57.8 1.8 %begin.5.refs_0_ = f32[1024,128]{1,0:T(8,128)S(1)} custom-call(bf16[1024,4096]{1,0:T(8,128)(2,1)S(1)} %get-tuple-element.13.matrix, f32[1024,128]{1,0:T(8,128)S(1)} %get-tuple-element.16.refs_0_, bf16[1024,128]{1,0:T(8,128)(2,1)S(1)} %collective-permute-done.3.refs_1_, bf16[1024,128]{1,0:T(8,128)(2,1)S(1)} %collective-permute-done.4.refs_2_, ...), custom_call_target="tpu_custom_call" | custom-call | tf_op jit(solution)/shard_map/begin/pallas_call | solution.py:92
  59.6 3.4 %collective-permute-done.11.refs_4_ = bf16[1024,128]{1,0:T(8,128)(2,1)S(1)} collective-permute-done((bf16[1024,128]{1,0:T(8,128)(2,1)S(1)}, bf16[1024,128]{1,0:T(8,128)(2,1)S(1)}, u32[]{:S(2)}, u32[]{:S(2)}) %collective-permute-start.11) | collective-permute-done | bytes 262176 | tf_op jit(solution)/shard_map/ppermute | solution.py:52
  63.1 2.7 %collective-permute-done.13.refs_6_ = bf16[1024,128]{1,0:T(8,128)(2,1)S(1)} collective-permute-done((bf16[1024,128]{1,0:T(8,128)(2,1)S(1)}, bf16[1024,128]{1,0:T(8,128)(2,1)S(1)}, u32[]{:S(2)}, u32[]{:S(2)}) %collective-permute-start.13) | collective-permute-done | bytes 262176 | tf_op jit(solution)/shard_map/ppermute | solution.py:52
  65.9 2.0 %finish.1 = bf16[1024,256]{1,0:T(8,128)(2,1)} custom-call(bf16[1024,4096]{1,0:T(8,128)(2,1)S(1)} %get-tuple-element.13.matrix, f32[1024,128]{1,0:T(8,128)S(1)} %begin.5.refs_0_, f32[1024,128]{1,0:T(8,128)S(1)} %begin.7.refs_1_, bf16[1024,128]{1,0:T(8,128)(2,1)S(1)} %get-tuple-element.17.refs_2_, bf16[1024,128]{1,0:T(8,128)(2,1)S(1)} %get-tuple-element.20.refs_3_, ...), custom_call_target="tpu_custom_call" | custom-call | tf_op jit(solution)/shard_map/finish/pallas_call | solution.py:147
  (17 shorter events, 4.2 us)
Async XLA Ops:
  1.1 11.6 %collective-permute-start.1 = (bf16[1024,128]{1,0:T(8,128)(2,1)S(1)}, bf16[1024,128]{1,0:T(8,128)(2,1)S(1)}, u32[]{:S(2)}, u32[]{:S(2)}) collective-permute-start(bf16[1024,128]{1,0:T(8,128)(2,1)S(1)} %get-tuple-element.22.refs_0_), channel_id=1, source_target_pairs={{0,12},{4,8},{8,4},{12,0},{1,13},{5,9},{9,5},{13,1},{2,14},{6,10},... | collective-permute-start | bytes 786440 | tf_op jit(solution)/shard_map/ppermute | solution.py:47
  4.7 14.1 %collective-permute-start = (bf16[1024,128]{1,0:T(8,128)(2,1)S(1)}, bf16[1024,128]{1,0:T(8,128)(2,1)S(1)}, u32[]{:S(2)}, u32[]{:S(2)}) collective-permute-start(bf16[1024,128]{1,0:T(8,128)(2,1)S(1)} %get-tuple-element.22.refs_0_), channel_id=1, source_target_pairs={{0,4},{4,0},{8,12},{12,8},{1,5},{5,1},{9,13},{13,9},{2,6},{6,2},{1... | collective-permute-start | bytes 786440 | tf_op jit(solution)/shard_map/ppermute | solution.py:47
  4.7 3.4 %copy-start = (bf16[1,1024,4096]{2,1,0:T(8,128)(2,1)S(1)}, bf16[1,1024,4096]{2,1,0:T(8,128)(2,1)}, u32[]{:S(2)}) copy-start(bf16[1,1024,4096]{2,1,0:T(8,128)(2,1)} %param.4) | copy-start | bytes 25165828
  8.1 3.4 %copy-start.1 = (bf16[1,1024,4096]{2,1,0:T(8,128)(2,1)S(1)}, bf16[1,1024,4096]{2,1,0:T(8,128)(2,1)}, u32[]{:S(2)}) copy-start(bf16[1,1024,4096]{2,1,0:T(8,128)(2,1)} %param.5) | copy-start | bytes 25165828
  12.7 10.5 %collective-permute-start.2 = (bf16[1024,128]{1,0:T(8,128)(2,1)S(1)}, bf16[1024,128]{1,0:T(8,128)(2,1)S(1)}, u32[]{:S(2)}, u32[]{:S(2)}) collective-permute-start(bf16[1024,128]{1,0:T(8,128)(2,1)S(1)} %collective-permute-done.1.refs_2_), channel_id=1, source_target_pairs={{0,4},{4,0},{8,12},{12,8},{1,5},{5,1},{9,13},{13,9},{2,6},{6,2},{1... | collective-permute-start | bytes 786440 | tf_op jit(solution)/shard_map/ppermute | solution.py:47
  16.4 15.3 %collective-permute-start.7 = (bf16[1024,128]{1,0:T(8,128)(2,1)S(1)}, bf16[1024,128]{1,0:T(8,128)(2,1)S(1)}, u32[]{:S(2)}, u32[]{:S(2)}) collective-permute-start(bf16[1024,128]{1,0:T(8,128)(2,1)S(1)} %get-tuple-element.18.refs_0_), channel_id=1, source_target_pairs={{0,12},{4,8},{8,4},{12,0},{1,13},{5,9},{9,5},{13,1},{2,14},{6,10},... | collective-permute-start | bytes 786440 | tf_op jit(solution)/shard_map/ppermute | solution.py:47
  23.9 7.8 %collective-permute-start.3 = (bf16[1024,128]{1,0:T(8,128)(2,1)S(1)}, bf16[1024,128]{1,0:T(8,128)(2,1)S(1)}, u32[]{:S(2)}, u32[]{:S(2)}) collective-permute-start(bf16[1024,128]{1,0:T(8,128)(2,1)S(1)} %get-tuple-element.17.refs_2_), channel_id=1, source_target_pairs={{0,2},{4,6},{8,10},{12,14},{2,0},{6,4},{10,8},{14,12},{1,3},{5,7},... | collective-permute-start | bytes 786440 | tf_op jit(solution)/shard_map/ppermute | solution.py:52
  24.5 11.3 %collective-permute-start.6 = (bf16[1024,128]{1,0:T(8,128)(2,1)S(1)}, bf16[1024,128]{1,0:T(8,128)(2,1)S(1)}, u32[]{:S(2)}, u32[]{:S(2)}) collective-permute-start(bf16[1024,128]{1,0:T(8,128)(2,1)S(1)} %get-tuple-element.18.refs_0_), channel_id=1, source_target_pairs={{0,4},{4,0},{8,12},{12,8},{1,5},{5,1},{9,13},{13,9},{2,6},{6,2},{1... | collective-permute-start | bytes 786440 | tf_op jit(solution)/shard_map/ppermute | solution.py:47
  31.7 10.1 %collective-permute-start.8 = (bf16[1024,128]{1,0:T(8,128)(2,1)S(1)}, bf16[1024,128]{1,0:T(8,128)(2,1)S(1)}, u32[]{:S(2)}, u32[]{:S(2)}) collective-permute-start(bf16[1024,128]{1,0:T(8,128)(2,1)S(1)} %collective-permute-done.7.refs_2_), channel_id=1, source_target_pairs={{0,4},{4,0},{8,12},{12,8},{1,5},{5,1},{9,13},{13,9},{2,6},{6,2},{1... | collective-permute-start | bytes 786440 | tf_op jit(solution)/shard_map/ppermute | solution.py:47
  31.7 14.9 %collective-permute-start.4 = (bf16[1024,128]{1,0:T(8,128)(2,1)S(1)}, bf16[1024,128]{1,0:T(8,128)(2,1)S(1)}, u32[]{:S(2)}, u32[]{:S(2)}) collective-permute-start(bf16[1024,128]{1,0:T(8,128)(2,1)S(1)} %collective-permute-done.3.refs_1_), channel_id=1, source_target_pairs={{2,14},{6,10},{10,6},{14,2},{3,15},{7,11},{11,7},{15,3},{18,30},{2... | collective-permute-start | bytes 786440 | tf_op jit(solution)/shard_map/ppermute | solution.py:52
  42.5 12.2 %collective-permute-start.9 = (bf16[1024,128]{1,0:T(8,128)(2,1)S(1)}, bf16[1024,128]{1,0:T(8,128)(2,1)S(1)}, u32[]{:S(2)}, u32[]{:S(2)}) collective-permute-start(bf16[1024,128]{1,0:T(8,128)(2,1)S(1)} %get-tuple-element.20.refs_3_), channel_id=1, source_target_pairs={{0,2},{4,6},{8,10},{12,14},{2,0},{6,4},{10,8},{14,12},{1,3},{5,7},... | collective-permute-start | bytes 786440 | tf_op jit(solution)/shard_map/ppermute | solution.py:52
  42.5 14.0 %collective-permute-start.10 = (bf16[1024,128]{1,0:T(8,128)(2,1)S(1)}, bf16[1024,128]{1,0:T(8,128)(2,1)S(1)}, u32[]{:S(2)}, u32[]{:S(2)}) collective-permute-start(bf16[1024,128]{1,0:T(8,128)(2,1)S(1)} %get-tuple-element.20.refs_3_), channel_id=1, source_target_pairs={{0,14},{4,10},{8,6},{12,2},{2,0},{6,4},{10,8},{14,12},{1,15},{5,11... | collective-permute-start | bytes 786440 | tf_op jit(solution)/shard_map/ppermute | solution.py:52
  46.6 11.3 %collective-permute-start.5 = (bf16[1024,128]{1,0:T(8,128)(2,1)S(1)}, bf16[1024,128]{1,0:T(8,128)(2,1)S(1)}, u32[]{:S(2)}, u32[]{:S(2)}) collective-permute-start(bf16[1024,128]{1,0:T(8,128)(2,1)S(1)} %collective-permute-done.4.refs_2_), channel_id=1, source_target_pairs={{2,6},{6,2},{10,14},{14,10},{3,7},{7,3},{11,15},{15,11},{18,22},{2... | collective-permute-start | bytes 786440 | tf_op jit(solution)/shard_map/ppermute | solution.py:52
  49.5 16.3 %collective-permute-start.13 = (bf16[1024,128]{1,0:T(8,128)(2,1)S(1)}, bf16[1024,128]{1,0:T(8,128)(2,1)S(1)}, u32[]{:S(2)}, u32[]{:S(2)}) collective-permute-start(bf16[1024,128]{1,0:T(8,128)(2,1)S(1)} %get-tuple-element.20.refs_3_), channel_id=1, source_target_pairs={{0,10},{4,14},{8,2},{12,6},{2,0},{6,4},{10,8},{14,12},{1,11},{5,15... | collective-permute-start | bytes 786440 | tf_op jit(solution)/shard_map/ppermute | solution.py:52
  49.6 13.5 %collective-permute-start.11 = (bf16[1024,128]{1,0:T(8,128)(2,1)S(1)}, bf16[1024,128]{1,0:T(8,128)(2,1)S(1)}, u32[]{:S(2)}, u32[]{:S(2)}) collective-permute-start(bf16[1024,128]{1,0:T(8,128)(2,1)S(1)} %collective-permute-done.3.refs_1_), channel_id=1, source_target_pairs={{2,6},{6,2},{10,14},{14,10},{3,7},{7,3},{11,15},{15,11},{18,22},{2... | collective-permute-start | bytes 786440 | tf_op jit(solution)/shard_map/ppermute | solution.py:52
  54.7 11.2 %collective-permute-start.12 = (bf16[1024,128]{1,0:T(8,128)(2,1)S(1)}, bf16[1024,128]{1,0:T(8,128)(2,1)S(1)}, u32[]{:S(2)}, u32[]{:S(2)}) collective-permute-start(bf16[1024,128]{1,0:T(8,128)(2,1)S(1)} %collective-permute-done.9.refs_1_), channel_id=1, source_target_pairs={{2,6},{6,2},{10,14},{14,10},{3,7},{7,3},{11,15},{15,11},{18,22},{2... | collective-permute-start | bytes 786440 | tf_op jit(solution)/shard_map/ppermute | solution.py:52

commit v4 on v3

--- a/solution.py
+++ b/solution.py
@@ -119,74 +119,88 @@
     )(matrix, begun, across)
 
 
-def finish_kernel(plan, k, matrix, *refs):
-    left, narrow, blocks, out = refs[0:2], refs[2:4], list(refs[4:-1]), refs[-1]
-    me = lax.axis_index("panel")
-    mine = lax.axis_index("zone") == k
-    depth, cols = blocks[0].shape
-    totals = [None, None]
-    for apart, halves in plan:
-        start = pl.multiple_of((me ^ apart) * depth, depth)
-        here, blocks = [block[...] for block in blocks[: len(halves)]], blocks[len(halves) :]
-        block = here[0] if len(here) == 1 else jnp.concatenate(here, axis=1)
-        part = jnp.dot(
-            matrix[:, pl.ds(start, depth)], block, preferred_element_type=jnp.float32
-        )
-        for i, half in enumerate(halves):
-            mine_part = part[:, i * cols : (i + 1) * cols]
-            totals[half] = mine_part if totals[half] is None else totals[half] + mine_part
-    for half, total in enumerate(totals):
-        rest = (left[half][...] - total).astype(jnp.bfloat16)
-        out[:, half * cols : (half + 1) * cols] = jnp.where(mine, rest, narrow[half][...])
-
-
-def finish(matrix, left, narrow, last, k):
-    rows, cols = narrow[0].shape
-    plan = tuple((apart, tuple(blocks)) for apart, blocks in last)
-    operands = (matrix, *left, *narrow, *(b for _, blocks in last for b in blocks.values()))
-    return pl.pallas_call(
-        functools.partial(finish_kernel, plan, k),
+def settle_kernel(k, matrix, left, left2, narrow, near, near2, first_out, left2_out):
+    cols = near.shape[1]
+    block = jnp.concatenate([near[...], near2[...]], axis=1)
+    depth = block.shape[0]
+    start = pl.multiple_of((lax.axis_index("panel") ^ 1) * depth, depth)
+    part = jnp.dot(matrix[:, pl.ds(start, depth)], block, preferred_element_type=jnp.float32)
+    rest = (left[...] - part[:, :cols]).astype(jnp.bfloat16)
+    first_out[...] = jnp.where(lax.axis_index("zone") == k, rest, narrow[...])
+    left2_out[...] = left2[...] - part[:, cols:]
+
+
+def settle(matrix, left, left2, narrow, near, near2, k):
+    return pl.pallas_call(
+        functools.partial(settle_kernel, k),
+        out_shape=(
+            jax.ShapeDtypeStruct(narrow.shape, jnp.bfloat16),
+            jax.ShapeDtypeStruct(left2.shape, jnp.float32),
+        ),
+        in_specs=[VMEM] * 6,
+        out_specs=(VMEM,) * 2,
+        compiler_params=params(8),
+        name="settle",
+    )(matrix, left, left2, narrow, near, near2)
+
+
+def finish_kernel(apart, k, matrix, first, left2, narrow2, *refs):
+    blocks, out = refs[:-1], refs[-1]
+    cols = first.shape[1]
+    rest = (left2[...] - product(apart, matrix, blocks)).astype(jnp.bfloat16)
+    out[:, :cols] = first[...]
+    out[:, cols:] = jnp.where(lax.axis_index("zone") == k, rest, narrow2[...])
+
+
+def finish(matrix, first, left2, narrow2, blocks, apart, k):
+    rows, cols = first.shape
+    return pl.pallas_call(
+        functools.partial(finish_kernel, apart, k),
         out_shape=jax.ShapeDtypeStruct((rows, 2 * cols), jnp.bfloat16),
-        in_specs=[VMEM] * len(operands),
+        in_specs=[VMEM] * (4 + len(blocks)),
         out_specs=VMEM,
         compiler_params=params(8),
         name="finish",
-    )(*operands)
+    )(matrix, first, left2, narrow2, *blocks)
 
 
 def local_four(source, inverse, coupling):
     zones = lax.axis_size("zone")
     width = source.shape[1] // 2
-    first, second = source[:, :width], source[:, width:]
+    first = source[:, :width]
     inverse, coupling = fetch(inverse, coupling)
 
     far = swap_panels(first, 3)
     near = swap_panels(first, 1)
     passed, _ = together((far, inverse))
     across = swap_panels(passed, 1)
-    second, _ = together((second, far))
+    later, _ = together((source, inverse))
+    second, _ = together((later[:, width:], far))
     far2 = swap_panels(second, 3)
     begun = begin(inverse, [first, near, far], (0, 1, 3))
     wide, narrow = project(inverse, begun, across)
-    near2 = swap_panels(second, 1)
+    late, _ = together((second, across))
+    near2 = swap_panels(late, 1)
     across2 = swap_panels(far2, 1)
-    begun2 = begin(inverse, [second, near2, far2], (0, 1, 3))
+    own = swap_zones(narrow, 1)
+    begun2 = begin(inverse, [second, near2, far2], (0, 1, 3), after=(own,))
     wide2, narrow2 = project(inverse, begun2, across2)
 
     for k in range(1, zones):
-        own = swap_zones(narrow, k)
+        if k > 1:
+            own = swap_zones(narrow, k)
         own2 = swap_zones(narrow2, k)
         far = swap_in_zone(own, 3, k)
         near = swap_in_zone(own, 1, k)
         across = swap_in_zone(far, 1, k)
-        near2 = swap_in_zone(own2, 1, k)
-        far2 = straight(narrow2, 3, k)
+        later, _ = together((narrow2, own2))
+        far2 = swap_in_zone(own2, 3, k)
+        near2 = straight(later, 1, k)
         across2 = straight(narrow2, 2, k)
         left = begin(coupling, [own, far, across], (0, 3, 2,), wide)
-        left2 = begin(coupling, [own2, far2], (0, 3,), wide2)
-        both = finish(
-            coupling, (left, left2), (narrow, narrow2), [(1, {0: near, 1: near2}), (2, {1: across2})], k
-        )
+        left2 = begin(coupling, [own2, across2], (0, 2,), wide2)
+        done, left2 = settle(coupling, left, left2, narrow, near, near2, k)
+        both = finish(coupling, done, left2, narrow2, [far2], (3,), k)
         narrow, narrow2 = both[:, :width], both[:, width:]
     return both
 

time: 68.2 us -> 66.9 us (0.981)
  the two profiles are of different devices: /device:TPU:6 before, /device:TPU:18 now
where the time goes in v4:
time: 66.9 us; the launch traced here: 66.6 us
  waiting for transfers between devices  25.6 us (38%)
  starting transfers between devices  21.8 us (33%)
  Pallas kernels  11.4 us (17%)
  local copies, waits for them, and re-layouts  7.75 us (12%)
    ppermute x6, waiting for transfers between devices, swap_panels(): return lax.ppermute(block, 'panel', [(p, p ^ apart) for p in range(4)])  15.5 us
    ppermute x8, starting transfers between devices, across_zones(): lax.ppermute(block, ('panel', 'zone'), [(a * zones + y, b * zones + z) fo...  13.7 us
    ppermute x8, waiting for transfers between devices, across_zones(): lax.ppermute(block, ('panel', 'zone'), [(a * zones + y, b * zones + z) fo...  10.1 us
    ppermute x6, starting transfers between devices, swap_panels(): return lax.ppermute(block, 'panel', [(p, p ^ apart) for p in range(4)])  8.03 us
    unnamed x6, local copies, waits for them, and re-layouts  6.77 us
    pallas_call x4, Pallas kernels, begin(): pl.pallas_call(functools.partial(begin_kernel, apart, len(held) - 1), out...  6.59 us
    pallas_call x1, Pallas kernels, finish(): pl.pallas_call(functools.partial(finish_kernel, apart, k), out_shape=jax....  1.51 us
    pallas_call x2, Pallas kernels, project(): pl.pallas_call(project_kernel, out_shape=(jax.ShapeDtypeStruct(across.sha...  1.42 us
  transfers between devices with their start and end apart: 14, of which 9 were waited for; matrix products, arithmetic and copies ran while one was open for 0% of the time, Pallas kernels for 15%

profile of v4, /device:TPU:18, one launch (start us, length us, event | category | flops | bytes accessed | tf_op | source)
XLA Modules:
  0.0 66.6 jit_solution(10438972656884830505)
XLA Ops:
  0.0 1.0 %slice.8.refs_0_ = bf16[1024,128]{1,0:T(8,128)(2,1)S(1)} slice(bf16[1024,256]{1,0:T(8,128)(2,1)} %bitcast.6), slice={[0:1024], [0:128]} | slice | bytes 524288 | tf_op jit(solution)/shard_map/slice | solution.py:170
  1.5 1.3 %collective-permute-start = (bf16[1024,128]{1,0:T(8,128)(2,1)S(1)}, bf16[1024,128]{1,0:T(8,128)(2,1)S(1)}, u32[]{:S(2)}, u32[]{:S(2)}) collective-permute-start(bf16[1024,128]{1,0:T(8,128)(2,1)S(1)} %slice.8.refs_0_), channel_id=1, source_target_pairs={{0,4},{4,0},{8,12},{12,8},{1,5},{5,1},{9,13},{13,9},{2,6},{6,2},{1... | collective-permute-start | bytes 786440 | tf_op jit(solution)/shard_map/ppermute | solution.py:47
  2.8 3.4 %copy-done = bf16[1,1024,4096]{2,1,0:T(8,128)(2,1)S(1)} copy-done((bf16[1,1024,4096]{2,1,0:T(8,128)(2,1)S(1)}, bf16[1,1024,4096]{2,1,0:T(8,128)(2,1)}, u32[]{:S(2)}) %copy-start) | copy-done | bytes 8388632
  6.2 3.4 %copy-done.1 = bf16[1,1024,4096]{2,1,0:T(8,128)(2,1)S(1)} copy-done((bf16[1,1024,4096]{2,1,0:T(8,128)(2,1)S(1)}, bf16[1,1024,4096]{2,1,0:T(8,128)(2,1)}, u32[]{:S(2)}) %copy-start.1) | copy-done | bytes 8388632
  9.6 1.1 %fetch.1 = (bf16[1024,4096]{1,0:T(8,128)(2,1)S(1)}, bf16[1024,4096]{1,0:T(8,128)(2,1)S(1)}) custom-call(bf16[1024,4096]{1,0:T(8,128)(2,1)S(1)} %bitcast.4, bf16[1024,4096]{1,0:T(8,128)(2,1)S(1)} %bitcast.5), custom_call_target="tpu_custom_call" | custom-call | tf_op jit(solution)/shard_map/fetch/pallas_call | solution.py:32
  10.7 4.0 %collective-permute-done.1.refs_2_ = bf16[1024,128]{1,0:T(8,128)(2,1)S(1)} collective-permute-done((bf16[1024,128]{1,0:T(8,128)(2,1)S(1)}, bf16[1024,128]{1,0:T(8,128)(2,1)S(1)}, u32[]{:S(2)}, u32[]{:S(2)}) %collective-permute-start.1) | collective-permute-done | bytes 262176 | tf_op jit(solution)/shard_map/ppermute | solution.py:47
  15.2 1.8 %begin.4.begun = f32[1024,128]{1,0:T(8,128)S(1)} custom-call(bf16[1024,4096]{1,0:T(8,128)(2,1)S(1)} %get-tuple-element.19.matrix, bf16[1024,128]{1,0:T(8,128)(2,1)S(1)} %slice.8.refs_0_, bf16[1024,128]{1,0:T(8,128)(2,1)S(1)} %collective-permute-done.refs_1_, bf16[1024,128]{1,0:T(8,128)(2,1)S(1)} %collective-permute-done.1.refs_2_), custom_call_target="tpu_custom_call" | custom-call | tf_op jit(solution)/shard_map/begin/pallas_call | solution.py:92
  17.0 6.9 %collective-permute-done.2.across = bf16[1024,128]{1,0:T(8,128)(2,1)S(1)} collective-permute-done((bf16[1024,128]{1,0:T(8,128)(2,1)S(1)}, bf16[1024,128]{1,0:T(8,128)(2,1)S(1)}, u32[]{:S(2)}, u32[]{:S(2)}) %collective-permute-start.2) | collective-permute-done | bytes 262176 | tf_op jit(solution)/shard_map/ppermute | solution.py:47
  25.3 5.6 %collective-permute-start.8 = (bf16[1024,128]{1,0:T(8,128)(2,1)S(1)}, bf16[1024,128]{1,0:T(8,128)(2,1)S(1)}, u32[]{:S(2)}, u32[]{:S(2)}) collective-permute-start(bf16[1024,128]{1,0:T(8,128)(2,1)S(1)} %collective-permute-done.7.refs_2_), channel_id=1, source_target_pairs={{0,4},{4,0},{8,12},{12,8},{1,5},{5,1},{9,13},{13,9},{2,6},{6,2},{1... | collective-permute-start | bytes 786440 | tf_op jit(solution)/shard_map/ppermute | solution.py:47
  31.1 3.3 %collective-permute-start.4 = (bf16[1024,128]{1,0:T(8,128)(2,1)S(1)}, bf16[1024,128]{1,0:T(8,128)(2,1)S(1)}, u32[]{:S(2)}, u32[]{:S(2)}) collective-permute-start(bf16[1024,128]{1,0:T(8,128)(2,1)S(1)} %collective-permute-done.3.refs_1_.refs_3_), channel_id=1, source_target_pairs={{2,14},{6,10},{10,6},{14,2},{3,15},{7,11},{11,7},{15,3},{18,30},{2... | collective-permute-start | bytes 786440 | tf_op jit(solution)/shard_map/ppermute | solution.py:52
  34.4 0.8 %collective-permute-done.6.refs_1_ = bf16[1024,128]{1,0:T(8,128)(2,1)S(1)} collective-permute-done((bf16[1024,128]{1,0:T(8,128)(2,1)S(1)}, bf16[1024,128]{1,0:T(8,128)(2,1)S(1)}, u32[]{:S(2)}, u32[]{:S(2)}) %collective-permute-start.6) | collective-permute-done | bytes 262176 | tf_op jit(solution)/shard_map/ppermute | solution.py:47
  35.2 1.8 %begin.6.begun = f32[1024,128]{1,0:T(8,128)S(1)} custom-call(bf16[1024,4096]{1,0:T(8,128)(2,1)S(1)} %get-tuple-element.19.matrix, bf16[1024,128]{1,0:T(8,128)(2,1)S(1)} %slice.7.refs_0_, bf16[1024,128]{1,0:T(8,128)(2,1)S(1)} %collective-permute-done.6.refs_1_, bf16[1024,128]{1,0:T(8,128)(2,1)S(1)} %collective-permute-done.7.refs_2_, ...), custom_call_target="tpu_custom_call" | custom-call | tf_op jit(solution)/shard_map/begin/pallas_call | solution.py:92
  37.0 3.8 %collective-permute-done.8.across = bf16[1024,128]{1,0:T(8,128)(2,1)S(1)} collective-permute-done((bf16[1024,128]{1,0:T(8,128)(2,1)S(1)}, bf16[1024,128]{1,0:T(8,128)(2,1)S(1)}, u32[]{:S(2)}, u32[]{:S(2)}) %collective-permute-start.8) | collective-permute-done | bytes 262176 | tf_op jit(solution)/shard_map/ppermute | solution.py:47
  41.6 2.0 %collective-permute-start.10 = (bf16[1024,128]{1,0:T(8,128)(2,1)S(1)}, bf16[1024,128]{1,0:T(8,128)(2,1)S(1)}, u32[]{:S(2)}, u32[]{:S(2)}) collective-permute-start(bf16[1024,128]{1,0:T(8,128)(2,1)S(1)} %get-tuple-element.28.narrow2), channel_id=1, source_target_pairs={{0,10},{4,14},{8,2},{12,6},{2,0},{6,4},{10,8},{14,12},{1,11},{5,15... | collective-permute-start | bytes 786440 | tf_op jit(solution)/shard_map/ppermute | solution.py:52
  43.6 2.1 %collective-permute-start.11 = (bf16[1024,128]{1,0:T(8,128)(2,1)S(1)}, bf16[1024,128]{1,0:T(8,128)(2,1)S(1)}, u32[]{:S(2)}, u32[]{:S(2)}) collective-permute-start(bf16[1024,128]{1,0:T(8,128)(2,1)S(1)} %collective-permute-done.3.refs_1_.refs_3_), channel_id=1, source_target_pairs={{2,6},{6,2},{10,14},{14,10},{3,7},{7,3},{11,15},{15,11},{18,22},{2... | collective-permute-start | bytes 786440 | tf_op jit(solution)/shard_map/ppermute | solution.py:52
  45.7 3.8 %collective-permute-start.5 = (bf16[1024,128]{1,0:T(8,128)(2,1)S(1)}, bf16[1024,128]{1,0:T(8,128)(2,1)S(1)}, u32[]{:S(2)}, u32[]{:S(2)}) collective-permute-start(bf16[1024,128]{1,0:T(8,128)(2,1)S(1)} %collective-permute-done.4.refs_2_), channel_id=1, source_target_pairs={{2,6},{6,2},{10,14},{14,10},{3,7},{7,3},{11,15},{15,11},{18,22},{2... | collective-permute-start | bytes 786440 | tf_op jit(solution)/shard_map/ppermute | solution.py:52
  49.5 4.7 %collective-permute-done.9.refs_1_ = bf16[1024,128]{1,0:T(8,128)(2,1)S(1)} collective-permute-done((bf16[1024,128]{1,0:T(8,128)(2,1)S(1)}, bf16[1024,128]{1,0:T(8,128)(2,1)S(1)}, u32[]{:S(2)}, u32[]{:S(2)}) %collective-permute-start.9) | collective-permute-done | bytes 262176 | tf_op jit(solution)/shard_map/ppermute | solution.py:52
  54.2 1.9 %collective-permute-start.13 = (bf16[1024,128]{1,0:T(8,128)(2,1)S(1)}, bf16[1024,128]{1,0:T(8,128)(2,1)S(1)}, u32[]{:S(2)}, u32[]{:S(2)}) collective-permute-start(bf16[1024,128]{1,0:T(8,128)(2,1)S(1)} %collective-permute-done.9.refs_1_), channel_id=1, source_target_pairs={{2,14},{6,10},{10,6},{14,2},{3,15},{7,11},{11,7},{15,3},{18,30},{2... | collective-permute-start | bytes 786440 | tf_op jit(solution)/shard_map/ppermute | solution.py:52
  56.1 1.2 %begin.7.left2 = f32[1024,128]{1,0:T(8,128)S(1)} custom-call(bf16[1024,4096]{1,0:T(8,128)(2,1)S(1)} %get-tuple-element.18.matrix, f32[1024,128]{1,0:T(8,128)S(1)} %get-tuple-element.26.refs_0_, bf16[1024,128]{1,0:T(8,128)(2,1)S(1)} %collective-permute-done.9.refs_1_, bf16[1024,128]{1,0:T(8,128)(2,1)S(1)} %collective-permute-done.10.refs_2_), custom_call_target="tpu_custom_call" | custom-call | tf_op jit(solution)/shard_map/begin/pallas_call | solution.py:92
  57.4 1.4 %collective-permute-done.5.refs_3_ = bf16[1024,128]{1,0:T(8,128)(2,1)S(1)} collective-permute-done((bf16[1024,128]{1,0:T(8,128)(2,1)S(1)}, bf16[1024,128]{1,0:T(8,128)(2,1)S(1)}, u32[]{:S(2)}, u32[]{:S(2)}) %collective-permute-start.5) | collective-permute-done | bytes 262176 | tf_op jit(solution)/shard_map/ppermute | solution.py:52
  58.8 1.8 %begin.5.left = f32[1024,128]{1,0:T(8,128)S(1)} custom-call(bf16[1024,4096]{1,0:T(8,128)(2,1)S(1)} %get-tuple-element.18.matrix, f32[1024,128]{1,0:T(8,128)S(1)} %get-tuple-element.21.refs_0_, bf16[1024,128]{1,0:T(8,128)(2,1)S(1)} %collective-permute-done.3.refs_1_.refs_3_, bf16[1024,128]{1,0:T(8,128)(2,1)S(1)} %collective-permute-done.4.refs_2_, ...), custom_call_target="tpu_custom_call" | custom-call | tf_op jit(solution)/shard_map/begin/pallas_call | solution.py:92
  60.6 0.9 %collective-permute-done.12.near2 = bf16[1024,128]{1,0:T(8,128)(2,1)S(1)} collective-permute-done((bf16[1024,128]{1,0:T(8,128)(2,1)S(1)}, bf16[1024,128]{1,0:T(8,128)(2,1)S(1)}, u32[]{:S(2)}, u32[]{:S(2)}) %collective-permute-start.12) | collective-permute-done | bytes 262176 | tf_op jit(solution)/shard_map/ppermute | solution.py:52
  62.2 2.9 %collective-permute-done.13.refs_0_ = bf16[1024,128]{1,0:T(8,128)(2,1)S(1)} collective-permute-done((bf16[1024,128]{1,0:T(8,128)(2,1)S(1)}, bf16[1024,128]{1,0:T(8,128)(2,1)S(1)}, u32[]{:S(2)}, u32[]{:S(2)}) %collective-permute-start.13) | collective-permute-done | bytes 262176 | tf_op jit(solution)/shard_map/ppermute | solution.py:52
  65.1 1.5 %finish.1 = bf16[1024,256]{1,0:T(8,128)(2,1)} custom-call(bf16[1024,4096]{1,0:T(8,128)(2,1)S(1)} %get-tuple-element.18.matrix, bf16[1024,128]{1,0:T(8,128)(2,1)S(1)} %get-tuple-element.29.first, f32[1024,128]{1,0:T(8,128)S(1)} %get-tuple-element.30.left2, bf16[1024,128]{1,0:T(8,128)(2,1)S(1)} %get-tuple-element.28.narrow2, ...), custom_call_target="tpu_custom_call" | custom-call | tf_op jit(solution)/shard_map/finish/pallas_call | solution.py:157
  (21 shorter events, 4.1 us)
Async XLA Ops:
  1.0 13.7 %collective-permute-start.1 = (bf16[1024,128]{1,0:T(8,128)(2,1)S(1)}, bf16[1024,128]{1,0:T(8,128)(2,1)S(1)}, u32[]{:S(2)}, u32[]{:S(2)}) collective-permute-start(bf16[1024,128]{1,0:T(8,128)(2,1)S(1)} %slice.8.refs_0_), channel_id=1, source_target_pairs={{0,12},{4,8},{8,4},{12,0},{1,13},{5,9},{9,5},{13,1},{2,14},{6,10},... | collective-permute-start | bytes 786440 | tf_op jit(solution)/shard_map/ppermute | solution.py:47
  1.5 13.8 %collective-permute-start = (bf16[1024,128]{1,0:T(8,128)(2,1)S(1)}, bf16[1024,128]{1,0:T(8,128)(2,1)S(1)}, u32[]{:S(2)}, u32[]{:S(2)}) collective-permute-start(bf16[1024,128]{1,0:T(8,128)(2,1)S(1)} %slice.8.refs_0_), channel_id=1, source_target_pairs={{0,4},{4,0},{8,12},{12,8},{1,5},{5,1},{9,13},{13,9},{2,6},{6,2},{1... | collective-permute-start | bytes 786440 | tf_op jit(solution)/shard_map/ppermute | solution.py:47
  2.8 3.4 %copy-start = (bf16[1,1024,4096]{2,1,0:T(8,128)(2,1)S(1)}, bf16[1,1024,4096]{2,1,0:T(8,128)(2,1)}, u32[]{:S(2)}) copy-start(bf16[1,1024,4096]{2,1,0:T(8,128)(2,1)} %param.4) | copy-start | bytes 25165828
  6.2 3.4 %copy-start.1 = (bf16[1,1024,4096]{2,1,0:T(8,128)(2,1)S(1)}, bf16[1,1024,4096]{2,1,0:T(8,128)(2,1)}, u32[]{:S(2)}) copy-start(bf16[1,1024,4096]{2,1,0:T(8,128)(2,1)} %param.5) | copy-start | bytes 25165828
  9.6 5.1 %copy-start.2 = (bf16[1,1024,256]{2,1,0:T(8,128)(2,1)S(1)}, bf16[1,1024,256]{2,1,0:T(8,128)(2,1)}, u32[]{:S(2)}) copy-start(bf16[1,1024,256]{2,1,0:T(8,128)(2,1)} %param.3) | copy-start | bytes 1572868
  14.7 9.2 %collective-permute-start.2 = (bf16[1024,128]{1,0:T(8,128)(2,1)S(1)}, bf16[1024,128]{1,0:T(8,128)(2,1)S(1)}, u32[]{:S(2)}, u32[]{:S(2)}) collective-permute-start(bf16[1024,128]{1,0:T(8,128)(2,1)S(1)} %collective-permute-done.1.refs_2_), channel_id=1, source_target_pairs={{0,4},{4,0},{8,12},{12,8},{1,5},{5,1},{9,13},{13,9},{2,6},{6,2},{1... | collective-permute-start | bytes 786440 | tf_op jit(solution)/shard_map/ppermute | solution.py:47
  14.7 10.5 %collective-permute-start.7 = (bf16[1024,128]{1,0:T(8,128)(2,1)S(1)}, bf16[1024,128]{1,0:T(8,128)(2,1)S(1)}, u32[]{:S(2)}, u32[]{:S(2)}) collective-permute-start(bf16[1024,128]{1,0:T(8,128)(2,1)S(1)} %slice.7.refs_0_), channel_id=1, source_target_pairs={{0,12},{4,8},{8,4},{12,0},{1,13},{5,9},{9,5},{13,1},{2,14},{6,10},... | collective-permute-start | bytes 786440 | tf_op jit(solution)/shard_map/ppermute | solution.py:47
  24.7 6.4 %collective-permute-start.3 = (bf16[1024,128]{1,0:T(8,128)(2,1)S(1)}, bf16[1024,128]{1,0:T(8,128)(2,1)S(1)}, u32[]{:S(2)}, u32[]{:S(2)}) collective-permute-start(bf16[1024,128]{1,0:T(8,128)(2,1)S(1)} %get-tuple-element.22.narrow), channel_id=1, source_target_pairs={{0,2},{4,6},{8,10},{12,14},{2,0},{6,4},{10,8},{14,12},{1,3},{5,7},... | collective-permute-start | bytes 786440 | tf_op jit(solution)/shard_map/ppermute | solution.py:52
  25.3 9.9 %collective-permute-start.6 = (bf16[1024,128]{1,0:T(8,128)(2,1)S(1)}, bf16[1024,128]{1,0:T(8,128)(2,1)S(1)}, u32[]{:S(2)}, u32[]{:S(2)}) collective-permute-start(bf16[1024,128]{1,0:T(8,128)(2,1)S(1)} %slice.7.refs_0_), channel_id=1, source_target_pairs={{0,4},{4,0},{8,12},{12,8},{1,5},{5,1},{9,13},{13,9},{2,6},{6,2},{1... | collective-permute-start | bytes 786440 | tf_op jit(solution)/shard_map/ppermute | solution.py:47
  25.3 15.5 %collective-permute-start.8 = (bf16[1024,128]{1,0:T(8,128)(2,1)S(1)}, bf16[1024,128]{1,0:T(8,128)(2,1)S(1)}, u32[]{:S(2)}, u32[]{:S(2)}) collective-permute-start(bf16[1024,128]{1,0:T(8,128)(2,1)S(1)} %collective-permute-done.7.refs_2_), channel_id=1, source_target_pairs={{0,4},{4,0},{8,12},{12,8},{1,5},{5,1},{9,13},{13,9},{2,6},{6,2},{1... | collective-permute-start | bytes 786440 | tf_op jit(solution)/shard_map/ppermute | solution.py:47
  31.1 14.6 %collective-permute-start.4 = (bf16[1024,128]{1,0:T(8,128)(2,1)S(1)}, bf16[1024,128]{1,0:T(8,128)(2,1)S(1)}, u32[]{:S(2)}, u32[]{:S(2)}) collective-permute-start(bf16[1024,128]{1,0:T(8,128)(2,1)S(1)} %collective-permute-done.3.refs_1_.refs_3_), channel_id=1, source_target_pairs={{2,14},{6,10},{10,6},{14,2},{3,15},{7,11},{11,7},{15,3},{18,30},{2... | collective-permute-start | bytes 786440 | tf_op jit(solution)/shard_map/ppermute | solution.py:52
  41.5 12.7 %collective-permute-start.9 = (bf16[1024,128]{1,0:T(8,128)(2,1)S(1)}, bf16[1024,128]{1,0:T(8,128)(2,1)S(1)}, u32[]{:S(2)}, u32[]{:S(2)}) collective-permute-start(bf16[1024,128]{1,0:T(8,128)(2,1)S(1)} %get-tuple-element.28.narrow2), channel_id=1, source_target_pairs={{0,2},{4,6},{8,10},{12,14},{2,0},{6,4},{10,8},{14,12},{1,3},{5,7},... | collective-permute-start | bytes 786440 | tf_op jit(solution)/shard_map/ppermute | solution.py:52
  41.6 14.5 %collective-permute-start.10 = (bf16[1024,128]{1,0:T(8,128)(2,1)S(1)}, bf16[1024,128]{1,0:T(8,128)(2,1)S(1)}, u32[]{:S(2)}, u32[]{:S(2)}) collective-permute-start(bf16[1024,128]{1,0:T(8,128)(2,1)S(1)} %get-tuple-element.28.narrow2), channel_id=1, source_target_pairs={{0,10},{4,14},{8,2},{12,6},{2,0},{6,4},{10,8},{14,12},{1,11},{5,15... | collective-permute-start | bytes 786440 | tf_op jit(solution)/shard_map/ppermute | solution.py:52
  43.6 17.0 %collective-permute-start.11 = (bf16[1024,128]{1,0:T(8,128)(2,1)S(1)}, bf16[1024,128]{1,0:T(8,128)(2,1)S(1)}, u32[]{:S(2)}, u32[]{:S(2)}) collective-permute-start(bf16[1024,128]{1,0:T(8,128)(2,1)S(1)} %collective-permute-done.3.refs_1_.refs_3_), channel_id=1, source_target_pairs={{2,6},{6,2},{10,14},{14,10},{3,7},{7,3},{11,15},{15,11},{18,22},{2... | collective-permute-start | bytes 786440 | tf_op jit(solution)/shard_map/ppermute | solution.py:52
  45.7 13.1 %collective-permute-start.5 = (bf16[1024,128]{1,0:T(8,128)(2,1)S(1)}, bf16[1024,128]{1,0:T(8,128)(2,1)S(1)}, u32[]{:S(2)}, u32[]{:S(2)}) collective-permute-start(bf16[1024,128]{1,0:T(8,128)(2,1)S(1)} %collective-permute-done.4.refs_2_), channel_id=1, source_target_pairs={{2,6},{6,2},{10,14},{14,10},{3,7},{7,3},{11,15},{15,11},{18,22},{2... | collective-permute-start | bytes 786440 | tf_op jit(solution)/shard_map/ppermute | solution.py:52
  54.2 7.3 %collective-permute-start.12 = (bf16[1024,128]{1,0:T(8,128)(2,1)S(1)}, bf16[1024,128]{1,0:T(8,128)(2,1)S(1)}, u32[]{:S(2)}, u32[]{:S(2)}) collective-permute-start(bf16[1024,128]{1,0:T(8,128)(2,1)S(1)} %get-tuple-element.28.narrow2), channel_id=1, source_target_pairs={{0,6},{4,2},{8,14},{12,10},{2,0},{6,4},{10,8},{14,12},{1,7},{5,3},... | collective-permute-start | bytes 786440 | tf_op jit(solution)/shard_map/ppermute | solution.py:52
  54.2 10.9 %collective-permute-start.13 = (bf16[1024,128]{1,0:T(8,128)(2,1)S(1)}, bf16[1024,128]{1,0:T(8,128)(2,1)S(1)}, u32[]{:S(2)}, u32[]{:S(2)}) collective-permute-start(bf16[1024,128]{1,0:T(8,128)(2,1)S(1)} %collective-permute-done.9.refs_1_), channel_id=1, source_target_pairs={{2,14},{6,10},{10,6},{14,2},{3,15},{7,11},{11,7},{15,3},{18,30},{2... | collective-permute-start | bytes 786440 | tf_op jit(solution)/shard_map/ppermute | solution.py:52

commit v5 on v4

--- a/solution.py
+++ b/solution.py
@@ -119,37 +119,33 @@
     )(matrix, begun, across)
 
 
-def settle_kernel(k, matrix, left, left2, narrow, near, near2, first_out, left2_out):
-    cols = near.shape[1]
-    block = jnp.concatenate([near[...], near2[...]], axis=1)
-    depth = block.shape[0]
-    start = pl.multiple_of((lax.axis_index("panel") ^ 1) * depth, depth)
-    part = jnp.dot(matrix[:, pl.ds(start, depth)], block, preferred_element_type=jnp.float32)
-    rest = (left[...] - part[:, :cols]).astype(jnp.bfloat16)
-    first_out[...] = jnp.where(lax.axis_index("zone") == k, rest, narrow[...])
-    left2_out[...] = left2[...] - part[:, cols:]
-
-
-def settle(matrix, left, left2, narrow, near, near2, k):
+def settle_kernel(k, matrix, left, narrow, near, out):
+    rest = (left[...] - product((1,), matrix, [near])).astype(jnp.bfloat16)
+    out[...] = jnp.where(lax.axis_index("zone") == k, rest, narrow[...])
+
+
+def settle(matrix, left, narrow, near, k):
     return pl.pallas_call(
         functools.partial(settle_kernel, k),
-        out_shape=(
-            jax.ShapeDtypeStruct(narrow.shape, jnp.bfloat16),
-            jax.ShapeDtypeStruct(left2.shape, jnp.float32),
-        ),
-        in_specs=[VMEM] * 6,
-        out_specs=(VMEM,) * 2,
+        out_shape=jax.ShapeDtypeStruct(narrow.shape, jnp.bfloat16),
+        in_specs=[VMEM] * 4,
+        out_specs=VMEM,
         compiler_params=params(8),
         name="settle",
-    )(matrix, left, left2, narrow, near, near2)
+    )(matrix, left, narrow, near)
 
 
 def finish_kernel(apart, k, matrix, first, left2, narrow2, *refs):
-    blocks, out = refs[:-1], refs[-1]
+    blocks, (out, rest, sems) = refs[:-3], refs[-3:]
     cols = first.shape[1]
-    rest = (left2[...] - product(apart, matrix, blocks)).astype(jnp.bfloat16)
-    out[:, :cols] = first[...]
-    out[:, cols:] = jnp.where(lax.axis_index("zone") == k, rest, narrow2[...])
+    early = pltpu.make_async_copy(first, out.at[:, :cols], sems.at[0])
+    early.start()
+    total = (left2[...] - product(apart, matrix, blocks)).astype(jnp.bfloat16)
+    rest[...] = jnp.where(lax.axis_index("zone") == k, total, narrow2[...])
+    late = pltpu.make_async_copy(rest, out.at[:, cols:], sems.at[1])
+    late.start()
+    early.wait()
+    late.wait()
 
 
 def finish(matrix, first, left2, narrow2, blocks, apart, k):
@@ -158,7 +154,8 @@
         functools.partial(finish_kernel, apart, k),
         out_shape=jax.ShapeDtypeStruct((rows, 2 * cols), jnp.bfloat16),
         in_specs=[VMEM] * (4 + len(blocks)),
-        out_specs=VMEM,
+        out_specs=HBM,
+        scratch_shapes=[pltpu.VMEM((rows, cols), jnp.bfloat16), pltpu.SemaphoreType.DMA((2,))],
         compiler_params=params(8),
         name="finish",
     )(matrix, first, left2, narrow2, *blocks)
@@ -196,10 +193,12 @@
         later, _ = together((narrow2, own2))
         far2 = swap_in_zone(own2, 3, k)
         near2 = straight(later, 1, k)
-        across2 = straight(narrow2, 2, k)
-        left = begin(coupling, [own, far, across], (0, 3, 2,), wide)
-        left2 = begin(coupling, [own2, across2], (0, 2,), wide2)
-        done, left2 = settle(coupling, left, left2, narrow, near, near2, k)
+        across2 = straight(later, 2, k)
+        left = begin(coupling, [own, far, across], (0, 3, 2), wide)
+        done = settle(coupling, left, narrow, near, k)
+        left2 = begin(coupling, [own2], (0,), wide2)
+        left2 = begin(coupling, [near2], (1,), left2)
+        left2 = begin(coupling, [across2], (2,), left2)
         both = finish(coupling, done, left2, narrow2, [far2], (3,), k)
         narrow, narrow2 = both[:, :width], both[:, width:]
     return both

time: 66.9 us -> 65.8 us (0.984)
  the two profiles are of different devices: /device:TPU:18 before, /device:TPU:6 now
where the time goes in v5:
time: 65.8 us; the launch traced here: 65.3 us
  starting transfers between devices  28 us (43%)
  waiting for transfers between devices  17.3 us (26%)
  Pallas kernels  12.2 us (19%)
  local copies, waits for them, and re-layouts  7.75 us (12%)
    ppermute x8, starting transfers between devices, across_zones(): lax.ppermute(block, ('panel', 'zone'), [(a * zones + y, b * zones + z) fo...  15.6 us
    ppermute x6, starting transfers between devices, swap_panels(): return lax.ppermute(block, 'panel', [(p, p ^ apart) for p in range(4)])  12.4 us
    ppermute x6, waiting for transfers between devices, swap_panels(): return lax.ppermute(block, 'panel', [(p, p ^ apart) for p in range(4)])  12.2 us
    pallas_call x6, Pallas kernels, begin(): pl.pallas_call(functools.partial(begin_kernel, apart, len(held) - 1), out...  7.46 us
    unnamed x6, local copies, waits for them, and re-layouts  6.77 us
    ppermute x8, waiting for transfers between devices, across_zones(): lax.ppermute(block, ('panel', 'zone'), [(a * zones + y, b * zones + z) fo...  5.09 us
    pallas_call x1, Pallas kernels, finish(): pl.pallas_call(functools.partial(finish_kernel, apart, k), out_shape=jax....  1.43 us
    pallas_call x2, Pallas kernels, project(): pl.pallas_call(project_kernel, out_shape=(jax.ShapeDtypeStruct(across.sha...  1.42 us
  transfers between devices with their start and end apart: 14, of which 6 were waited for; matrix products, arithmetic and copies ran while one was open for 0% of the time, Pallas kernels for 16%

profile of v5, /device:TPU:6, one launch (start us, length us, event | category | flops | bytes accessed | tf_op | source)
XLA Modules:
  0.0 65.3 jit_solution(12152836906142852679)
XLA Ops:
  0.0 1.0 %slice.8.refs_0_ = bf16[1024,128]{1,0:T(8,128)(2,1)S(1)} slice(bf16[1024,256]{1,0:T(8,128)(2,1)} %bitcast.6), slice={[0:1024], [0:128]} | slice | bytes 524288 | tf_op jit(solution)/shard_map/slice | solution.py:167
  1.0 3.7 %collective-permute-start.1 = (bf16[1024,128]{1,0:T(8,128)(2,1)S(1)}, bf16[1024,128]{1,0:T(8,128)(2,1)S(1)}, u32[]{:S(2)}, u32[]{:S(2)}) collective-permute-start(bf16[1024,128]{1,0:T(8,128)(2,1)S(1)} %slice.8.refs_0_), channel_id=1, source_target_pairs={{0,12},{4,8},{8,4},{12,0},{1,13},{5,9},{9,5},{13,1},{2,14},{6,10},... | collective-permute-start | bytes 786440 | tf_op jit(solution)/shard_map/ppermute | solution.py:47
  4.6 3.4 %copy-done = bf16[1,1024,4096]{2,1,0:T(8,128)(2,1)S(1)} copy-done((bf16[1,1024,4096]{2,1,0:T(8,128)(2,1)S(1)}, bf16[1,1024,4096]{2,1,0:T(8,128)(2,1)}, u32[]{:S(2)}) %copy-start) | copy-done | bytes 8388632
  8.0 3.4 %copy-done.1 = bf16[1,1024,4096]{2,1,0:T(8,128)(2,1)S(1)} copy-done((bf16[1,1024,4096]{2,1,0:T(8,128)(2,1)S(1)}, bf16[1,1024,4096]{2,1,0:T(8,128)(2,1)}, u32[]{:S(2)}) %copy-start.1) | copy-done | bytes 8388632
  11.4 1.1 %fetch.1 = (bf16[1024,4096]{1,0:T(8,128)(2,1)S(1)}, bf16[1024,4096]{1,0:T(8,128)(2,1)S(1)}) custom-call(bf16[1024,4096]{1,0:T(8,128)(2,1)S(1)} %bitcast.4, bf16[1024,4096]{1,0:T(8,128)(2,1)S(1)} %bitcast.5), custom_call_target="tpu_custom_call" | custom-call | tf_op jit(solution)/shard_map/fetch/pallas_call | solution.py:32
  12.6 3.7 %collective-permute-start.2 = (bf16[1024,128]{1,0:T(8,128)(2,1)S(1)}, bf16[1024,128]{1,0:T(8,128)(2,1)S(1)}, u32[]{:S(2)}, u32[]{:S(2)}) collective-permute-start(bf16[1024,128]{1,0:T(8,128)(2,1)S(1)} %collective-permute-done.1.refs_2_), channel_id=1, source_target_pairs={{0,4},{4,0},{8,12},{12,8},{1,5},{5,1},{9,13},{13,9},{2,6},{6,2},{1... | collective-permute-start | bytes 786440 | tf_op jit(solution)/shard_map/ppermute | solution.py:47
  16.3 2.5 %collective-permute-start.8 = (bf16[1024,128]{1,0:T(8,128)(2,1)S(1)}, bf16[1024,128]{1,0:T(8,128)(2,1)S(1)}, u32[]{:S(2)}, u32[]{:S(2)}) collective-permute-start(bf16[1024,128]{1,0:T(8,128)(2,1)S(1)} %slice.7.refs_0_), channel_id=1, source_target_pairs={{0,12},{4,8},{8,4},{12,0},{1,13},{5,9},{9,5},{13,1},{2,14},{6,10},... | collective-permute-start | bytes 786440 | tf_op jit(solution)/shard_map/ppermute | solution.py:47
  18.8 1.8 %begin.6.begun = f32[1024,128]{1,0:T(8,128)S(1)} custom-call(bf16[1024,4096]{1,0:T(8,128)(2,1)S(1)} %get-tuple-element.17.matrix, bf16[1024,128]{1,0:T(8,128)(2,1)S(1)} %slice.8.refs_0_, bf16[1024,128]{1,0:T(8,128)(2,1)S(1)} %collective-permute-done.refs_1_, bf16[1024,128]{1,0:T(8,128)(2,1)S(1)} %collective-permute-done.1.refs_2_), custom_call_target="tpu_custom_call" | custom-call | tf_op jit(solution)/shard_map/begin/pallas_call | solution.py:92
  20.6 2.4 %collective-permute-done.2.across = bf16[1024,128]{1,0:T(8,128)(2,1)S(1)} collective-permute-done((bf16[1024,128]{1,0:T(8,128)(2,1)S(1)}, bf16[1024,128]{1,0:T(8,128)(2,1)S(1)}, u32[]{:S(2)}, u32[]{:S(2)}) %collective-permute-start.2) | collective-permute-done | bytes 262176 | tf_op jit(solution)/shard_map/ppermute | solution.py:47
  24.4 2.5 %collective-permute-start.7 = (bf16[1024,128]{1,0:T(8,128)(2,1)S(1)}, bf16[1024,128]{1,0:T(8,128)(2,1)S(1)}, u32[]{:S(2)}, u32[]{:S(2)}) collective-permute-start(bf16[1024,128]{1,0:T(8,128)(2,1)S(1)} %slice.7.refs_0_), channel_id=1, source_target_pairs={{0,4},{4,0},{8,12},{12,8},{1,5},{5,1},{9,13},{13,9},{2,6},{6,2},{1... | collective-permute-start | bytes 786440 | tf_op jit(solution)/shard_map/ppermute | solution.py:47
  26.8 4.7 %collective-permute-done.8.refs_2_ = bf16[1024,128]{1,0:T(8,128)(2,1)S(1)} collective-permute-done((bf16[1024,128]{1,0:T(8,128)(2,1)S(1)}, bf16[1024,128]{1,0:T(8,128)(2,1)S(1)}, u32[]{:S(2)}, u32[]{:S(2)}) %collective-permute-start.8) | collective-permute-done | bytes 262176 | tf_op jit(solution)/shard_map/ppermute | solution.py:47
  31.6 3.3 %collective-permute-start.4 = (bf16[1024,128]{1,0:T(8,128)(2,1)S(1)}, bf16[1024,128]{1,0:T(8,128)(2,1)S(1)}, u32[]{:S(2)}, u32[]{:S(2)}) collective-permute-start(bf16[1024,128]{1,0:T(8,128)(2,1)S(1)} %collective-permute-done.3.refs_1_.refs_3_), channel_id=1, source_target_pairs={{2,14},{6,10},{10,6},{14,2},{3,15},{7,11},{11,7},{15,3},{18,30},{2... | collective-permute-start | bytes 786440 | tf_op jit(solution)/shard_map/ppermute | solution.py:52
  34.9 0.8 %collective-permute-done.7.refs_1_ = bf16[1024,128]{1,0:T(8,128)(2,1)S(1)} collective-permute-done((bf16[1024,128]{1,0:T(8,128)(2,1)S(1)}, bf16[1024,128]{1,0:T(8,128)(2,1)S(1)}, u32[]{:S(2)}, u32[]{:S(2)}) %collective-permute-start.7) | collective-permute-done | bytes 262176 | tf_op jit(solution)/shard_map/ppermute | solution.py:47
  35.7 1.8 %begin.8.begun = f32[1024,128]{1,0:T(8,128)S(1)} custom-call(bf16[1024,4096]{1,0:T(8,128)(2,1)S(1)} %get-tuple-element.17.matrix, bf16[1024,128]{1,0:T(8,128)(2,1)S(1)} %slice.7.refs_0_, bf16[1024,128]{1,0:T(8,128)(2,1)S(1)} %collective-permute-done.7.refs_1_, bf16[1024,128]{1,0:T(8,128)(2,1)S(1)} %collective-permute-done.8.refs_2_, ...), custom_call_target="tpu_custom_call" | custom-call | tf_op jit(solution)/shard_map/begin/pallas_call | solution.py:92
  37.4 4.2 %collective-permute-done.9.across = bf16[1024,128]{1,0:T(8,128)(2,1)S(1)} collective-permute-done((bf16[1024,128]{1,0:T(8,128)(2,1)S(1)}, bf16[1024,128]{1,0:T(8,128)(2,1)S(1)}, u32[]{:S(2)}, u32[]{:S(2)}) %collective-permute-start.9) | collective-permute-done | bytes 262176 | tf_op jit(solution)/shard_map/ppermute | solution.py:47
  42.4 2.6 %collective-permute-start.6 = (bf16[1024,128]{1,0:T(8,128)(2,1)S(1)}, bf16[1024,128]{1,0:T(8,128)(2,1)S(1)}, u32[]{:S(2)}, u32[]{:S(2)}) collective-permute-start(bf16[1024,128]{1,0:T(8,128)(2,1)S(1)} %collective-permute-done.3.refs_1_.refs_3_), channel_id=1, source_target_pairs={{2,6},{6,2},{10,14},{14,10},{3,7},{7,3},{11,15},{15,11},{18,22},{2... | collective-permute-start | bytes 786440 | tf_op jit(solution)/shard_map/ppermute | solution.py:52
  45.1 2.5 %collective-permute-done.4.refs_2_ = bf16[1024,128]{1,0:T(8,128)(2,1)S(1)} collective-permute-done((bf16[1024,128]{1,0:T(8,128)(2,1)S(1)}, bf16[1024,128]{1,0:T(8,128)(2,1)S(1)}, u32[]{:S(2)}, u32[]{:S(2)}) %collective-permute-start.4) | collective-permute-done | bytes 262176 | tf_op jit(solution)/shard_map/ppermute | solution.py:52
  47.5 1.9 %collective-permute-start.5 = (bf16[1024,128]{1,0:T(8,128)(2,1)S(1)}, bf16[1024,128]{1,0:T(8,128)(2,1)S(1)}, u32[]{:S(2)}, u32[]{:S(2)}) collective-permute-start(bf16[1024,128]{1,0:T(8,128)(2,1)S(1)} %collective-permute-done.4.refs_2_), channel_id=1, source_target_pairs={{2,6},{6,2},{10,14},{14,10},{3,7},{7,3},{11,15},{15,11},{18,22},{2... | collective-permute-start | bytes 786440 | tf_op jit(solution)/shard_map/ppermute | solution.py:52
  49.5 3.5 %collective-permute-start.12 = (bf16[1024,128]{1,0:T(8,128)(2,1)S(1)}, bf16[1024,128]{1,0:T(8,128)(2,1)S(1)}, u32[]{:S(2)}, u32[]{:S(2)}) collective-permute-start(bf16[1024,128]{1,0:T(8,128)(2,1)S(1)} %get-tuple-element.26.narrow2), channel_id=1, source_target_pairs={{0,10},{4,14},{8,2},{12,6},{2,0},{6,4},{10,8},{14,12},{1,11},{5,15... | collective-permute-start | bytes 786440 | tf_op jit(solution)/shard_map/ppermute | solution.py:52
  53.0 3.6 %collective-permute-start.13 = (bf16[1024,128]{1,0:T(8,128)(2,1)S(1)}, bf16[1024,128]{1,0:T(8,128)(2,1)S(1)}, u32[]{:S(2)}, u32[]{:S(2)}) collective-permute-start(bf16[1024,128]{1,0:T(8,128)(2,1)S(1)} %collective-permute-done.10.refs_1_), channel_id=1, source_target_pairs={{2,14},{6,10},{10,6},{14,2},{3,15},{7,11},{11,7},{15,3},{18,30},{2... | collective-permute-start | bytes 786440 | tf_op jit(solution)/shard_map/ppermute | solution.py:52
  57.3 2.6 %collective-permute-done.5.refs_3_ = bf16[1024,128]{1,0:T(8,128)(2,1)S(1)} collective-permute-done((bf16[1024,128]{1,0:T(8,128)(2,1)S(1)}, bf16[1024,128]{1,0:T(8,128)(2,1)S(1)}, u32[]{:S(2)}, u32[]{:S(2)}) %collective-permute-start.5) | collective-permute-done | bytes 262176 | tf_op jit(solution)/shard_map/ppermute | solution.py:52
  59.9 1.8 %begin.7.left = f32[1024,128]{1,0:T(8,128)S(1)} custom-call(bf16[1024,4096]{1,0:T(8,128)(2,1)S(1)} %get-tuple-element.16.matrix, f32[1024,128]{1,0:T(8,128)S(1)} %get-tuple-element.19.refs_0_, bf16[1024,128]{1,0:T(8,128)(2,1)S(1)} %collective-permute-done.3.refs_1_.refs_3_, bf16[1024,128]{1,0:T(8,128)(2,1)S(1)} %collective-permute-done.4.refs_2_, ...), custom_call_target="tpu_custom_call" | custom-call | tf_op jit(solution)/shard_map/begin/pallas_call | solution.py:92
  61.7 0.7 %settle.1.first = bf16[1024,128]{1,0:T(8,128)(2,1)S(1)} custom-call(bf16[1024,4096]{1,0:T(8,128)(2,1)S(1)} %get-tuple-element.16.matrix, f32[1024,128]{1,0:T(8,128)S(1)} %begin.7.left, bf16[1024,128]{1,0:T(8,128)(2,1)S(1)} %get-tuple-element.20.narrow, bf16[1024,128]{1,0:T(8,128)(2,1)S(1)} %collective-permute-done.6.near), custom_call_target="tpu_custom_call" | custom-call | tf_op jit(solution)/shard_map/settle/pallas_call | solution.py:128
  63.9 1.4 %finish.1 = bf16[1024,256]{1,0:T(8,128)(2,1)} custom-call(bf16[1024,4096]{1,0:T(8,128)(2,1)S(1)} %get-tuple-element.16.matrix, bf16[1024,128]{1,0:T(8,128)(2,1)S(1)} %settle.1.first, f32[1024,128]{1,0:T(8,128)S(1)} %begin.11.left2, bf16[1024,128]{1,0:T(8,128)(2,1)S(1)} %get-tuple-element.26.narrow2, bf16[1024,128]{1,0:T(8,128)(2,1)S(1)} %collective-permute-done.13.refs_0_), custom_call_target="tpu_custom_call" | custom-call | tf_op jit(solution)/shard_map/finish/pallas_call | solution.py:153
  (23 shorter events, 4.3 us)
Async XLA Ops:
  1.0 11.6 %collective-permute-start.1 = (bf16[1024,128]{1,0:T(8,128)(2,1)S(1)}, bf16[1024,128]{1,0:T(8,128)(2,1)S(1)}, u32[]{:S(2)}, u32[]{:S(2)}) collective-permute-start(bf16[1024,128]{1,0:T(8,128)(2,1)S(1)} %slice.8.refs_0_), channel_id=1, source_target_pairs={{0,12},{4,8},{8,4},{12,0},{1,13},{5,9},{9,5},{13,1},{2,14},{6,10},... | collective-permute-start | bytes 786440 | tf_op jit(solution)/shard_map/ppermute | solution.py:47
  4.6 14.2 %collective-permute-start = (bf16[1024,128]{1,0:T(8,128)(2,1)S(1)}, bf16[1024,128]{1,0:T(8,128)(2,1)S(1)}, u32[]{:S(2)}, u32[]{:S(2)}) collective-permute-start(bf16[1024,128]{1,0:T(8,128)(2,1)S(1)} %slice.8.refs_0_), channel_id=1, source_target_pairs={{0,4},{4,0},{8,12},{12,8},{1,5},{5,1},{9,13},{13,9},{2,6},{6,2},{1... | collective-permute-start | bytes 786440 | tf_op jit(solution)/shard_map/ppermute | solution.py:47
  4.6 3.4 %copy-start = (bf16[1,1024,4096]{2,1,0:T(8,128)(2,1)S(1)}, bf16[1,1024,4096]{2,1,0:T(8,128)(2,1)}, u32[]{:S(2)}) copy-start(bf16[1,1024,4096]{2,1,0:T(8,128)(2,1)} %param.4) | copy-start | bytes 25165828
  8.0 3.4 %copy-start.1 = (bf16[1,1024,4096]{2,1,0:T(8,128)(2,1)S(1)}, bf16[1,1024,4096]{2,1,0:T(8,128)(2,1)}, u32[]{:S(2)}) copy-start(bf16[1,1024,4096]{2,1,0:T(8,128)(2,1)} %param.5) | copy-start | bytes 25165828
  11.4 4.9 %copy-start.2 = (bf16[1,1024,256]{2,1,0:T(8,128)(2,1)S(1)}, bf16[1,1024,256]{2,1,0:T(8,128)(2,1)}, u32[]{:S(2)}) copy-start(bf16[1,1024,256]{2,1,0:T(8,128)(2,1)} %param.3) | copy-start | bytes 1572868
  12.6 10.5 %collective-permute-start.2 = (bf16[1024,128]{1,0:T(8,128)(2,1)S(1)}, bf16[1024,128]{1,0:T(8,128)(2,1)S(1)}, u32[]{:S(2)}, u32[]{:S(2)}) collective-permute-start(bf16[1024,128]{1,0:T(8,128)(2,1)S(1)} %collective-permute-done.1.refs_2_), channel_id=1, source_target_pairs={{0,4},{4,0},{8,12},{12,8},{1,5},{5,1},{9,13},{13,9},{2,6},{6,2},{1... | collective-permute-start | bytes 786440 | tf_op jit(solution)/shard_map/ppermute | solution.py:47
  16.3 15.3 %collective-permute-start.8 = (bf16[1024,128]{1,0:T(8,128)(2,1)S(1)}, bf16[1024,128]{1,0:T(8,128)(2,1)S(1)}, u32[]{:S(2)}, u32[]{:S(2)}) collective-permute-start(bf16[1024,128]{1,0:T(8,128)(2,1)S(1)} %slice.7.refs_0_), channel_id=1, source_target_pairs={{0,12},{4,8},{8,4},{12,0},{1,13},{5,9},{9,5},{13,1},{2,14},{6,10},... | collective-permute-start | bytes 786440 | tf_op jit(solution)/shard_map/ppermute | solution.py:47
  23.8 7.8 %collective-permute-start.3 = (bf16[1024,128]{1,0:T(8,128)(2,1)S(1)}, bf16[1024,128]{1,0:T(8,128)(2,1)S(1)}, u32[]{:S(2)}, u32[]{:S(2)}) collective-permute-start(bf16[1024,128]{1,0:T(8,128)(2,1)S(1)} %get-tuple-element.20.narrow), channel_id=1, source_target_pairs={{0,2},{4,6},{8,10},{12,14},{2,0},{6,4},{10,8},{14,12},{1,3},{5,7},... | collective-permute-start | bytes 786440 | tf_op jit(solution)/shard_map/ppermute | solution.py:52
  24.4 11.3 %collective-permute-start.7 = (bf16[1024,128]{1,0:T(8,128)(2,1)S(1)}, bf16[1024,128]{1,0:T(8,128)(2,1)S(1)}, u32[]{:S(2)}, u32[]{:S(2)}) collective-permute-start(bf16[1024,128]{1,0:T(8,128)(2,1)S(1)} %slice.7.refs_0_), channel_id=1, source_target_pairs={{0,4},{4,0},{8,12},{12,8},{1,5},{5,1},{9,13},{13,9},{2,6},{6,2},{1... | collective-permute-start | bytes 786440 | tf_op jit(solution)/shard_map/ppermute | solution.py:47
  31.6 10.1 %collective-permute-start.9 = (bf16[1024,128]{1,0:T(8,128)(2,1)S(1)}, bf16[1024,128]{1,0:T(8,128)(2,1)S(1)}, u32[]{:S(2)}, u32[]{:S(2)}) collective-permute-start(bf16[1024,128]{1,0:T(8,128)(2,1)S(1)} %collective-permute-done.8.refs_2_), channel_id=1, source_target_pairs={{0,4},{4,0},{8,12},{12,8},{1,5},{5,1},{9,13},{13,9},{2,6},{6,2},{1... | collective-permute-start | bytes 786440 | tf_op jit(solution)/shard_map/ppermute | solution.py:47
  31.6 16.0 %collective-permute-start.4 = (bf16[1024,128]{1,0:T(8,128)(2,1)S(1)}, bf16[1024,128]{1,0:T(8,128)(2,1)S(1)}, u32[]{:S(2)}, u32[]{:S(2)}) collective-permute-start(bf16[1024,128]{1,0:T(8,128)(2,1)S(1)} %collective-permute-done.3.refs_1_.refs_3_), channel_id=1, source_target_pairs={{2,14},{6,10},{10,6},{14,2},{3,15},{7,11},{11,7},{15,3},{18,30},{2... | collective-permute-start | bytes 786440 | tf_op jit(solution)/shard_map/ppermute | solution.py:52
  42.4 7.1 %collective-permute-start.10 = (bf16[1024,128]{1,0:T(8,128)(2,1)S(1)}, bf16[1024,128]{1,0:T(8,128)(2,1)S(1)}, u32[]{:S(2)}, u32[]{:S(2)}) collective-permute-start(bf16[1024,128]{1,0:T(8,128)(2,1)S(1)} %get-tuple-element.26.narrow2), channel_id=1, source_target_pairs={{0,2},{4,6},{8,10},{12,14},{2,0},{6,4},{10,8},{14,12},{1,3},{5,7},... | collective-permute-start | bytes 786440 | tf_op jit(solution)/shard_map/ppermute | solution.py:52
  42.4 19.3 %collective-permute-start.6 = (bf16[1024,128]{1,0:T(8,128)(2,1)S(1)}, bf16[1024,128]{1,0:T(8,128)(2,1)S(1)}, u32[]{:S(2)}, u32[]{:S(2)}) collective-permute-start(bf16[1024,128]{1,0:T(8,128)(2,1)S(1)} %collective-permute-done.3.refs_1_.refs_3_), channel_id=1, source_target_pairs={{2,6},{6,2},{10,14},{14,10},{3,7},{7,3},{11,15},{15,11},{18,22},{2... | collective-permute-start | bytes 786440 | tf_op jit(solution)/shard_map/ppermute | solution.py:52
  47.5 12.4 %collective-permute-start.5 = (bf16[1024,128]{1,0:T(8,128)(2,1)S(1)}, bf16[1024,128]{1,0:T(8,128)(2,1)S(1)}, u32[]{:S(2)}, u32[]{:S(2)}) collective-permute-start(bf16[1024,128]{1,0:T(8,128)(2,1)S(1)} %collective-permute-done.4.refs_2_), channel_id=1, source_target_pairs={{2,6},{6,2},{10,14},{14,10},{3,7},{7,3},{11,15},{15,11},{18,22},{2... | collective-permute-start | bytes 786440 | tf_op jit(solution)/shard_map/ppermute | solution.py:52
  49.5 13.0 %collective-permute-start.11 = (bf16[1024,128]{1,0:T(8,128)(2,1)S(1)}, bf16[1024,128]{1,0:T(8,128)(2,1)S(1)}, u32[]{:S(2)}, u32[]{:S(2)}) collective-permute-start(bf16[1024,128]{1,0:T(8,128)(2,1)S(1)} %get-tuple-element.26.narrow2), channel_id=1, source_target_pairs={{0,6},{4,2},{8,14},{12,10},{2,0},{6,4},{10,8},{14,12},{1,7},{5,3},... | collective-permute-start | bytes 786440 | tf_op jit(solution)/shard_map/ppermute | solution.py:52
  49.5 13.6 %collective-permute-start.12 = (bf16[1024,128]{1,0:T(8,128)(2,1)S(1)}, bf16[1024,128]{1,0:T(8,128)(2,1)S(1)}, u32[]{:S(2)}, u32[]{:S(2)}) collective-permute-start(bf16[1024,128]{1,0:T(8,128)(2,1)S(1)} %get-tuple-element.26.narrow2), channel_id=1, source_target_pairs={{0,10},{4,14},{8,2},{12,6},{2,0},{6,4},{10,8},{14,12},{1,11},{5,15... | collective-permute-start | bytes 786440 | tf_op jit(solution)/shard_map/ppermute | solution.py:52
  53.0 10.9 %collective-permute-start.13 = (bf16[1024,128]{1,0:T(8,128)(2,1)S(1)}, bf16[1024,128]{1,0:T(8,128)(2,1)S(1)}, u32[]{:S(2)}, u32[]{:S(2)}) collective-permute-start(bf16[1024,128]{1,0:T(8,128)(2,1)S(1)} %collective-permute-done.10.refs_1_), channel_id=1, source_target_pairs={{2,14},{6,10},{10,6},{14,2},{3,15},{7,11},{11,7},{15,3},{18,30},{2... | collective-permute-start | bytes 786440 | tf_op jit(solution)/shard_map/ppermute | solution.py:52

commit v6 on v5

--- a/solution.py
+++ b/solution.py
@@ -16,28 +16,22 @@
     return pltpu.CompilerParams(vmem_limit_bytes=mib * MIB)
 
 
-def fetch_kernel(first, second, first_out, second_out, sems):
-    copies = [
-        pltpu.make_async_copy(first, first_out, sems.at[0]),
-        pltpu.make_async_copy(second, second_out, sems.at[1]),
-    ]
-    for copy in copies:
-        copy.start()
-    for copy in copies:
-        copy.wait()
-
-
-def fetch(inverse, coupling):
-    shape = jax.ShapeDtypeStruct(inverse.shape, inverse.dtype)
+def fetch_kernel(matrix, out, sem):
+    copy = pltpu.make_async_copy(matrix, out, sem)
+    copy.start()
+    copy.wait()
+
+
+def fetch(matrix):
     return pl.pallas_call(
         fetch_kernel,
-        out_shape=(shape, shape),
-        in_specs=[HBM, HBM],
-        out_specs=(VMEM, VMEM),
-        scratch_shapes=[pltpu.SemaphoreType.DMA((2,))],
-        compiler_params=params(18),
+        out_shape=jax.ShapeDtypeStruct(matrix.shape, matrix.dtype),
+        in_specs=[HBM],
+        out_specs=VMEM,
+        scratch_shapes=[pltpu.SemaphoreType.DMA],
+        compiler_params=params(10),
         name="fetch",
-    )(inverse, coupling)
+    )(matrix)
 
 
 together = lax.optimization_barrier
@@ -140,12 +134,17 @@
     cols = first.shape[1]
     early = pltpu.make_async_copy(first, out.at[:, :cols], sems.at[0])
     early.start()
-    total = (left2[...] - product(apart, matrix, blocks)).astype(jnp.bfloat16)
-    rest[...] = jnp.where(lax.axis_index("zone") == k, total, narrow2[...])
-    late = pltpu.make_async_copy(rest, out.at[:, cols:], sems.at[1])
-    late.start()
-    early.wait()
-    late.wait()
+    copies = [early]
+    tall = first.shape[0] // 2
+    for part in range(2):
+        rows = slice(part * tall, (part + 1) * tall)
+        total = (left2[rows] - product(apart, matrix.at[rows], blocks)).astype(jnp.bfloat16)
+        rest[rows] = jnp.where(lax.axis_index("zone") == k, total, narrow2[rows])
+        late = pltpu.make_async_copy(rest.at[rows], out.at[rows, cols:], sems.at[1 + part])
+        late.start()
+        copies.append(late)
+    for copy in copies:
+        copy.wait()
 
 
 def finish(matrix, first, left2, narrow2, blocks, apart, k):
@@ -155,7 +154,7 @@
         out_shape=jax.ShapeDtypeStruct((rows, 2 * cols), jnp.bfloat16),
         in_specs=[VMEM] * (4 + len(blocks)),
         out_specs=HBM,
-        scratch_shapes=[pltpu.VMEM((rows, cols), jnp.bfloat16), pltpu.SemaphoreType.DMA((2,))],
+        scratch_shapes=[pltpu.VMEM((rows, cols), jnp.bfloat16), pltpu.SemaphoreType.DMA((3,))],
         compiler_params=params(8),
         name="finish",
     )(matrix, first, left2, narrow2, *blocks)
@@ -165,7 +164,7 @@
     zones = lax.axis_size("zone")
     width = source.shape[1] // 2
     first = source[:, :width]
-    inverse, coupling = fetch(inverse, coupling)
+    inverse, coupling = fetch(inverse), fetch(coupling)
 
     far = swap_panels(first, 3)
     near = swap_panels(first, 1)
@@ -174,7 +173,7 @@
     later, _ = together((source, inverse))
     second, _ = together((later[:, width:], far))
     far2 = swap_panels(second, 3)
-    begun = begin(inverse, [first, near, far], (0, 1, 3))
+    begun = begin(inverse, [first, near, far], (0, 1, 3), after=(coupling,))
     wide, narrow = project(inverse, begun, across)
     late, _ = together((second, across))
     near2 = swap_panels(late, 1)
@@ -194,7 +193,8 @@
         far2 = swap_in_zone(own2, 3, k)
         near2 = straight(later, 1, k)
         across2 = straight(later, 2, k)
-        left = begin(coupling, [own, far, across], (0, 3, 2), wide)
+        left = begin(coupling, [own, far], (0, 3), wide)
+        left = begin(coupling, [across], (2,), left)
         done = settle(coupling, left, narrow, near, k)
         left2 = begin(coupling, [own2], (0,), wide2)
         left2 = begin(coupling, [near2], (1,), left2)

time: 65.8 us -> 65.8 us (level)
  local copies, waits for them, and re-layouts: 7.75 us -> 4.37 us
  waiting for transfers between devices: 17.3 us -> 19.4 us
    unnamed x6, local copies, waits for them, and re-layouts: 6.77 us -> 3.39 us
    ppermute x6, waiting for transfers between devices: 12.2 us -> 15 us  [swap_panels(): return lax.ppermute(block, 'panel', [(p, p ^ apart) for p in range(4)])]
    ppermute x8, waiting for transfers between devices: 5.09 us -> 4.4 us  [across_zones(): lax.ppermute(block, ('panel', 'zone'), [(a * zones + y, b * zones + z) fo...]
    pallas_call x6 -> x7, Pallas kernels: 7.46 us -> 7.63 us  [begin(): pl.pallas_call(functools.partial(begin_kernel, apart, len(held) - 1), out...]
  transfers between devices with their start and end apart: 14 -> 14, of which waited for: 6 -> 8; matrix products, arithmetic and copies ran while one was open for 0% -> 0% of each run, Pallas kernels for 16% -> 17%
where the time goes in v6:
time: 65.8 us; the launch traced here: 64.8 us
  starting transfers between devices  28.5 us (43%)
  waiting for transfers between devices  19.4 us (29%)
  Pallas kernels  12.3 us (19%)
  local copies, waits for them, and re-layouts  4.37 us (7%)
    ppermute x8, starting transfers between devices, across_zones(): lax.ppermute(block, ('panel', 'zone'), [(a * zones + y, b * zones + z) fo...  15.6 us
    ppermute x6, waiting for transfers between devices, swap_panels(): return lax.ppermute(block, 'panel', [(p, p ^ apart) for p in range(4)])  15 us
    ppermute x6, starting transfers between devices, swap_panels(): return lax.ppermute(block, 'panel', [(p, p ^ apart) for p in range(4)])  12.9 us
    pallas_call x7, Pallas kernels, begin(): pl.pallas_call(functools.partial(begin_kernel, apart, len(held) - 1), out...  7.63 us
    ppermute x8, waiting for transfers between devices, across_zones(): lax.ppermute(block, ('panel', 'zone'), [(a * zones + y, b * zones + z) fo...  4.4 us
    unnamed x6, local copies, waits for them, and re-layouts  3.39 us
    pallas_call x1, Pallas kernels, finish(): pl.pallas_call(functools.partial(finish_kernel, apart, k), out_shape=jax....  1.43 us
    pallas_call x2, Pallas kernels, project(): pl.pallas_call(project_kernel, out_shape=(jax.ShapeDtypeStruct(across.sha...  1.42 us
  transfers between devices with their start and end apart: 14, of which 8 were waited for; matrix products, arithmetic and copies ran while one was open for 0% of the time, Pallas kernels for 17%

profile of v6, /device:TPU:6, one launch (start us, length us, event | category | flops | bytes accessed | tf_op | source)
XLA Modules:
  0.0 64.8 jit_solution(2533330740664591272)
XLA Ops:
  0.0 1.0 %slice.8.refs_0_ = bf16[1024,128]{1,0:T(8,128)(2,1)S(1)} slice(bf16[1024,256]{1,0:T(8,128)(2,1)} %bitcast.6), slice={[0:1024], [0:128]} | slice | bytes 524288 | tf_op jit(solution)/shard_map/slice | solution.py:166
  1.0 3.7 %collective-permute-start.1 = (bf16[1024,128]{1,0:T(8,128)(2,1)S(1)}, bf16[1024,128]{1,0:T(8,128)(2,1)S(1)}, u32[]{:S(2)}, u32[]{:S(2)}) collective-permute-start(bf16[1024,128]{1,0:T(8,128)(2,1)S(1)} %slice.8.refs_0_), channel_id=1, source_target_pairs={{0,12},{4,8},{8,4},{12,0},{1,13},{5,9},{9,5},{13,1},{2,14},{6,10},... | collective-permute-start | bytes 786440 | tf_op jit(solution)/shard_map/ppermute | solution.py:41
  4.6 3.4 %copy-done = bf16[1,1024,4096]{2,1,0:T(8,128)(2,1)S(1)} copy-done((bf16[1,1024,4096]{2,1,0:T(8,128)(2,1)S(1)}, bf16[1,1024,4096]{2,1,0:T(8,128)(2,1)}, u32[]{:S(2)}) %copy-start) | copy-done | bytes 8388632
  8.6 3.5 %collective-permute-done.1.refs_2_ = bf16[1024,128]{1,0:T(8,128)(2,1)S(1)} collective-permute-done((bf16[1024,128]{1,0:T(8,128)(2,1)S(1)}, bf16[1024,128]{1,0:T(8,128)(2,1)S(1)}, u32[]{:S(2)}, u32[]{:S(2)}) %collective-permute-start.1) | collective-permute-done | bytes 262176 | tf_op jit(solution)/shard_map/ppermute | solution.py:41
  12.1 4.2 %collective-permute-start.2 = (bf16[1024,128]{1,0:T(8,128)(2,1)S(1)}, bf16[1024,128]{1,0:T(8,128)(2,1)S(1)}, u32[]{:S(2)}, u32[]{:S(2)}) collective-permute-start(bf16[1024,128]{1,0:T(8,128)(2,1)S(1)} %collective-permute-done.1.refs_2_), channel_id=1, source_target_pairs={{0,4},{4,0},{8,12},{12,8},{1,5},{5,1},{9,13},{13,9},{2,6},{6,2},{1... | collective-permute-start | bytes 786440 | tf_op jit(solution)/shard_map/ppermute | solution.py:41
  16.3 2.5 %collective-permute-start.8 = (bf16[1024,128]{1,0:T(8,128)(2,1)S(1)}, bf16[1024,128]{1,0:T(8,128)(2,1)S(1)}, u32[]{:S(2)}, u32[]{:S(2)}) collective-permute-start(bf16[1024,128]{1,0:T(8,128)(2,1)S(1)} %slice.7.refs_0_), channel_id=1, source_target_pairs={{0,12},{4,8},{8,4},{12,0},{1,13},{5,9},{9,5},{13,1},{2,14},{6,10},... | collective-permute-start | bytes 786440 | tf_op jit(solution)/shard_map/ppermute | solution.py:41
  19.4 1.8 %begin.7.begun = f32[1024,128]{1,0:T(8,128)S(1)} custom-call(bf16[1024,4096]{1,0:T(8,128)(2,1)S(1)} %fetch.3.matrix, bf16[1024,128]{1,0:T(8,128)(2,1)S(1)} %slice.8.refs_0_, bf16[1024,128]{1,0:T(8,128)(2,1)S(1)} %collective-permute-done.refs_1_, bf16[1024,128]{1,0:T(8,128)(2,1)S(1)} %collective-permute-done.1.refs_2_, bf16[1024,4096]{1,0:T(8,128)(2,1)S(1)} %fetch.2.refs_3_.matrix), custom_call_target="tpu_custom_call" | custom-call | tf_op jit(solution)/shard_map/begin/pallas_call | solution.py:86
  21.2 1.8 %collective-permute-done.2.across = bf16[1024,128]{1,0:T(8,128)(2,1)S(1)} collective-permute-done((bf16[1024,128]{1,0:T(8,128)(2,1)S(1)}, bf16[1024,128]{1,0:T(8,128)(2,1)S(1)}, u32[]{:S(2)}, u32[]{:S(2)}) %collective-permute-start.2) | collective-permute-done | bytes 262176 | tf_op jit(solution)/shard_map/ppermute | solution.py:41
  24.4 2.5 %collective-permute-start.7 = (bf16[1024,128]{1,0:T(8,128)(2,1)S(1)}, bf16[1024,128]{1,0:T(8,128)(2,1)S(1)}, u32[]{:S(2)}, u32[]{:S(2)}) collective-permute-start(bf16[1024,128]{1,0:T(8,128)(2,1)S(1)} %slice.7.refs_0_), channel_id=1, source_target_pairs={{0,4},{4,0},{8,12},{12,8},{1,5},{5,1},{9,13},{13,9},{2,6},{6,2},{1... | collective-permute-start | bytes 786440 | tf_op jit(solution)/shard_map/ppermute | solution.py:41
  26.8 4.7 %collective-permute-done.8.refs_2_ = bf16[1024,128]{1,0:T(8,128)(2,1)S(1)} collective-permute-done((bf16[1024,128]{1,0:T(8,128)(2,1)S(1)}, bf16[1024,128]{1,0:T(8,128)(2,1)S(1)}, u32[]{:S(2)}, u32[]{:S(2)}) %collective-permute-start.8) | collective-permute-done | bytes 262176 | tf_op jit(solution)/shard_map/ppermute | solution.py:41
  31.6 3.3 %collective-permute-start.4 = (bf16[1024,128]{1,0:T(8,128)(2,1)S(1)}, bf16[1024,128]{1,0:T(8,128)(2,1)S(1)}, u32[]{:S(2)}, u32[]{:S(2)}) collective-permute-start(bf16[1024,128]{1,0:T(8,128)(2,1)S(1)} %collective-permute-done.3.refs_1_.refs_3_), channel_id=1, source_target_pairs={{2,14},{6,10},{10,6},{14,2},{3,15},{7,11},{11,7},{15,3},{18,30},{2... | collective-permute-start | bytes 786440 | tf_op jit(solution)/shard_map/ppermute | solution.py:46
  34.9 0.8 %collective-permute-done.7.refs_1_ = bf16[1024,128]{1,0:T(8,128)(2,1)S(1)} collective-permute-done((bf16[1024,128]{1,0:T(8,128)(2,1)S(1)}, bf16[1024,128]{1,0:T(8,128)(2,1)S(1)}, u32[]{:S(2)}, u32[]{:S(2)}) %collective-permute-start.7) | collective-permute-done | bytes 262176 | tf_op jit(solution)/shard_map/ppermute | solution.py:41
  35.7 1.8 %begin.10.begun = f32[1024,128]{1,0:T(8,128)S(1)} custom-call(bf16[1024,4096]{1,0:T(8,128)(2,1)S(1)} %fetch.3.matrix, bf16[1024,128]{1,0:T(8,128)(2,1)S(1)} %slice.7.refs_0_, bf16[1024,128]{1,0:T(8,128)(2,1)S(1)} %collective-permute-done.7.refs_1_, bf16[1024,128]{1,0:T(8,128)(2,1)S(1)} %collective-permute-done.8.refs_2_, ...), custom_call_target="tpu_custom_call" | custom-call | tf_op jit(solution)/shard_map/begin/pallas_call | solution.py:86
  37.4 4.2 %collective-permute-done.9.across = bf16[1024,128]{1,0:T(8,128)(2,1)S(1)} collective-permute-done((bf16[1024,128]{1,0:T(8,128)(2,1)S(1)}, bf16[1024,128]{1,0:T(8,128)(2,1)S(1)}, u32[]{:S(2)}, u32[]{:S(2)}) %collective-permute-start.9) | collective-permute-done | bytes 262176 | tf_op jit(solution)/shard_map/ppermute | solution.py:41
  41.6 0.7 %project.3 = (f32[1024,128]{1,0:T(8,128)S(1)}, bf16[1024,128]{1,0:T(8,128)(2,1)S(1)}) custom-call(bf16[1024,4096]{1,0:T(8,128)(2,1)S(1)} %fetch.3.matrix, f32[1024,128]{1,0:T(8,128)S(1)} %begin.10.begun, bf16[1024,128]{1,0:T(8,128)(2,1)S(1)} %collective-permute-done.9.across), custom_call_target="tpu_custom_call" | custom-call | tf_op jit(solution)/shard_map/project/pallas_call | solution.py:103
  42.4 2.6 %collective-permute-start.6 = (bf16[1024,128]{1,0:T(8,128)(2,1)S(1)}, bf16[1024,128]{1,0:T(8,128)(2,1)S(1)}, u32[]{:S(2)}, u32[]{:S(2)}) collective-permute-start(bf16[1024,128]{1,0:T(8,128)(2,1)S(1)} %collective-permute-done.3.refs_1_.refs_3_), channel_id=1, source_target_pairs={{2,6},{6,2},{10,14},{14,10},{3,7},{7,3},{11,15},{15,11},{18,22},{2... | collective-permute-start | bytes 786440 | tf_op jit(solution)/shard_map/ppermute | solution.py:46
  45.1 2.5 %collective-permute-done.4.refs_2_ = bf16[1024,128]{1,0:T(8,128)(2,1)S(1)} collective-permute-done((bf16[1024,128]{1,0:T(8,128)(2,1)S(1)}, bf16[1024,128]{1,0:T(8,128)(2,1)S(1)}, u32[]{:S(2)}, u32[]{:S(2)}) %collective-permute-start.4) | collective-permute-done | bytes 262176 | tf_op jit(solution)/shard_map/ppermute | solution.py:46
  47.6 1.9 %collective-permute-start.5 = (bf16[1024,128]{1,0:T(8,128)(2,1)S(1)}, bf16[1024,128]{1,0:T(8,128)(2,1)S(1)}, u32[]{:S(2)}, u32[]{:S(2)}) collective-permute-start(bf16[1024,128]{1,0:T(8,128)(2,1)S(1)} %collective-permute-done.4.refs_2_), channel_id=1, source_target_pairs={{2,6},{6,2},{10,14},{14,10},{3,7},{7,3},{11,15},{15,11},{18,22},{2... | collective-permute-start | bytes 786440 | tf_op jit(solution)/shard_map/ppermute | solution.py:46
  49.5 3.5 %collective-permute-start.12 = (bf16[1024,128]{1,0:T(8,128)(2,1)S(1)}, bf16[1024,128]{1,0:T(8,128)(2,1)S(1)}, u32[]{:S(2)}, u32[]{:S(2)}) collective-permute-start(bf16[1024,128]{1,0:T(8,128)(2,1)S(1)} %get-tuple-element.22.narrow2), channel_id=1, source_target_pairs={{0,10},{4,14},{8,2},{12,6},{2,0},{6,4},{10,8},{14,12},{1,11},{5,15... | collective-permute-start | bytes 786440 | tf_op jit(solution)/shard_map/ppermute | solution.py:46
  53.0 3.6 %collective-permute-start.13 = (bf16[1024,128]{1,0:T(8,128)(2,1)S(1)}, bf16[1024,128]{1,0:T(8,128)(2,1)S(1)}, u32[]{:S(2)}, u32[]{:S(2)}) collective-permute-start(bf16[1024,128]{1,0:T(8,128)(2,1)S(1)} %collective-permute-done.10.refs_1_), channel_id=1, source_target_pairs={{2,14},{6,10},{10,6},{14,2},{3,15},{7,11},{11,7},{15,3},{18,30},{2... | collective-permute-start | bytes 786440 | tf_op jit(solution)/shard_map/ppermute | solution.py:46
  56.6 1.2 %begin.8.refs_0_ = f32[1024,128]{1,0:T(8,128)S(1)} custom-call(bf16[1024,4096]{1,0:T(8,128)(2,1)S(1)} %fetch.2.refs_3_.matrix, f32[1024,128]{1,0:T(8,128)S(1)} %get-tuple-element.15.refs_0_, bf16[1024,128]{1,0:T(8,128)(2,1)S(1)} %collective-permute-done.3.refs_1_.refs_3_, bf16[1024,128]{1,0:T(8,128)(2,1)S(1)} %collective-permute-done.4.refs_2_), custom_call_target="tpu_custom_call" | custom-call | tf_op jit(solution)/shard_map/begin/pallas_call | solution.py:86
  58.6 1.4 %collective-permute-done.5.refs_1_ = bf16[1024,128]{1,0:T(8,128)(2,1)S(1)} collective-permute-done((bf16[1024,128]{1,0:T(8,128)(2,1)S(1)}, bf16[1024,128]{1,0:T(8,128)(2,1)S(1)}, u32[]{:S(2)}, u32[]{:S(2)}) %collective-permute-start.5) | collective-permute-done | bytes 262176 | tf_op jit(solution)/shard_map/ppermute | solution.py:46
  60.7 0.7 %settle.1.first = bf16[1024,128]{1,0:T(8,128)(2,1)S(1)} custom-call(bf16[1024,4096]{1,0:T(8,128)(2,1)S(1)} %fetch.2.refs_3_.matrix, f32[1024,128]{1,0:T(8,128)S(1)} %begin.9.left, bf16[1024,128]{1,0:T(8,128)(2,1)S(1)} %get-tuple-element.16.narrow, bf16[1024,128]{1,0:T(8,128)(2,1)S(1)} %collective-permute-done.6.near), custom_call_target="tpu_custom_call" | custom-call | tf_op jit(solution)/shard_map/settle/pallas_call | solution.py:122
  63.4 1.4 %finish.1 = bf16[1024,256]{1,0:T(8,128)(2,1)} custom-call(bf16[1024,4096]{1,0:T(8,128)(2,1)S(1)} %fetch.2.refs_3_.matrix, bf16[1024,128]{1,0:T(8,128)(2,1)S(1)} %settle.1.first, f32[1024,128]{1,0:T(8,128)S(1)} %begin.13.left2, bf16[1024,128]{1,0:T(8,128)(2,1)S(1)} %get-tuple-element.22.narrow2, bf16[1024,128]{1,0:T(8,128)(2,1)S(1)} %collective-permute-done.13.refs_0_), custom_call_target="tpu_custom_call" | custom-call | tf_op jit(solution)/shard_map/finish/pallas_call | solution.py:152
  (25 shorter events, 6.0 us)
Async XLA Ops:
  1.0 11.1 %collective-permute-start.1 = (bf16[1024,128]{1,0:T(8,128)(2,1)S(1)}, bf16[1024,128]{1,0:T(8,128)(2,1)S(1)}, u32[]{:S(2)}, u32[]{:S(2)}) collective-permute-start(bf16[1024,128]{1,0:T(8,128)(2,1)S(1)} %slice.8.refs_0_), channel_id=1, source_target_pairs={{0,12},{4,8},{8,4},{12,0},{1,13},{5,9},{9,5},{13,1},{2,14},{6,10},... | collective-permute-start | bytes 786440 | tf_op jit(solution)/shard_map/ppermute | solution.py:41
  4.6 14.8 %collective-permute-start = (bf16[1024,128]{1,0:T(8,128)(2,1)S(1)}, bf16[1024,128]{1,0:T(8,128)(2,1)S(1)}, u32[]{:S(2)}, u32[]{:S(2)}) collective-permute-start(bf16[1024,128]{1,0:T(8,128)(2,1)S(1)} %slice.8.refs_0_), channel_id=1, source_target_pairs={{0,4},{4,0},{8,12},{12,8},{1,5},{5,1},{9,13},{13,9},{2,6},{6,2},{1... | collective-permute-start | bytes 786440 | tf_op jit(solution)/shard_map/ppermute | solution.py:41
  4.6 3.4 %copy-start = (bf16[1,1024,4096]{2,1,0:T(8,128)(2,1)S(1)}, bf16[1,1024,4096]{2,1,0:T(8,128)(2,1)}, u32[]{:S(2)}) copy-start(bf16[1,1024,4096]{2,1,0:T(8,128)(2,1)} %param.4) | copy-start | bytes 25165828
  8.0 8.3 %copy-start.2 = (bf16[1,1024,256]{2,1,0:T(8,128)(2,1)S(1)}, bf16[1,1024,256]{2,1,0:T(8,128)(2,1)}, u32[]{:S(2)}) copy-start(bf16[1,1024,256]{2,1,0:T(8,128)(2,1)} %param.3) | copy-start | bytes 1572868
  8.0 10.8 %copy-start.1 = (bf16[1,1024,4096]{2,1,0:T(8,128)(2,1)S(1)}, bf16[1,1024,4096]{2,1,0:T(8,128)(2,1)}, u32[]{:S(2)}) copy-start(bf16[1,1024,4096]{2,1,0:T(8,128)(2,1)} %param.5) | copy-start | bytes 25165828
  12.1 11.0 %collective-permute-start.2 = (bf16[1024,128]{1,0:T(8,128)(2,1)S(1)}, bf16[1024,128]{1,0:T(8,128)(2,1)S(1)}, u32[]{:S(2)}, u32[]{:S(2)}) collective-permute-start(bf16[1024,128]{1,0:T(8,128)(2,1)S(1)} %collective-permute-done.1.refs_2_), channel_id=1, source_target_pairs={{0,4},{4,0},{8,12},{12,8},{1,5},{5,1},{9,13},{13,9},{2,6},{6,2},{1... | collective-permute-start | bytes 786440 | tf_op jit(solution)/shard_map/ppermute | solution.py:41
  16.3 15.3 %collective-permute-start.8 = (bf16[1024,128]{1,0:T(8,128)(2,1)S(1)}, bf16[1024,128]{1,0:T(8,128)(2,1)S(1)}, u32[]{:S(2)}, u32[]{:S(2)}) collective-permute-start(bf16[1024,128]{1,0:T(8,128)(2,1)S(1)} %slice.7.refs_0_), channel_id=1, source_target_pairs={{0,12},{4,8},{8,4},{12,0},{1,13},{5,9},{9,5},{13,1},{2,14},{6,10},... | collective-permute-start | bytes 786440 | tf_op jit(solution)/shard_map/ppermute | solution.py:41
  23.8 7.8 %collective-permute-start.3 = (bf16[1024,128]{1,0:T(8,128)(2,1)S(1)}, bf16[1024,128]{1,0:T(8,128)(2,1)S(1)}, u32[]{:S(2)}, u32[]{:S(2)}) collective-permute-start(bf16[1024,128]{1,0:T(8,128)(2,1)S(1)} %get-tuple-element.16.narrow), channel_id=1, source_target_pairs={{0,2},{4,6},{8,10},{12,14},{2,0},{6,4},{10,8},{14,12},{1,3},{5,7},... | collective-permute-start | bytes 786440 | tf_op jit(solution)/shard_map/ppermute | solution.py:46
  24.4 11.3 %collective-permute-start.7 = (bf16[1024,128]{1,0:T(8,128)(2,1)S(1)}, bf16[1024,128]{1,0:T(8,128)(2,1)S(1)}, u32[]{:S(2)}, u32[]{:S(2)}) collective-permute-start(bf16[1024,128]{1,0:T(8,128)(2,1)S(1)} %slice.7.refs_0_), channel_id=1, source_target_pairs={{0,4},{4,0},{8,12},{12,8},{1,5},{5,1},{9,13},{13,9},{2,6},{6,2},{1... | collective-permute-start | bytes 786440 | tf_op jit(solution)/shard_map/ppermute | solution.py:41
  31.6 10.1 %collective-permute-start.9 = (bf16[1024,128]{1,0:T(8,128)(2,1)S(1)}, bf16[1024,128]{1,0:T(8,128)(2,1)S(1)}, u32[]{:S(2)}, u32[]{:S(2)}) collective-permute-start(bf16[1024,128]{1,0:T(8,128)(2,1)S(1)} %collective-permute-done.8.refs_2_), channel_id=1, source_target_pairs={{0,4},{4,0},{8,12},{12,8},{1,5},{5,1},{9,13},{13,9},{2,6},{6,2},{1... | collective-permute-start | bytes 786440 | tf_op jit(solution)/shard_map/ppermute | solution.py:41
  31.6 16.0 %collective-permute-start.4 = (bf16[1024,128]{1,0:T(8,128)(2,1)S(1)}, bf16[1024,128]{1,0:T(8,128)(2,1)S(1)}, u32[]{:S(2)}, u32[]{:S(2)}) collective-permute-start(bf16[1024,128]{1,0:T(8,128)(2,1)S(1)} %collective-permute-done.3.refs_1_.refs_3_), channel_id=1, source_target_pairs={{2,14},{6,10},{10,6},{14,2},{3,15},{7,11},{11,7},{15,3},{18,30},{2... | collective-permute-start | bytes 786440 | tf_op jit(solution)/shard_map/ppermute | solution.py:46
  42.4 7.1 %collective-permute-start.10 = (bf16[1024,128]{1,0:T(8,128)(2,1)S(1)}, bf16[1024,128]{1,0:T(8,128)(2,1)S(1)}, u32[]{:S(2)}, u32[]{:S(2)}) collective-permute-start(bf16[1024,128]{1,0:T(8,128)(2,1)S(1)} %get-tuple-element.22.narrow2), channel_id=1, source_target_pairs={{0,2},{4,6},{8,10},{12,14},{2,0},{6,4},{10,8},{14,12},{1,3},{5,7},... | collective-permute-start | bytes 786440 | tf_op jit(solution)/shard_map/ppermute | solution.py:46
  42.4 18.2 %collective-permute-start.6 = (bf16[1024,128]{1,0:T(8,128)(2,1)S(1)}, bf16[1024,128]{1,0:T(8,128)(2,1)S(1)}, u32[]{:S(2)}, u32[]{:S(2)}) collective-permute-start(bf16[1024,128]{1,0:T(8,128)(2,1)S(1)} %collective-permute-done.3.refs_1_.refs_3_), channel_id=1, source_target_pairs={{2,6},{6,2},{10,14},{14,10},{3,7},{7,3},{11,15},{15,11},{18,22},{2... | collective-permute-start | bytes 786440 | tf_op jit(solution)/shard_map/ppermute | solution.py:46
  47.6 12.4 %collective-permute-start.5 = (bf16[1024,128]{1,0:T(8,128)(2,1)S(1)}, bf16[1024,128]{1,0:T(8,128)(2,1)S(1)}, u32[]{:S(2)}, u32[]{:S(2)}) collective-permute-start(bf16[1024,128]{1,0:T(8,128)(2,1)S(1)} %collective-permute-done.4.refs_2_), channel_id=1, source_target_pairs={{2,6},{6,2},{10,14},{14,10},{3,7},{7,3},{11,15},{15,11},{18,22},{2... | collective-permute-start | bytes 786440 | tf_op jit(solution)/shard_map/ppermute | solution.py:46
  49.5 11.9 %collective-permute-start.11 = (bf16[1024,128]{1,0:T(8,128)(2,1)S(1)}, bf16[1024,128]{1,0:T(8,128)(2,1)S(1)}, u32[]{:S(2)}, u32[]{:S(2)}) collective-permute-start(bf16[1024,128]{1,0:T(8,128)(2,1)S(1)} %get-tuple-element.22.narrow2), channel_id=1, source_target_pairs={{0,6},{4,2},{8,14},{12,10},{2,0},{6,4},{10,8},{14,12},{1,7},{5,3},... | collective-permute-start | bytes 786440 | tf_op jit(solution)/shard_map/ppermute | solution.py:46
  49.5 12.6 %collective-permute-start.12 = (bf16[1024,128]{1,0:T(8,128)(2,1)S(1)}, bf16[1024,128]{1,0:T(8,128)(2,1)S(1)}, u32[]{:S(2)}, u32[]{:S(2)}) collective-permute-start(bf16[1024,128]{1,0:T(8,128)(2,1)S(1)} %get-tuple-element.22.narrow2), channel_id=1, source_target_pairs={{0,10},{4,14},{8,2},{12,6},{2,0},{6,4},{10,8},{14,12},{1,11},{5,15... | collective-permute-start | bytes 786440 | tf_op jit(solution)/shard_map/ppermute | solution.py:46
  53.0 10.4 %collective-permute-start.13 = (bf16[1024,128]{1,0:T(8,128)(2,1)S(1)}, bf16[1024,128]{1,0:T(8,128)(2,1)S(1)}, u32[]{:S(2)}, u32[]{:S(2)}) collective-permute-start(bf16[1024,128]{1,0:T(8,128)(2,1)S(1)} %collective-permute-done.10.refs_1_), channel_id=1, source_target_pairs={{2,14},{6,10},{10,6},{14,2},{3,15},{7,11},{11,7},{15,3},{18,30},{2... | collective-permute-start | bytes 786440 | tf_op jit(solution)/shard_map/ppermute | solution.py:46

commit v7 on v6

--- a/solution.py
+++ b/solution.py
@@ -135,8 +135,8 @@
     early = pltpu.make_async_copy(first, out.at[:, :cols], sems.at[0])
     early.start()
     copies = [early]
-    tall = first.shape[0] // 2
-    for part in range(2):
+    tall = first.shape[0] // 4
+    for part in range(4):
         rows = slice(part * tall, (part + 1) * tall)
         total = (left2[rows] - product(apart, matrix.at[rows], blocks)).astype(jnp.bfloat16)
         rest[rows] = jnp.where(lax.axis_index("zone") == k, total, narrow2[rows])
@@ -154,7 +154,7 @@
         out_shape=jax.ShapeDtypeStruct((rows, 2 * cols), jnp.bfloat16),
         in_specs=[VMEM] * (4 + len(blocks)),
         out_specs=HBM,
-        scratch_shapes=[pltpu.VMEM((rows, cols), jnp.bfloat16), pltpu.SemaphoreType.DMA((3,))],
+        scratch_shapes=[pltpu.VMEM((rows, cols), jnp.bfloat16), pltpu.SemaphoreType.DMA((5,))],
         compiler_params=params(8),
         name="finish",
     )(matrix, first, left2, narrow2, *blocks)

time: 65.8 us -> 65.7 us (level)
  no operation moved by 1% of the time
where the time goes in v7:
time: 65.7 us; the launch traced here: 64.8 us
  starting transfers between devices  28.5 us (43%)
  waiting for transfers between devices  19.4 us (30%)
  Pallas kernels  12.3 us (19%)
  local copies, waits for them, and re-layouts  4.37 us (7%)
    ppermute x8, starting transfers between devices, across_zones(): lax.ppermute(block, ('panel', 'zone'), [(a * zones + y, b * zones + z) fo...  15.6 us
    ppermute x6, waiting for transfers between devices, swap_panels(): return lax.ppermute(block, 'panel', [(p, p ^ apart) for p in range(4)])  15 us
    ppermute x6, starting transfers between devices, swap_panels(): return lax.ppermute(block, 'panel', [(p, p ^ apart) for p in range(4)])  12.9 us
    pallas_call x7, Pallas kernels, begin(): pl.pallas_call(functools.partial(begin_kernel, apart, len(held) - 1), out...  7.63 us
    ppermute x8, waiting for transfers between devices, across_zones(): lax.ppermute(block, ('panel', 'zone'), [(a * zones + y, b * zones + z) fo...  4.4 us
    unnamed x6, local copies, waits for them, and re-layouts  3.39 us
    pallas_call x2, Pallas kernels, project(): pl.pallas_call(project_kernel, out_shape=(jax.ShapeDtypeStruct(across.sha...  1.42 us
    pallas_call x1, Pallas kernels, finish(): pl.pallas_call(functools.partial(finish_kernel, apart, k), out_shape=jax....  1.38 us
  transfers between devices with their start and end apart: 14, of which 8 were waited for; matrix products, arithmetic and copies ran while one was open for 0% of the time, Pallas kernels for 17%

profile of v7, /device:TPU:6, one launch (start us, length us, event | category | flops | bytes accessed | tf_op | source)
XLA Modules:
  0.0 64.8 jit_solution(6716336255836436030)
XLA Ops:
  0.0 1.0 %slice.8.refs_0_ = bf16[1024,128]{1,0:T(8,128)(2,1)S(1)} slice(bf16[1024,256]{1,0:T(8,128)(2,1)} %bitcast.6), slice={[0:1024], [0:128]} | slice | bytes 524288 | tf_op jit(solution)/shard_map/slice | solution.py:166
  1.0 3.7 %collective-permute-start.1 = (bf16[1024,128]{1,0:T(8,128)(2,1)S(1)}, bf16[1024,128]{1,0:T(8,128)(2,1)S(1)}, u32[]{:S(2)}, u32[]{:S(2)}) collective-permute-start(bf16[1024,128]{1,0:T(8,128)(2,1)S(1)} %slice.8.refs_0_), channel_id=1, source_target_pairs={{0,12},{4,8},{8,4},{12,0},{1,13},{5,9},{9,5},{13,1},{2,14},{6,10},... | collective-permute-start | bytes 786440 | tf_op jit(solution)/shard_map/ppermute | solution.py:41
  4.6 3.4 %copy-done = bf16[1,1024,4096]{2,1,0:T(8,128)(2,1)S(1)} copy-done((bf16[1,1024,4096]{2,1,0:T(8,128)(2,1)S(1)}, bf16[1,1024,4096]{2,1,0:T(8,128)(2,1)}, u32[]{:S(2)}) %copy-start) | copy-done | bytes 8388632
  8.6 3.5 %collective-permute-done.1.refs_2_ = bf16[1024,128]{1,0:T(8,128)(2,1)S(1)} collective-permute-done((bf16[1024,128]{1,0:T(8,128)(2,1)S(1)}, bf16[1024,128]{1,0:T(8,128)(2,1)S(1)}, u32[]{:S(2)}, u32[]{:S(2)}) %collective-permute-start.1) | collective-permute-done | bytes 262176 | tf_op jit(solution)/shard_map/ppermute | solution.py:41
  12.1 4.2 %collective-permute-start.2 = (bf16[1024,128]{1,0:T(8,128)(2,1)S(1)}, bf16[1024,128]{1,0:T(8,128)(2,1)S(1)}, u32[]{:S(2)}, u32[]{:S(2)}) collective-permute-start(bf16[1024,128]{1,0:T(8,128)(2,1)S(1)} %collective-permute-done.1.refs_2_), channel_id=1, source_target_pairs={{0,4},{4,0},{8,12},{12,8},{1,5},{5,1},{9,13},{13,9},{2,6},{6,2},{1... | collective-permute-start | bytes 786440 | tf_op jit(solution)/shard_map/ppermute | solution.py:41
  16.3 2.5 %collective-permute-start.8 = (bf16[1024,128]{1,0:T(8,128)(2,1)S(1)}, bf16[1024,128]{1,0:T(8,128)(2,1)S(1)}, u32[]{:S(2)}, u32[]{:S(2)}) collective-permute-start(bf16[1024,128]{1,0:T(8,128)(2,1)S(1)} %slice.7.refs_0_), channel_id=1, source_target_pairs={{0,12},{4,8},{8,4},{12,0},{1,13},{5,9},{9,5},{13,1},{2,14},{6,10},... | collective-permute-start | bytes 786440 | tf_op jit(solution)/shard_map/ppermute | solution.py:41
  19.4 1.8 %begin.7.begun = f32[1024,128]{1,0:T(8,128)S(1)} custom-call(bf16[1024,4096]{1,0:T(8,128)(2,1)S(1)} %fetch.3.matrix, bf16[1024,128]{1,0:T(8,128)(2,1)S(1)} %slice.8.refs_0_, bf16[1024,128]{1,0:T(8,128)(2,1)S(1)} %collective-permute-done.refs_1_, bf16[1024,128]{1,0:T(8,128)(2,1)S(1)} %collective-permute-done.1.refs_2_, bf16[1024,4096]{1,0:T(8,128)(2,1)S(1)} %fetch.2.refs_3_.matrix), custom_call_target="tpu_custom_call" | custom-call | tf_op jit(solution)/shard_map/begin/pallas_call | solution.py:86
  21.2 1.8 %collective-permute-done.2.across = bf16[1024,128]{1,0:T(8,128)(2,1)S(1)} collective-permute-done((bf16[1024,128]{1,0:T(8,128)(2,1)S(1)}, bf16[1024,128]{1,0:T(8,128)(2,1)S(1)}, u32[]{:S(2)}, u32[]{:S(2)}) %collective-permute-start.2) | collective-permute-done | bytes 262176 | tf_op jit(solution)/shard_map/ppermute | solution.py:41
  24.4 2.5 %collective-permute-start.7 = (bf16[1024,128]{1,0:T(8,128)(2,1)S(1)}, bf16[1024,128]{1,0:T(8,128)(2,1)S(1)}, u32[]{:S(2)}, u32[]{:S(2)}) collective-permute-start(bf16[1024,128]{1,0:T(8,128)(2,1)S(1)} %slice.7.refs_0_), channel_id=1, source_target_pairs={{0,4},{4,0},{8,12},{12,8},{1,5},{5,1},{9,13},{13,9},{2,6},{6,2},{1... | collective-permute-start | bytes 786440 | tf_op jit(solution)/shard_map/ppermute | solution.py:41
  26.8 4.7 %collective-permute-done.8.refs_2_ = bf16[1024,128]{1,0:T(8,128)(2,1)S(1)} collective-permute-done((bf16[1024,128]{1,0:T(8,128)(2,1)S(1)}, bf16[1024,128]{1,0:T(8,128)(2,1)S(1)}, u32[]{:S(2)}, u32[]{:S(2)}) %collective-permute-start.8) | collective-permute-done | bytes 262176 | tf_op jit(solution)/shard_map/ppermute | solution.py:41
  31.6 3.3 %collective-permute-start.4 = (bf16[1024,128]{1,0:T(8,128)(2,1)S(1)}, bf16[1024,128]{1,0:T(8,128)(2,1)S(1)}, u32[]{:S(2)}, u32[]{:S(2)}) collective-permute-start(bf16[1024,128]{1,0:T(8,128)(2,1)S(1)} %collective-permute-done.3.refs_1_.refs_3_), channel_id=1, source_target_pairs={{2,14},{6,10},{10,6},{14,2},{3,15},{7,11},{11,7},{15,3},{18,30},{2... | collective-permute-start | bytes 786440 | tf_op jit(solution)/shard_map/ppermute | solution.py:46
  34.9 0.8 %collective-permute-done.7.refs_1_ = bf16[1024,128]{1,0:T(8,128)(2,1)S(1)} collective-permute-done((bf16[1024,128]{1,0:T(8,128)(2,1)S(1)}, bf16[1024,128]{1,0:T(8,128)(2,1)S(1)}, u32[]{:S(2)}, u32[]{:S(2)}) %collective-permute-start.7) | collective-permute-done | bytes 262176 | tf_op jit(solution)/shard_map/ppermute | solution.py:41
  35.7 1.8 %begin.10.begun = f32[1024,128]{1,0:T(8,128)S(1)} custom-call(bf16[1024,4096]{1,0:T(8,128)(2,1)S(1)} %fetch.3.matrix, bf16[1024,128]{1,0:T(8,128)(2,1)S(1)} %slice.7.refs_0_, bf16[1024,128]{1,0:T(8,128)(2,1)S(1)} %collective-permute-done.7.refs_1_, bf16[1024,128]{1,0:T(8,128)(2,1)S(1)} %collective-permute-done.8.refs_2_, ...), custom_call_target="tpu_custom_call" | custom-call | tf_op jit(solution)/shard_map/begin/pallas_call | solution.py:86
  37.4 4.2 %collective-permute-done.9.across = bf16[1024,128]{1,0:T(8,128)(2,1)S(1)} collective-permute-done((bf16[1024,128]{1,0:T(8,128)(2,1)S(1)}, bf16[1024,128]{1,0:T(8,128)(2,1)S(1)}, u32[]{:S(2)}, u32[]{:S(2)}) %collective-permute-start.9) | collective-permute-done | bytes 262176 | tf_op jit(solution)/shard_map/ppermute | solution.py:41
  41.6 0.7 %project.3 = (f32[1024,128]{1,0:T(8,128)S(1)}, bf16[1024,128]{1,0:T(8,128)(2,1)S(1)}) custom-call(bf16[1024,4096]{1,0:T(8,128)(2,1)S(1)} %fetch.3.matrix, f32[1024,128]{1,0:T(8,128)S(1)} %begin.10.begun, bf16[1024,128]{1,0:T(8,128)(2,1)S(1)} %collective-permute-done.9.across), custom_call_target="tpu_custom_call" | custom-call | tf_op jit(solution)/shard_map/project/pallas_call | solution.py:103
  42.4 2.6 %collective-permute-start.6 = (bf16[1024,128]{1,0:T(8,128)(2,1)S(1)}, bf16[1024,128]{1,0:T(8,128)(2,1)S(1)}, u32[]{:S(2)}, u32[]{:S(2)}) collective-permute-start(bf16[1024,128]{1,0:T(8,128)(2,1)S(1)} %collective-permute-done.3.refs_1_.refs_3_), channel_id=1, source_target_pairs={{2,6},{6,2},{10,14},{14,10},{3,7},{7,3},{11,15},{15,11},{18,22},{2... | collective-permute-start | bytes 786440 | tf_op jit(solution)/shard_map/ppermute | solution.py:46
  45.1 2.5 %collective-permute-done.4.refs_2_ = bf16[1024,128]{1,0:T(8,128)(2,1)S(1)} collective-permute-done((bf16[1024,128]{1,0:T(8,128)(2,1)S(1)}, bf16[1024,128]{1,0:T(8,128)(2,1)S(1)}, u32[]{:S(2)}, u32[]{:S(2)}) %collective-permute-start.4) | collective-permute-done | bytes 262176 | tf_op jit(solution)/shard_map/ppermute | solution.py:46
  47.6 1.9 %collective-permute-start.5 = (bf16[1024,128]{1,0:T(8,128)(2,1)S(1)}, bf16[1024,128]{1,0:T(8,128)(2,1)S(1)}, u32[]{:S(2)}, u32[]{:S(2)}) collective-permute-start(bf16[1024,128]{1,0:T(8,128)(2,1)S(1)} %collective-permute-done.4.refs_2_), channel_id=1, source_target_pairs={{2,6},{6,2},{10,14},{14,10},{3,7},{7,3},{11,15},{15,11},{18,22},{2... | collective-permute-start | bytes 786440 | tf_op jit(solution)/shard_map/ppermute | solution.py:46
  49.5 3.5 %collective-permute-start.12 = (bf16[1024,128]{1,0:T(8,128)(2,1)S(1)}, bf16[1024,128]{1,0:T(8,128)(2,1)S(1)}, u32[]{:S(2)}, u32[]{:S(2)}) collective-permute-start(bf16[1024,128]{1,0:T(8,128)(2,1)S(1)} %get-tuple-element.22.narrow2), channel_id=1, source_target_pairs={{0,10},{4,14},{8,2},{12,6},{2,0},{6,4},{10,8},{14,12},{1,11},{5,15... | collective-permute-start | bytes 786440 | tf_op jit(solution)/shard_map/ppermute | solution.py:46
  53.0 3.6 %collective-permute-start.13 = (bf16[1024,128]{1,0:T(8,128)(2,1)S(1)}, bf16[1024,128]{1,0:T(8,128)(2,1)S(1)}, u32[]{:S(2)}, u32[]{:S(2)}) collective-permute-start(bf16[1024,128]{1,0:T(8,128)(2,1)S(1)} %collective-permute-done.10.refs_1_), channel_id=1, source_target_pairs={{2,14},{6,10},{10,6},{14,2},{3,15},{7,11},{11,7},{15,3},{18,30},{2... | collective-permute-start | bytes 786440 | tf_op jit(solution)/shard_map/ppermute | solution.py:46
  56.6 1.2 %begin.8.refs_0_ = f32[1024,128]{1,0:T(8,128)S(1)} custom-call(bf16[1024,4096]{1,0:T(8,128)(2,1)S(1)} %fetch.2.refs_3_.matrix, f32[1024,128]{1,0:T(8,128)S(1)} %get-tuple-element.15.refs_0_, bf16[1024,128]{1,0:T(8,128)(2,1)S(1)} %collective-permute-done.3.refs_1_.refs_3_, bf16[1024,128]{1,0:T(8,128)(2,1)S(1)} %collective-permute-done.4.refs_2_), custom_call_target="tpu_custom_call" | custom-call | tf_op jit(solution)/shard_map/begin/pallas_call | solution.py:86
  58.6 1.4 %collective-permute-done.5.refs_1_ = bf16[1024,128]{1,0:T(8,128)(2,1)S(1)} collective-permute-done((bf16[1024,128]{1,0:T(8,128)(2,1)S(1)}, bf16[1024,128]{1,0:T(8,128)(2,1)S(1)}, u32[]{:S(2)}, u32[]{:S(2)}) %collective-permute-start.5) | collective-permute-done | bytes 262176 | tf_op jit(solution)/shard_map/ppermute | solution.py:46
  60.7 0.7 %settle.1.first = bf16[1024,128]{1,0:T(8,128)(2,1)S(1)} custom-call(bf16[1024,4096]{1,0:T(8,128)(2,1)S(1)} %fetch.2.refs_3_.matrix, f32[1024,128]{1,0:T(8,128)S(1)} %begin.9.left, bf16[1024,128]{1,0:T(8,128)(2,1)S(1)} %get-tuple-element.16.narrow, bf16[1024,128]{1,0:T(8,128)(2,1)S(1)} %collective-permute-done.6.near), custom_call_target="tpu_custom_call" | custom-call | tf_op jit(solution)/shard_map/settle/pallas_call | solution.py:122
  63.4 1.4 %finish.1 = bf16[1024,256]{1,0:T(8,128)(2,1)} custom-call(bf16[1024,4096]{1,0:T(8,128)(2,1)S(1)} %fetch.2.refs_3_.matrix, bf16[1024,128]{1,0:T(8,128)(2,1)S(1)} %settle.1.first, f32[1024,128]{1,0:T(8,128)S(1)} %begin.13.left2, bf16[1024,128]{1,0:T(8,128)(2,1)S(1)} %get-tuple-element.22.narrow2, bf16[1024,128]{1,0:T(8,128)(2,1)S(1)} %collective-permute-done.13.refs_0_), custom_call_target="tpu_custom_call" | custom-call | tf_op jit(solution)/shard_map/finish/pallas_call | solution.py:152
  (25 shorter events, 6.0 us)
Async XLA Ops:
  1.0 11.1 %collective-permute-start.1 = (bf16[1024,128]{1,0:T(8,128)(2,1)S(1)}, bf16[1024,128]{1,0:T(8,128)(2,1)S(1)}, u32[]{:S(2)}, u32[]{:S(2)}) collective-permute-start(bf16[1024,128]{1,0:T(8,128)(2,1)S(1)} %slice.8.refs_0_), channel_id=1, source_target_pairs={{0,12},{4,8},{8,4},{12,0},{1,13},{5,9},{9,5},{13,1},{2,14},{6,10},... | collective-permute-start | bytes 786440 | tf_op jit(solution)/shard_map/ppermute | solution.py:41
  4.6 14.8 %collective-permute-start = (bf16[1024,128]{1,0:T(8,128)(2,1)S(1)}, bf16[1024,128]{1,0:T(8,128)(2,1)S(1)}, u32[]{:S(2)}, u32[]{:S(2)}) collective-permute-start(bf16[1024,128]{1,0:T(8,128)(2,1)S(1)} %slice.8.refs_0_), channel_id=1, source_target_pairs={{0,4},{4,0},{8,12},{12,8},{1,5},{5,1},{9,13},{13,9},{2,6},{6,2},{1... | collective-permute-start | bytes 786440 | tf_op jit(solution)/shard_map/ppermute | solution.py:41
  4.6 3.4 %copy-start = (bf16[1,1024,4096]{2,1,0:T(8,128)(2,1)S(1)}, bf16[1,1024,4096]{2,1,0:T(8,128)(2,1)}, u32[]{:S(2)}) copy-start(bf16[1,1024,4096]{2,1,0:T(8,128)(2,1)} %param.4) | copy-start | bytes 25165828
  8.0 8.3 %copy-start.2 = (bf16[1,1024,256]{2,1,0:T(8,128)(2,1)S(1)}, bf16[1,1024,256]{2,1,0:T(8,128)(2,1)}, u32[]{:S(2)}) copy-start(bf16[1,1024,256]{2,1,0:T(8,128)(2,1)} %param.3) | copy-start | bytes 1572868
  8.0 10.8 %copy-start.1 = (bf16[1,1024,4096]{2,1,0:T(8,128)(2,1)S(1)}, bf16[1,1024,4096]{2,1,0:T(8,128)(2,1)}, u32[]{:S(2)}) copy-start(bf16[1,1024,4096]{2,1,0:T(8,128)(2,1)} %param.5) | copy-start | bytes 25165828
  12.1 11.0 %collective-permute-start.2 = (bf16[1024,128]{1,0:T(8,128)(2,1)S(1)}, bf16[1024,128]{1,0:T(8,128)(2,1)S(1)}, u32[]{:S(2)}, u32[]{:S(2)}) collective-permute-start(bf16[1024,128]{1,0:T(8,128)(2,1)S(1)} %collective-permute-done.1.refs_2_), channel_id=1, source_target_pairs={{0,4},{4,0},{8,12},{12,8},{1,5},{5,1},{9,13},{13,9},{2,6},{6,2},{1... | collective-permute-start | bytes 786440 | tf_op jit(solution)/shard_map/ppermute | solution.py:41
  16.3 15.3 %collective-permute-start.8 = (bf16[1024,128]{1,0:T(8,128)(2,1)S(1)}, bf16[1024,128]{1,0:T(8,128)(2,1)S(1)}, u32[]{:S(2)}, u32[]{:S(2)}) collective-permute-start(bf16[1024,128]{1,0:T(8,128)(2,1)S(1)} %slice.7.refs_0_), channel_id=1, source_target_pairs={{0,12},{4,8},{8,4},{12,0},{1,13},{5,9},{9,5},{13,1},{2,14},{6,10},... | collective-permute-start | bytes 786440 | tf_op jit(solution)/shard_map/ppermute | solution.py:41
  23.8 7.8 %collective-permute-start.3 = (bf16[1024,128]{1,0:T(8,128)(2,1)S(1)}, bf16[1024,128]{1,0:T(8,128)(2,1)S(1)}, u32[]{:S(2)}, u32[]{:S(2)}) collective-permute-start(bf16[1024,128]{1,0:T(8,128)(2,1)S(1)} %get-tuple-element.16.narrow), channel_id=1, source_target_pairs={{0,2},{4,6},{8,10},{12,14},{2,0},{6,4},{10,8},{14,12},{1,3},{5,7},... | collective-permute-start | bytes 786440 | tf_op jit(solution)/shard_map/ppermute | solution.py:46
  24.4 11.3 %collective-permute-start.7 = (bf16[1024,128]{1,0:T(8,128)(2,1)S(1)}, bf16[1024,128]{1,0:T(8,128)(2,1)S(1)}, u32[]{:S(2)}, u32[]{:S(2)}) collective-permute-start(bf16[1024,128]{1,0:T(8,128)(2,1)S(1)} %slice.7.refs_0_), channel_id=1, source_target_pairs={{0,4},{4,0},{8,12},{12,8},{1,5},{5,1},{9,13},{13,9},{2,6},{6,2},{1... | collective-permute-start | bytes 786440 | tf_op jit(solution)/shard_map/ppermute | solution.py:41
  31.6 10.1 %collective-permute-start.9 = (bf16[1024,128]{1,0:T(8,128)(2,1)S(1)}, bf16[1024,128]{1,0:T(8,128)(2,1)S(1)}, u32[]{:S(2)}, u32[]{:S(2)}) collective-permute-start(bf16[1024,128]{1,0:T(8,128)(2,1)S(1)} %collective-permute-done.8.refs_2_), channel_id=1, source_target_pairs={{0,4},{4,0},{8,12},{12,8},{1,5},{5,1},{9,13},{13,9},{2,6},{6,2},{1... | collective-permute-start | bytes 786440 | tf_op jit(solution)/shard_map/ppermute | solution.py:41
  31.6 16.0 %collective-permute-start.4 = (bf16[1024,128]{1,0:T(8,128)(2,1)S(1)}, bf16[1024,128]{1,0:T(8,128)(2,1)S(1)}, u32[]{:S(2)}, u32[]{:S(2)}) collective-permute-start(bf16[1024,128]{1,0:T(8,128)(2,1)S(1)} %collective-permute-done.3.refs_1_.refs_3_), channel_id=1, source_target_pairs={{2,14},{6,10},{10,6},{14,2},{3,15},{7,11},{11,7},{15,3},{18,30},{2... | collective-permute-start | bytes 786440 | tf_op jit(solution)/shard_map/ppermute | solution.py:46
  42.4 7.1 %collective-permute-start.10 = (bf16[1024,128]{1,0:T(8,128)(2,1)S(1)}, bf16[1024,128]{1,0:T(8,128)(2,1)S(1)}, u32[]{:S(2)}, u32[]{:S(2)}) collective-permute-start(bf16[1024,128]{1,0:T(8,128)(2,1)S(1)} %get-tuple-element.22.narrow2), channel_id=1, source_target_pairs={{0,2},{4,6},{8,10},{12,14},{2,0},{6,4},{10,8},{14,12},{1,3},{5,7},... | collective-permute-start | bytes 786440 | tf_op jit(solution)/shard_map/ppermute | solution.py:46
  42.4 18.2 %collective-permute-start.6 = (bf16[1024,128]{1,0:T(8,128)(2,1)S(1)}, bf16[1024,128]{1,0:T(8,128)(2,1)S(1)}, u32[]{:S(2)}, u32[]{:S(2)}) collective-permute-start(bf16[1024,128]{1,0:T(8,128)(2,1)S(1)} %collective-permute-done.3.refs_1_.refs_3_), channel_id=1, source_target_pairs={{2,6},{6,2},{10,14},{14,10},{3,7},{7,3},{11,15},{15,11},{18,22},{2... | collective-permute-start | bytes 786440 | tf_op jit(solution)/shard_map/ppermute | solution.py:46
  47.6 12.4 %collective-permute-start.5 = (bf16[1024,128]{1,0:T(8,128)(2,1)S(1)}, bf16[1024,128]{1,0:T(8,128)(2,1)S(1)}, u32[]{:S(2)}, u32[]{:S(2)}) collective-permute-start(bf16[1024,128]{1,0:T(8,128)(2,1)S(1)} %collective-permute-done.4.refs_2_), channel_id=1, source_target_pairs={{2,6},{6,2},{10,14},{14,10},{3,7},{7,3},{11,15},{15,11},{18,22},{2... | collective-permute-start | bytes 786440 | tf_op jit(solution)/shard_map/ppermute | solution.py:46
  49.5 11.9 %collective-permute-start.11 = (bf16[1024,128]{1,0:T(8,128)(2,1)S(1)}, bf16[1024,128]{1,0:T(8,128)(2,1)S(1)}, u32[]{:S(2)}, u32[]{:S(2)}) collective-permute-start(bf16[1024,128]{1,0:T(8,128)(2,1)S(1)} %get-tuple-element.22.narrow2), channel_id=1, source_target_pairs={{0,6},{4,2},{8,14},{12,10},{2,0},{6,4},{10,8},{14,12},{1,7},{5,3},... | collective-permute-start | bytes 786440 | tf_op jit(solution)/shard_map/ppermute | solution.py:46
  49.5 12.6 %collective-permute-start.12 = (bf16[1024,128]{1,0:T(8,128)(2,1)S(1)}, bf16[1024,128]{1,0:T(8,128)(2,1)S(1)}, u32[]{:S(2)}, u32[]{:S(2)}) collective-permute-start(bf16[1024,128]{1,0:T(8,128)(2,1)S(1)} %get-tuple-element.22.narrow2), channel_id=1, source_target_pairs={{0,10},{4,14},{8,2},{12,6},{2,0},{6,4},{10,8},{14,12},{1,11},{5,15... | collective-permute-start | bytes 786440 | tf_op jit(solution)/shard_map/ppermute | solution.py:46
  53.0 10.4 %collective-permute-start.13 = (bf16[1024,128]{1,0:T(8,128)(2,1)S(1)}, bf16[1024,128]{1,0:T(8,128)(2,1)S(1)}, u32[]{:S(2)}, u32[]{:S(2)}) collective-permute-start(bf16[1024,128]{1,0:T(8,128)(2,1)S(1)} %collective-permute-done.10.refs_1_), channel_id=1, source_target_pairs={{2,14},{6,10},{10,6},{14,2},{3,15},{7,11},{11,7},{15,3},{18,30},{2... | collective-permute-start | bytes 786440 | tf_op jit(solution)/shard_map/ppermute | solution.py:46
